TPU v7x, 32 devices: a whole 2x2x4 slice. The times are simulated.
32 devices in a mesh: mask: 2 (over x), gx: 16 (over z, y, core).
Axes of the slice: x: 2, y: 2, z: 4, core: 2. Of those that a mesh axis runs over, the one named last changes fastest.
Arguments:
- e_field: float32 [3, 192, 24, 768], P(None, ('mask', 'gx')), parts along dimension 1, may hold values from -6 to 6
- h_field: float32 [3, 192, 24, 768], P(None, ('mask', 'gx')), parts along dimension 1, may hold values from -6 to 6
- polar: float32 [3, 192, 24, 768], P(None, ('mask', 'gx')), parts along dimension 1, may hold values from -6 to 6
- current: float32 [3, 192, 24, 768], P(None, ('mask', 'gx')), parts along dimension 1, may hold values from -6 to 6
- psi_h: float32 [2, 192, 6, 768], P(None, ('mask', 'gx')), parts along dimension 1, may hold values from -6 to 6
- psi_e: float32 [2, 192, 6, 768], P(None, ('mask', 'gx')), parts along dimension 1, may hold values from -6 to 6
- material: int32 [192, 24, 768], P(('mask', 'gx')), parts along dimension 0, may hold values from 0 to 3, as said below
- inv_eps_table: float32 [4], replicated, may hold values from 0.3 to 1
- decay_table: float32 [4], replicated, may hold values from 0.3 to 0.95
- drive_table: float32 [4], replicated, may hold values from 0.1 to 0.5
- strength_table: float32 [4], replicated, may hold values from 0.2 to 1
- spring_table: float32 [4], replicated, may hold values from 0.05 to 1
- orders: int32 [2, 4096], replicated, may hold values from -32 to 31
Outputs:
- e_out: float32 [3, 192, 24, 768], P(None, ('mask', 'gx')), parts along dimension 1
- h_out: float32 [3, 192, 24, 768], P(None, ('mask', 'gx')), parts along dimension 1
- polar_out: float32 [3, 192, 24, 768], P(None, ('mask', 'gx')), parts along dimension 1
- current_out: float32 [3, 192, 24, 768], P(None, ('mask', 'gx')), parts along dimension 1
- psi_h_out: float32 [2, 192, 6, 768], P(None, ('mask', 'gx')), parts along dimension 1
- psi_e_out: float32 [2, 192, 6, 768], P(None, ('mask', 'gx')), parts along dimension 1
- pupil: float32 [4, 8192], P(None, 'mask'), parts along dimension 1
There are 2 independent parts, one for each index of `mask`. A program takes and returns all parts, laid end to end along the dimension named above; an argument that names none is the same for every part. Nothing has to cross between parts.
Inputs may be any that keep to these rules, and one draw needn't show every extreme that they name: `material`: 0 is vacuum, 1 absorber, 2 molybdenum, 3 silicon.
All inputs are finite; a program needn't handle non-finite values.
Results may differ from a plain program's by a relative error of at most 0.000082.
Values sent between devices are 32-bit elements; how exact they have to be, the bound alone decides.
No kernel may reach another device: no remote copies, remote signals or barrier semaphores. Data moves between devices by JAX's collectives and lax.ppermute only.
A program may use at most 64 MiB of HBM per device.

v0:
```python
import math

import jax
import jax.numpy as jnp
from jax import lax
from jax.sharding import PartitionSpec as P

NPML = 6
KSPAN = 64
STEPS = 4


COURANT = 0.5
SIGMA_MAX = 0.8
PML_ALPHA = 0.05


def passed_along(value, axis, steps):
    count = lax.axis_size(axis)
    pairs = [(source, (source + steps) % count) for source in range(count)]
    return lax.ppermute(value, axis, pairs)


def z_forward(field):
    after = jnp.concatenate([field[..., 1:, :], jnp.zeros_like(field[..., :1, :])], axis=-2)
    return after - field


def z_backward(field):
    before = jnp.concatenate([jnp.zeros_like(field[..., :1, :]), field[..., :-1, :]], axis=-2)
    return field - before


def y_forward(field):
    return jnp.roll(field, -1, axis=-1) - field


def y_backward(field):
    return field - jnp.roll(field, 1, axis=-1)


def pad_rows(memory, total):
    return jnp.pad(memory, ((0, 0), (0, total - memory.shape[-2]), (0, 0)))


def pml_coefficients(layers, offset):
    depth = (layers - jnp.arange(layers, dtype=jnp.float32) - offset) / layers
    sigma = SIGMA_MAX * depth**3
    decay = jnp.exp(-(sigma + PML_ALPHA))
    gain = sigma / (sigma + PML_ALPHA) * (decay - 1.0)
    return (decay[:, None], gain[:, None])


def lookup(material, table):
    total = jnp.zeros(material.shape, table.dtype)
    for index in range(table.shape[0]):
        total = total + jnp.where(material == index, table[index], 0.0)
    return total


def h_update(e_x, e_y, e_z, ey_ahead, ez_ahead, h_x, h_y, h_z, psi_hx, psi_hy, decay, gain):
    layers = psi_hx.shape[-2]
    depth_cells = e_x.shape[-2]
    dey_dz = z_forward(e_y)
    dex_dz = z_forward(e_x)
    psi_hx_new = decay * psi_hx + gain * dey_dz[:, :layers]
    psi_hy_new = decay * psi_hy + gain * dex_dz[:, :layers]
    hx_new = h_x - COURANT * (y_forward(e_z) - dey_dz - pad_rows(psi_hx_new, depth_cells))
    hy_new = h_y - COURANT * (dex_dz + pad_rows(psi_hy_new, depth_cells) - (ez_ahead - e_z))
    hz_new = h_z - COURANT * (ey_ahead - e_y - y_forward(e_x))
    return (hx_new, hy_new, hz_new, psi_hx_new, psi_hy_new)


def e_update(
    hx_new,
    hy_new,
    hz_new,
    hy_behind,
    hz_behind,
    psi_ex,
    psi_ey,
    decay,
    gain,
    e_field,
    polar,
    current,
    coefs,
):
    inv_eps, decay_j, drive_j, strength, spring = coefs
    layers = psi_ex.shape[-2]
    depth_cells = hx_new.shape[-2]
    dhy_dz = z_backward(hy_new)
    dhx_dz = z_backward(hx_new)
    psi_ex_new = decay * psi_ex + gain * dhy_dz[:, :layers]
    psi_ey_new = decay * psi_ey + gain * dhx_dz[:, :layers]
    curl_x = y_backward(hz_new) - (dhy_dz + pad_rows(psi_ex_new, depth_cells))
    curl_y = dhx_dz + pad_rows(psi_ey_new, depth_cells) - (hz_new - hz_behind)
    curl_z = hy_new - hy_behind - y_backward(hx_new)
    curl = jnp.stack([curl_x, curl_y, curl_z])
    current_new = decay_j * current + drive_j * (strength * e_field - spring * polar)
    polar_new = polar + current_new
    e_new = e_field + inv_eps * (COURANT * curl - current_new)
    return (e_new, polar_new, current_new, psi_ex_new, psi_ey_new)


def y_table(cells, span):
    rows = jnp.arange(cells, dtype=jnp.int32)
    waves = jnp.arange(span, dtype=jnp.int32) - span // 2
    phase = (rows[:, None] * waves[None, :] % cells).astype(jnp.float32) * (2.0 * math.pi / cells)
    return jnp.concatenate([jnp.cos(phase), jnp.sin(phase)], axis=1)


def x_table(rows, cells, span):
    waves = jnp.arange(span, dtype=jnp.int32) - span // 2
    phase = (rows[:, None] * waves[None, :] % cells).astype(jnp.float32) * (2.0 * math.pi / cells)
    return (jnp.cos(phase), jnp.sin(phase))


def local_spectrum(plane, rows, cells_x, span):
    comps, planes, cells_y = plane.shape
    highest = lax.Precision.HIGHEST
    table = y_table(cells_y, span)
    mixed = jnp.dot(
        plane.reshape(comps * planes, cells_y),
        table,
        precision=highest,
        preferred_element_type=jnp.float32,
    )
    mixed = mixed.reshape(comps, planes, 2, span)
    real_y = mixed[:, :, 0]
    imag_y = -mixed[:, :, 1]
    cos_x, sin_x = x_table(rows, cells_x, span)
    real = jnp.einsum("cxk,xj->cjk", real_y, cos_x, precision=highest) + jnp.einsum(
        "cxk,xj->cjk", imag_y, sin_x, precision=highest
    )
    imag = jnp.einsum("cxk,xj->cjk", imag_y, cos_x, precision=highest) - jnp.einsum(
        "cxk,xj->cjk", real_y, sin_x, precision=highest
    )
    return jnp.stack([real, imag], axis=1)


def pick_orders(spectrum, orders, cells_total):
    span = spectrum.shape[-1]
    flat = spectrum.reshape(4, span * span) / math.sqrt(cells_total)
    index = (orders[0] + span // 2) * span + (orders[1] + span // 2)
    return jnp.take(flat, index, axis=1)


def shards(
    e_field,
    h_field,
    polar,
    current,
    psi_h,
    psi_e,
    material,
    inv_eps_table,
    decay_table,
    drive_table,
    strength_table,
    spring_table,
    orders,
):
    planes = e_field.shape[1]
    layers = psi_h.shape[2]
    coefs = tuple(
        (
            lookup(material, table)
            for table in (inv_eps_table, decay_table, drive_table, strength_table, spring_table)
        )
    )
    decay_h, gain_h = pml_coefficients(layers, 0.5)
    decay_e, gain_e = pml_coefficients(layers, 0.0)
    for step in range(STEPS):
        e_x, e_y, e_z = (e_field[0], e_field[1], e_field[2])
        front = passed_along(e_field[1:3, 0], "gx", -1)
        ey_ahead = jnp.concatenate([e_y[1:], front[0:1]], axis=0)
        ez_ahead = jnp.concatenate([e_z[1:], front[1:2]], axis=0)
        hx_new, hy_new, hz_new, psi_hx, psi_hy = h_update(
            e_x,
            e_y,
            e_z,
            ey_ahead,
            ez_ahead,
            h_field[0],
            h_field[1],
            h_field[2],
            psi_h[0],
            psi_h[1],
            decay_h,
            gain_h,
        )
        sent = passed_along(jnp.stack([hy_new[planes - 1], hz_new[planes - 1]]), "gx", 1)
        hy_edge, hz_edge = (sent[0:1], sent[1:2])
        hy_behind = jnp.concatenate([hy_edge, hy_new[:-1]], axis=0)
        hz_behind = jnp.concatenate([hz_edge, hz_new[:-1]], axis=0)
        h_field = jnp.stack([hx_new, hy_new, hz_new])
        psi_h = jnp.stack([psi_hx, psi_hy])
        e_field, polar, current, psi_ex, psi_ey = e_update(
            hx_new,
            hy_new,
            hz_new,
            hy_behind,
            hz_behind,
            psi_e[0],
            psi_e[1],
            decay_e,
            gain_e,
            e_field,
            polar,
            current,
            coefs,
        )
        psi_e = jnp.stack([psi_ex, psi_ey])
    total_x = planes * lax.axis_size("gx")
    rows = lax.axis_index("gx") * planes + jnp.arange(planes, dtype=jnp.int32)
    partial_spectrum = local_spectrum(e_field[0:2, :, NPML, :], rows, total_x, KSPAN)
    spectrum = lax.psum(partial_spectrum, "gx")
    pupil = pick_orders(spectrum, orders, total_x * e_field.shape[3])
    return (e_field, h_field, polar, current, psi_h, psi_e, pupil)


def solution(mesh):
    in_specs = (
        P(None, ("mask", "gx"), None, None),
        P(None, ("mask", "gx"), None, None),
        P(None, ("mask", "gx"), None, None),
        P(None, ("mask", "gx"), None, None),
        P(None, ("mask", "gx"), None, None),
        P(None, ("mask", "gx"), None, None),
        P(("mask", "gx"), None, None),
        P(),
        P(),
        P(),
        P(),
        P(),
        P(),
    )
    out_specs = (
        P(None, ("mask", "gx"), None, None),
        P(None, ("mask", "gx"), None, None),
        P(None, ("mask", "gx"), None, None),
        P(None, ("mask", "gx"), None, None),
        P(None, ("mask", "gx"), None, None),
        P(None, ("mask", "gx"), None, None),
        P(None, "mask"),
    )
    return jax.shard_map(shards, mesh=mesh, in_specs=in_specs, out_specs=out_specs, check_vma=False)
```

profile of v0, /device:TPU:0, one launch (start us, length us, event | category | flops | bytes accessed | tf_op | source)
XLA Modules:
  0.0 214.2 jit_solution(3916744526809756581)
XLA Ops:
  7.2 0.9 slice_bitcast_fusion.19
  8.1 5.5 %collective-permute-start = (f32[2,24,768]{2,1,0:T(8,128)S(1)}, f32[2,24,768]{2,1,0:T(8,128)S(1)}, u32[]{:S(2)}, u32[]{:S(2)}) collective-permute-start(f32[2,24,768]{2,1,0:T(8,128)S(1)} %slice_bitcast_fusion.19), channel_id=1, source_target_pairs={{0,15},{1,0},{2,1},{3,2},{4,3},{5,4},{6,5},{7,6},{8,7},{9,8},{10,9... | collective-permute-start | bytes 442376 | tf_op jit(solution)/shard_map/ppermute | solution.py:21
  13.7 1.4 slice_bitcast_fusion.3
  15.3 0.9 slice_bitcast_fusion.38
  16.7 0.8 fusion.182
  17.9 0.9 fusion.183
  18.8 0.6 fusion.193
  19.4 0.6 fusion.192
  20.0 0.7 fusion.189
  20.7 0.7 fusion.191
  21.3 0.7 fusion.190
  22.0 1.6 fusion.96
  23.6 0.6 compare_select_fusion
  24.4 0.9 copy-done.23
  25.3 2.9 %select_add_fusion.4 = (f32[6,24,768]{2,1,0:T(8,128)S(1)}, pred[6,24,768]{2,1,0:T(8,128)(4,1)S(1)}, pred[6,24,768]{2,1,0:T(8,128)(4,1)S(1)}, pred[6,24,768]{2,1,0:T(8,128)(4,1)S(1)}, pred[6,24,768]{2,1,0:T(8,128)(4,1)S(1)}) fusion(f32[]{:T(128)} %bitcast.3, f32[]{:T(128)} %bitcast.2, f32[]{:T(128)} %bitcast.1, f32[]{:T(128)} %bitcast, ...), kind=kLoop, calls=%fused_computation.169 | loop fusion | flops 1216512 | bytes 1327120 | tf_op jit(solution)/shard_map/add | solution.py:57
  28.3 2.6 %select_add_fusion = f32[6,24,768]{2,1,0:T(8,128)S(1)} fusion(pred[6,24,768]{2,1,0:T(8,128)(4,1)S(1)} %get-tuple-element.46, pred[6,24,768]{2,1,0:T(8,128)(4,1)S(1)} %get-tuple-element.45, pred[6,24,768]{2,1,0:T(8,128)(4,1)S(1)} %get-tuple-element.44, pred[6,24,768]{2,1,0:T(8,128)(4,1)S(1)} %get-tuple-element.43, f32[]{:T(128)} %bitcast.35, f32[]{:T(128)} %bitcast.34, ...), kind=kLoop, calls=%fused_computation.160 | loop fusion | flops 774144 | bytes 884752 | tf_op jit(solution)/shard_map/add | solution.py:57
  31.0 9.1 %select_add_fusion.3 = (f32[6,24,768]{2,1,0:T(8,128)}, f32[6,24,768]{2,1,0:T(8,128)}, f32[6,24,768]{2,1,0:T(8,128)}) fusion(pred[6,24,768]{2,1,0:T(8,128)(4,1)S(1)} %get-tuple-element.46, pred[6,24,768]{2,1,0:T(8,128)(4,1)S(1)} %get-tuple-element.45, pred[6,24,768]{2,1,0:T(8,128)(4,1)S(1)} %get-tuple-element.44, ...), kind=kLoop, calls=%fused_computation.163 | loop fusion | flops 2322432 | bytes 1769520 | tf_op jit(solution)/shard_map/add | solution.py:57
  40.1 0.6 slice_bitcast_fusion.29
  40.7 0.6 slice_bitcast_fusion.30
  41.8 0.7 pad_maximum_fusion.4
  42.8 7.3 %collective-permute-done.1 = f32[2,24,768]{2,1,0:T(8,128)} collective-permute-done((f32[2,24,768]{2,1,0:T(8,128)}, f32[2,24,768]{2,1,0:T(8,128)}, u32[]{:S(2)}, u32[]{:S(2)}) %collective-permute-start.1) | collective-permute-done | bytes 147488 | tf_op jit(solution)/shard_map/ppermute | solution.py:21
  50.1 0.9 fusion.188
  51.4 0.6 copy-done.21
  52.4 0.9 copy-done.14
  54.1 0.6 fusion.2
  55.5 0.7 copy-done.13
  56.3 1.7 collective-permute-done.2
  58.5 0.5 copy-done.11
  60.1 6.9 %collective-permute-done.3 = f32[2,24,768]{2,1,0:T(8,128)S(1)} collective-permute-done((f32[2,24,768]{2,1,0:T(8,128)S(1)}, f32[2,24,768]{2,1,0:T(8,128)S(1)}, u32[]{:S(2)}, u32[]{:S(2)}) %collective-permute-start.3) | collective-permute-done | bytes 147488 | tf_op jit(solution)/shard_map/ppermute | solution.py:21
  67.6 0.7 fusion.5
  69.3 2.4 %collective-permute-done.4 = f32[2,24,768]{2,1,0:T(8,128)S(1)} collective-permute-done((f32[2,24,768]{2,1,0:T(8,128)S(1)}, f32[2,24,768]{2,1,0:T(8,128)S(1)}, u32[]{:S(2)}, u32[]{:S(2)}) %collective-permute-start.4) | collective-permute-done | bytes 147488 | tf_op jit(solution)/shard_map/ppermute | solution.py:21
  73.5 6.7 %collective-permute-done.5 = f32[2,24,768]{2,1,0:T(8,128)S(1)} collective-permute-done((f32[2,24,768]{2,1,0:T(8,128)S(1)}, f32[2,24,768]{2,1,0:T(8,128)S(1)}, u32[]{:S(2)}, u32[]{:S(2)}) %collective-permute-start.5) | collective-permute-done | bytes 147488 | tf_op jit(solution)/shard_map/ppermute | solution.py:21
  80.9 2.2 %fusion.14 = (f32[3,6,24,768]{3,2,1,0:T(8,128)}, f32[3,6,24,768]{3,2,1,0:T(8,128)S(1)}, f32[3,6,24,768]{3,2,1,0:T(8,128)S(1)}) fusion(f32[3,6,24,768]{3,2,1,0:T(8,128)S(1)} %copy-done.1, f32[3,6,24,768]{3,2,1,0:T(8,128)S(1)} %get-tuple-element.41, f32[6,24,768]{2,1,0:T(8,128)S(1)} %select_add_fusion, f32[3,6,24,768]{3,2,1,0:T(8,128)S(1)} %fusion.5, ...), kind=kLoop, calls=%fused_computation.28 | loop fusion | flops 9289728 | bytes 12828672 | tf_op jit(solution)/shard_map/add | solution.py:101
  84.0 2.5 %collective-permute-done.6 = f32[2,24,768]{2,1,0:T(8,128)S(1)} collective-permute-done((f32[2,24,768]{2,1,0:T(8,128)S(1)}, f32[2,24,768]{2,1,0:T(8,128)S(1)}, u32[]{:S(2)}, u32[]{:S(2)}) %collective-permute-start.6) | collective-permute-done | bytes 147488 | tf_op jit(solution)/shard_map/ppermute | solution.py:21
  87.3 0.7 copy-done.7
  88.2 1.7 fusion.84
  90.2 0.9 copy.180
  91.1 1.2 pad_maximum_fusion
  92.2 2.6 %collective-permute-done.7 = f32[2,24,768]{2,1,0:T(8,128)S(1)} collective-permute-done((f32[2,24,768]{2,1,0:T(8,128)S(1)}, f32[2,24,768]{2,1,0:T(8,128)S(1)}, u32[]{:S(2)}, u32[]{:S(2)}) %collective-permute-start.7) | collective-permute-done | bytes 147488 | tf_op jit(solution)/shard_map/ppermute | solution.py:21
  96.5 0.6 fusion.118
  98.6 0.7 pad_maximum_fusion.8
  99.4 0.9 copy.181
  100.2 86.3 %all-reduce.34.cloned.1.call-done = f32[2,2,64,64]{3,2,0,1:T(8,128)} async-done(((f32[2,2,64,64]{3,2,0,1:T(8,128)}), f32[2,2,64,64]{3,2,0,1:T(8,128)}) %all-reduce.34.cloned.1.call-update) | async-done | bytes 65552 | tf_op jit(solution)/shard_map/psum | solution.py:218
  186.6 0.9 broadcast_multiply_fusion
  187.6 0.6 copy.179
  188.3 14.2 %gather_fusion = f32[4096,4]{1,0:T(8,128)} fusion(f32[4,4096]{0,1:T(8,128)S(1)} %copy.179, s32[4096]{0:T(1024)S(1)} %broadcast_clamp_fusion), kind=kCustom, calls=%fused_computation | custom fusion | bytes 147456 | tf_op jit(solution)/shard_map/jit(_take)/gather | solution.py:146
  202.5 3.6 %select_bitcast_fusion = f32[4,4096]{0,1:T(8,128)S(1)} fusion(f32[4096,4]{1,0:T(8,128)} %gather_fusion, pred[4096]{0:T(1024)(128)(4,1)S(1)} %compare_and_fusion), kind=kLoop, calls=%fused_computation.1 | loop fusion | flops 16384 | bytes 135168 | tf_op jit(solution)/shard_map/jit(_take)/select_n | solution.py:146
  206.1 1.2 copy.182
  (199 shorter events, 15.1 us)
Async XLA Ops:
  7.2 179.4 %all-reduce.34.cloned.1.call-start = ((), (), s32[]{:S(2)}) async-start(), calls=%async_computation | async-start | bytes 262144 | tf_op jit(solution)/shard_map/psum | solution.py:218
  8.1 32.6 %collective-permute-start = (f32[2,24,768]{2,1,0:T(8,128)S(1)}, f32[2,24,768]{2,1,0:T(8,128)S(1)}, u32[]{:S(2)}, u32[]{:S(2)}) collective-permute-start(f32[2,24,768]{2,1,0:T(8,128)S(1)} %slice_bitcast_fusion.19), channel_id=1, source_target_pairs={{0,15},{1,0},{2,1},{3,2},{4,3},{5,4},{6,5},{7,6},{8,7},{9,8},{10,9... | collective-permute-start | bytes 442376 | tf_op jit(solution)/shard_map/ppermute | solution.py:21
  15.2 1.5 copy-start
  15.3 12.9 %copy-start.30 = (f32[6]{0:T(128)}, f32[6]{0:T(128)S(1)}, u32[]{:S(2)}) copy-start(f32[6]{0:T(128)S(1)} %get-tuple-element.180) | copy-start | bytes 76
  15.3 12.9 %copy-start.32 = (f32[6]{0:T(128)}, f32[6]{0:T(128)S(1)}, u32[]{:S(2)}) copy-start(f32[6]{0:T(128)S(1)} %get-tuple-element.181) | copy-start | bytes 76
  16.7 1.0 copy-start.26
  16.7 1.2 copy-start.27
  17.6 1.2 copy-start.36
  17.6 1.8 copy-start.37
  17.6 2.4 %copy-start.38 = (f32[4]{0:T(128)S(1)}, f32[4]{0:T(128)}, u32[]{:S(2)}) copy-start(f32[4]{0:T(128)} %param.21) | copy-start | bytes 52
  17.6 3.1 %copy-start.39 = (f32[4]{0:T(128)S(1)}, f32[4]{0:T(128)}, u32[]{:S(2)}) copy-start(f32[4]{0:T(128)} %param.23) | copy-start | bytes 52
  17.6 3.8 %copy-start.40 = (f32[4]{0:T(128)S(1)}, f32[4]{0:T(128)}, u32[]{:S(2)}) copy-start(f32[4]{0:T(128)} %param.22) | copy-start | bytes 52
  17.6 6.0 %copy-start.29 = (s32[2,4096]{1,0:T(2,128)S(1)}, s32[2,4096]{1,0:T(2,128)}, u32[]{:S(2)}) copy-start(s32[2,4096]{1,0:T(2,128)} %param.25) | copy-start | bytes 98308
  17.6 6.0 %copy-start.34 = (s32[64]{0:T(128)}, s32[64]{0:T(128)S(1)}, u32[]{:S(2)}) copy-start(s32[64]{0:T(128)S(1)} %iota_add_fusion) | copy-start | bytes 772
  24.3 1.0 copy-start.23
  28.3 13.0 %copy-start.10 = (f32[6,6,768]{2,1,0:T(8,128)}, f32[6,6,768]{2,1,0:T(8,128)S(1)}, u32[]{:S(2)}) copy-start(f32[6,6,768]{2,1,0:T(8,128)S(1)} %get-tuple-element.157) | copy-start | bytes 331780
  28.3 13.0 %copy-start.12 = (f32[6,6,768]{2,1,0:T(8,128)}, f32[6,6,768]{2,1,0:T(8,128)S(1)}, u32[]{:S(2)}) copy-start(f32[6,6,768]{2,1,0:T(8,128)S(1)} %get-tuple-element.156) | copy-start | bytes 331780
  31.0 10.4 %copy-start.6 = (f32[3,6,24,768]{3,2,1,0:T(8,128)S(1)}, f32[3,6,24,768]{3,2,1,0:T(8,128)}, u32[]{:S(2)}) copy-start(f32[3,6,24,768]{3,2,1,0:T(8,128)} %param.14) | copy-start | bytes 3981316
  42.5 7.6 %collective-permute-start.1 = (f32[2,24,768]{2,1,0:T(8,128)}, f32[2,24,768]{2,1,0:T(8,128)}, u32[]{:S(2)}, u32[]{:S(2)}) collective-permute-start(f32[2,24,768]{2,1,0:T(8,128)} %pad_maximum_fusion.4), channel_id=1, source_target_pairs={{0,1},{1,2},{2,3},{3,4},{4,5},{5,6},{6,7},{7,8},{8,9},{9,10},{10,1... | collective-permute-start | bytes 442376 | tf_op jit(solution)/shard_map/ppermute | solution.py:21
  51.0 0.9 copy-start.21
  51.0 0.9 copy-start.22
  52.0 1.3 copy-start.14
  52.1 1.6 copy-start.1
  52.1 1.7 copy-start.2
  52.1 1.8 copy-start.3
  52.1 2.0 copy-start.4
  55.3 0.9 copy-start.13
  55.3 0.9 copy-start.31
  55.3 0.9 copy-start.33
  55.3 2.7 %collective-permute-start.2 = (f32[2,24,768]{2,1,0:T(8,128)S(1)}, f32[2,24,768]{2,1,0:T(8,128)S(1)}, u32[]{:S(2)}, u32[]{:S(2)}) collective-permute-start(f32[2,24,768]{2,1,0:T(8,128)S(1)} %slice_bitcast_fusion.18), channel_id=1, source_target_pairs={{0,15},{1,0},{2,1},{3,2},{4,3},{5,4},{6,5},{7,6},{8,7},{9,8},{10,9... | collective-permute-start | bytes 442376 | tf_op jit(solution)/shard_map/ppermute | solution.py:21
  58.1 0.9 copy-start.11
  59.1 0.7 copy-start.28
  59.3 7.6 %collective-permute-start.3 = (f32[2,24,768]{2,1,0:T(8,128)S(1)}, f32[2,24,768]{2,1,0:T(8,128)S(1)}, u32[]{:S(2)}, u32[]{:S(2)}) collective-permute-start(f32[2,24,768]{2,1,0:T(8,128)S(1)} %pad_maximum_fusion.5), channel_id=1, source_target_pairs={{0,1},{1,2},{2,3},{3,4},{4,5},{5,6},{6,7},{7,8},{8,9},{9,10},{10,1... | collective-permute-start | bytes 442376 | tf_op jit(solution)/shard_map/ppermute | solution.py:21
  69.0 2.7 %collective-permute-start.4 = (f32[2,24,768]{2,1,0:T(8,128)S(1)}, f32[2,24,768]{2,1,0:T(8,128)S(1)}, u32[]{:S(2)}, u32[]{:S(2)}) collective-permute-start(f32[2,24,768]{2,1,0:T(8,128)S(1)} %slice_bitcast_fusion.17), channel_id=1, source_target_pairs={{0,15},{1,0},{2,1},{3,2},{4,3},{5,4},{6,5},{7,6},{8,7},{9,8},{10,9... | collective-permute-start | bytes 442376 | tf_op jit(solution)/shard_map/ppermute | solution.py:21
  72.3 0.9 copy-start.19
  72.3 1.0 copy-start.20
  72.5 7.8 %collective-permute-start.5 = (f32[2,24,768]{2,1,0:T(8,128)S(1)}, f32[2,24,768]{2,1,0:T(8,128)S(1)}, u32[]{:S(2)}, u32[]{:S(2)}) collective-permute-start(f32[2,24,768]{2,1,0:T(8,128)S(1)} %pad_maximum_fusion.6), channel_id=1, source_target_pairs={{0,1},{1,2},{2,3},{3,4},{4,5},{5,6},{6,7},{7,8},{8,9},{9,10},{10,1... | collective-permute-start | bytes 442376 | tf_op jit(solution)/shard_map/ppermute | solution.py:21
  83.1 12.8 %copy-start.5 = (f32[3,6,24,768]{3,2,1,0:T(8,128)}, f32[3,6,24,768]{3,2,1,0:T(8,128)S(1)}, u32[]{:S(2)}) copy-start(f32[3,6,24,768]{3,2,1,0:T(8,128)S(1)} %get-tuple-element.38) | copy-start | bytes 3981316
  83.8 2.7 %collective-permute-start.6 = (f32[2,24,768]{2,1,0:T(8,128)S(1)}, f32[2,24,768]{2,1,0:T(8,128)S(1)}, u32[]{:S(2)}, u32[]{:S(2)}) collective-permute-start(f32[2,24,768]{2,1,0:T(8,128)S(1)} %slice_bitcast_fusion.16), channel_id=1, source_target_pairs={{0,15},{1,0},{2,1},{3,2},{4,3},{5,4},{6,5},{7,6},{8,7},{9,8},{10,9... | collective-permute-start | bytes 442376 | tf_op jit(solution)/shard_map/ppermute | solution.py:21
  87.0 1.0 copy-start.7
  87.1 1.1 copy-start.8
  87.1 1.1 copy-start.24
  87.1 1.1 copy-start.25
  87.3 7.6 %collective-permute-start.7 = (f32[2,24,768]{2,1,0:T(8,128)S(1)}, f32[2,24,768]{2,1,0:T(8,128)S(1)}, u32[]{:S(2)}, u32[]{:S(2)}) collective-permute-start(f32[2,24,768]{2,1,0:T(8,128)S(1)} %pad_maximum_fusion.7), channel_id=1, source_target_pairs={{0,1},{1,2},{2,3},{3,4},{4,5},{5,6},{6,7},{7,8},{8,9},{9,10},{10,1... | collective-permute-start | bytes 442376 | tf_op jit(solution)/shard_map/ppermute | solution.py:21
  96.0 1.1 copy-start.35
  96.4 91.1 %copy-start.9 = (f32[3,6,24,768]{3,2,1,0:T(8,128)}, f32[3,6,24,768]{3,2,1,0:T(8,128)S(1)}, u32[]{:S(2)}) copy-start(f32[3,6,24,768]{3,2,1,0:T(8,128)S(1)} %fusion.11) | copy-start | bytes 3981316
  96.4 2.9 %copy-start.16 = (f32[6,6,768]{2,1,0:T(8,128)S(1)}, f32[6,6,768]{2,1,0:T(8,128)}, u32[]{:S(2)}) copy-start(f32[6,6,768]{2,1,0:T(8,128)} %copy-done.15) | copy-start | bytes 331780
  96.4 2.9 %copy-start.18 = (f32[6,6,768]{2,1,0:T(8,128)S(1)}, f32[6,6,768]{2,1,0:T(8,128)}, u32[]{:S(2)}) copy-start(f32[6,6,768]{2,1,0:T(8,128)} %copy-done.17) | copy-start | bytes 331780
  (2 other events, 1.4 us)
Sparse Core Ops, SparseCore 0:
  99.4 87.0 all-reduce.33
where the time goes:
time: 216 us; the launch traced here: 214 us
  waiting for transfers between devices  116 us (54%)
  local copies, waits for them, and re-layouts  39 us (18%)
  other arithmetic  35.5 us (16%)
  between operations  15 us (7%)
  starting transfers between devices  6.09 us (3%)
    psum x1, waiting for transfers between devices, shards(): spectrum = lax.psum(partial_spectrum, 'gx')  86.3 us
    ppermute x8, waiting for transfers between devices, passed_along(): return lax.ppermute(value, axis, pairs)  30.1 us
    add x3, other arithmetic, lookup(): total = total + jnp.where(material == index, table[index], 0.0)  14.6 us
    gather x1, local copies, waits for them, and re-layouts, pick_orders(): return jnp.take(flat, index, axis=1)  14.2 us
    unnamed x85, local copies, waits for them, and re-layouts  10.3 us
    ppermute x8, starting transfers between devices, passed_along(): return lax.ppermute(value, axis, pairs)  6.06 us
  transfers between devices with their start and end apart: 9, of which 8 were waited for; matrix products, arithmetic and copies ran while one was open for 15% of the time, Pallas kernels for 0%

commit v1 on v0

v1 whole, which is shorter than its diff:
```python
import math

import jax
import jax.numpy as jnp
import numpy as np
from jax import lax
from jax.experimental import pallas as pl
from jax.experimental.pallas import tpu as pltpu
from jax.sharding import PartitionSpec as P

KSPAN = 64
STEPS = 4

COURANT = 0.5
SIGMA_MAX = 0.8
PML_ALPHA = 0.05

ROWS = 8
LANES = 128
F32 = jnp.float32

HBM = pl.BlockSpec(memory_space=pltpu.HBM)
VMEM = pl.BlockSpec(memory_space=pltpu.VMEM)
SMEM = pl.BlockSpec(memory_space=pltpu.SMEM)


def params():
    return pltpu.CompilerParams(vmem_limit_bytes=24 << 20)


def passed_along(value, steps):
    count = lax.axis_size("gx")
    pairs = [(source, (source + steps) % count) for source in range(count)]
    return lax.ppermute(value, "gx", pairs)


def swapped(value, mask):
    count = lax.axis_size("gx")
    return lax.ppermute(value, "gx", [(source, source ^ mask) for source in range(count)])


def pml(layers, offset, width):
    row = lax.broadcasted_iota(jnp.int32, (ROWS, LANES), 0)
    depth = (layers - row.astype(F32) - offset) / layers
    sigma = SIGMA_MAX * depth * depth * depth
    decay = jnp.exp(-(sigma + PML_ALPHA))
    gain = sigma / (sigma + PML_ALPHA) * (decay - 1.0)
    inside = row < layers
    wide = lambda v: jnp.concatenate([jnp.where(inside, v, 0.0)] * (width // LANES), axis=1)
    return wide(decay), wide(gain)


def tile_of(ref, lead, k):
    return ref[(*lead, slice(ROWS * k, ROWS * k + ROWS), slice(None))]


def put_tile(ref, lead, k, value):
    ref[(*lead, slice(ROWS * k, ROWS * k + ROWS), slice(None))] = value


def row_ids(value):
    return lax.broadcasted_iota(jnp.int32, value.shape, 0)


def z_forward(ref, lead, k, tiles, here):
    if k + 1 < tiles:
        after = ref[(*lead, slice(ROWS * k + 1, ROWS * k + ROWS + 1), slice(None))]
    else:
        after = jnp.where(row_ids(here) < ROWS - 1, pltpu.roll(here, ROWS - 1, 0), 0.0)
    return after - here


def z_backward(ref, lead, k, here):
    if k > 0:
        before = ref[(*lead, slice(ROWS * k - 1, ROWS * k + ROWS - 1), slice(None))]
    else:
        before = jnp.where(row_ids(here) > 0, pltpu.roll(here, 1, 0), 0.0)
    return here - before


def y_forward(value):
    return pltpu.roll(value, value.shape[-1] - 1, 1) - value


def y_backward(value):
    return value - pltpu.roll(value, 1, 1)


def lookup(material, table):
    count = table.shape[0]
    total = jnp.full(material.shape, table[count - 1], F32)
    for index in range(count - 1):
        total = jnp.where(material == index, table[index], total)
    return total


def h_plane(e, h, psi_h, i, tiles, coef, last):
    decay, gain = coef
    for k in range(tiles):
        ex, ey, ez = (tile_of(e, (c, i), k) for c in range(3))
        dey_dz = z_forward(e, (1, i), k, tiles, ey)
        curl = y_forward(ez) - dey_dz
        if k == 0:
            memory = decay * psi_h[0, i] + gain * dey_dz
            psi_h[0, i] = memory
            curl = curl - memory
        put_tile(h, (0, i), k, tile_of(h, (0, i), k) - COURANT * curl)
        if last:
            continue
        dex_dz = z_forward(e, (0, i), k, tiles, ex)
        curl = dex_dz - (tile_of(e, (2, i + 1), k) - ez)
        if k == 0:
            memory = decay * psi_h[1, i] + gain * dex_dz
            psi_h[1, i] = memory
            curl = curl + memory
        put_tile(h, (1, i), k, tile_of(h, (1, i), k) - COURANT * curl)
        curl = tile_of(e, (1, i + 1), k) - ey - y_forward(ex)
        put_tile(h, (2, i), k, tile_of(h, (2, i), k) - COURANT * curl)


def e_plane(e, h, polar, current, psi_e, mats, i, tiles, coef, first=False, last=False):
    inv_eps, decay_j, pull, spring = mats
    decay, gain = coef
    for k in range(tiles):
        hx = tile_of(h, (0, i), k)
        dhx_dz = z_backward(h, (0, i), k, hx)
        old = [tile_of(e, (c, i), k) for c in range(3)]
        curl_y = dhx_dz
        curl_z = -y_backward(hx)
        curl_x = None
        if k == 0:
            memory = decay * psi_e[1, i] + gain * dhx_dz
            psi_e[1, i] = memory
            curl_y = curl_y + memory
        if not last:
            hy, hz = (tile_of(h, (c, i), k) for c in (1, 2))
            dhy_dz = z_backward(h, (1, i), k, hy)
            curl_x = y_backward(hz) - dhy_dz
            if k == 0:
                memory = decay * psi_e[0, i] + gain * dhy_dz
                psi_e[0, i] = memory
                curl_x = curl_x - memory
            curl_y = curl_y - hz
            curl_z = curl_z + hy
        if first:
            curl_y = curl_y - COURANT * old[1]
            curl_z = curl_z - COURANT * old[2]
        else:
            curl_y = curl_y + tile_of(h, (2, i - 1), k)
            curl_z = curl_z - tile_of(h, (1, i - 1), k)
        inv, dec, drv, spr = (tile_of(m, (i,), k) for m in mats)
        for c, curl in enumerate((curl_x, curl_y, curl_z)):
            pol = tile_of(polar, (c, i), k)
            cur = dec * tile_of(current, (c, i), k) + (drv * old[c] - spr * pol)
            put_tile(current, (c, i), k, cur)
            put_tile(polar, (c, i), k, pol + cur)
            change = -cur if curl is None else COURANT * curl - cur
            put_tile(e, (c, i), k, old[c] + inv * change)


def sent_ahead(e, h, psi_hy, put_psi, lead_e, lead_h, k, tiles, coef):
    decay, gain = coef
    ex, ey, ez = (tile_of(e, lead_e(c), k) for c in range(3))
    dex_dz = z_forward(e, lead_e(0), k, tiles, ex)
    curl = dex_dz + ez
    if k == 0:
        memory = decay * psi_hy + gain * dex_dz
        put_psi(memory)
        curl = curl + memory
    part_y = tile_of(h, lead_h(0), k) - COURANT * curl
    part_z = tile_of(h, lead_h(1), k) + COURANT * (ey + y_forward(ex))
    return part_y, part_z


def start_all(copies):
    for copy in copies:
        copy.start()


def wait_all(copies):
    for copy in copies:
        copy.wait()


def first_message(e_field, h_field, psi_h, material, inv_table):
    planes, depth, width = e_field.shape[1:]
    layers = psi_h.shape[2]
    tiles = depth // ROWS
    edge = planes - 1
    probe = layers // ROWS * ROWS

    def body(e_in, h_in, psi_in, mat_in, table, back, ahead, psi_out, e, h, psi, mat, sem):
        wanted = [
            (e_in.at[1, 0], back.at[0:depth]),
            (e_in.at[2, 0], back.at[depth : 2 * depth]),
            (e_in.at[:, edge], e),
            (h_in.at[1:3, edge], h),
            (psi_in.at[1, edge], psi.at[0:layers]),
            (mat_in.at[0, probe : probe + ROWS], mat.at[0]),
            (mat_in.at[edge, probe : probe + ROWS], mat.at[1]),
        ]
        psi[...] = jnp.zeros_like(psi)
        copies = [pltpu.make_async_copy(s, d, sem.at[n]) for n, (s, d) in enumerate(wanted)]
        start_all(copies)
        coef = pml(layers, 0.5, width)
        wait_all(copies)
        back[2 * depth : 2 * depth + ROWS, :] = lookup(mat[0], table)
        ahead[2 * depth : 2 * depth + ROWS, :] = lookup(mat[1], table)

        def put_psi(value):
            psi_out[...] = value

        for k in range(tiles):
            part_y, part_z = sent_ahead(e, h, psi[...], put_psi, lambda c: (c,), lambda c: (c,), k, tiles, coef)
            put_tile(ahead, (), k, part_y)
            put_tile(ahead, (), tiles + k, part_z)

    message = pltpu.VMEM((2 * depth + ROWS, width), F32)
    return pl.pallas_call(
        body,
        name="first_message",
        out_shape=(message, message, pltpu.VMEM((ROWS, width), F32)),
        in_specs=[HBM, HBM, HBM, HBM, SMEM],
        out_specs=(VMEM, VMEM, VMEM),
        scratch_shapes=[
            pltpu.VMEM((3, depth, width), F32),
            pltpu.VMEM((2, depth, width), F32),
            pltpu.VMEM((ROWS, width), F32),
            pltpu.VMEM((2, ROWS, width), jnp.int32),
            pltpu.SemaphoreType.DMA((7,)),
        ],
        compiler_params=params(),
    )(e_field, h_field, psi_h, material, inv_table)


def all_planes(e, h, polar, current, psi_h, psi_e, mats, planes, tiles, coef_h, coef_e):
    h_plane(e, h, psi_h, 0, tiles, coef_h, False)
    e_plane(e, h, polar, current, psi_e, mats, 0, tiles, coef_e, first=True)

    def step(i, carry):
        h_plane(e, h, psi_h, i, tiles, coef_h, False)
        e_plane(e, h, polar, current, psi_e, mats, i, tiles, coef_e)
        return carry

    lax.fori_loop(1, planes - 1, step, 0)
    h_plane(e, h, psi_h, planes - 1, tiles, coef_h, True)
    e_plane(e, h, polar, current, psi_e, mats, planes - 1, tiles, coef_e, last=True)


def state_shapes(planes, depth, width):
    field = pltpu.VMEM((3, planes, depth, width), F32)
    memory = pltpu.VMEM((2, planes, ROWS, width), F32)
    return (field, field, field, field, memory, memory)


def first_interior(fields, memories, material, tables, ahead, psi_edge):
    planes, depth, width = material.shape
    layers = memories[0].shape[2]
    tiles = depth // ROWS
    edge = planes - 1

    def body(e_in, h_in, p_in, c_in, ph_in, pe_in, mat_in, t0, t1, t2, t3, t4, ahead, psi_edge, *rest):
        e, h, polar, current, psi_h, psi_e, inv, dec, drv, spr, mat, sem = rest
        zero = jnp.zeros((ROWS, width), F32)
        for c in range(2):
            for i in range(planes):
                psi_h[c, i] = zero
                psi_e[c, i] = zero
        pairs = [(e_in, e), (h_in, h), (p_in, polar), (c_in, current)]

        def copies(i):
            found = [pltpu.make_async_copy(s.at[:, i], d.at[:, i], sem.at[n, i]) for n, (s, d) in enumerate(pairs)]
            found.append(pltpu.make_async_copy(ph_in.at[:, i], psi_h.at[:, i, 0:layers], sem.at[4, i]))
            found.append(pltpu.make_async_copy(pe_in.at[:, i], psi_e.at[:, i, 0:layers], sem.at[5, i]))
            found.append(pltpu.make_async_copy(mat_in.at[i], mat.at[i], sem.at[6, i]))
            return found

        for i in range(planes):
            start_all(copies(i))
        coef_h = pml(layers, 0.5, width)
        coef_e = pml(layers, 0.0, width)
        mats = (inv, dec, drv, spr)

        def arrive(i):
            wait_all(copies(i))
            for k in range(tiles):
                m = tile_of(mat, (i,), k)
                put_tile(inv, (i,), k, lookup(m, t0))
                put_tile(dec, (i,), k, lookup(m, t1))
                drive = lookup(m, t2)
                put_tile(drv, (i,), k, drive * lookup(m, t3))
                put_tile(spr, (i,), k, drive * lookup(m, t4))

        arrive(0)

        def step(i, carry):
            arrive(i + 1)
            h_plane(e, h, psi_h, i, tiles, coef_h, False)
            return carry

        arrive(1)
        h_plane(e, h, psi_h, 0, tiles, coef_h, False)
        e_plane(e, h, polar, current, psi_e, mats, 0, tiles, coef_e, first=True)

        def step(i, carry):
            arrive(i + 1)
            h_plane(e, h, psi_h, i, tiles, coef_h, False)
            e_plane(e, h, polar, current, psi_e, mats, i, tiles, coef_e)
            return carry

        lax.fori_loop(1, edge, step, 0)
        h_plane(e, h, psi_h, edge, tiles, coef_h, True)
        for k in range(tiles):
            put_tile(h, (1, edge), k, tile_of(ahead, (), k))
            put_tile(h, (2, edge), k, tile_of(ahead, (), tiles + k))
        psi_h[1, edge] = psi_edge[...]
        e_plane(e, h, polar, current, psi_e, mats, edge, tiles, coef_e, last=True)

    coef = pltpu.VMEM((planes, depth, width), F32)
    return pl.pallas_call(
        body,
        name="first_interior",
        out_shape=(*state_shapes(planes, depth, width), coef, coef, coef, coef),
        in_specs=[HBM] * 7 + [SMEM] * 5 + [VMEM, VMEM],
        out_specs=(VMEM,) * 10,
        scratch_shapes=[
            pltpu.VMEM((planes, depth, width), jnp.int32),
            pltpu.SemaphoreType.DMA((7, planes)),
        ],
        compiler_params=params(),
    )(*fields, *memories, material, *tables, ahead, psi_edge)


def interior(state, mats, layers):
    planes, depth, width = state[0].shape[1:]
    tiles = depth // ROWS

    def body(*refs):
        mats_in = refs[6:10]
        e, h, polar, current, psi_h, psi_e = refs[10:16]
        coef_h = pml(layers, 0.5, width)
        coef_e = pml(layers, 0.0, width)
        all_planes(e, h, polar, current, psi_h, psi_e, mats_in, planes, tiles, coef_h, coef_e)

    return pl.pallas_call(
        body,
        name="interior",
        out_shape=state_shapes(planes, depth, width),
        in_specs=[VMEM] * 10,
        out_specs=(VMEM,) * 6,
        input_output_aliases={n: n for n in range(6)},
        compiler_params=params(),
    )(*state, *mats)


def close_edges(e, h, psi_e, inv, from_ahead, from_behind, edge, tiles, coef_e):
    decay, gain = coef_e
    for k in range(tiles):
        half = COURANT * tile_of(inv, (0,), k)
        put_tile(e, (1, 0), k, tile_of(e, (1, 0), k) + half * tile_of(from_behind, (), tiles + k))
        put_tile(e, (2, 0), k, tile_of(e, (2, 0), k) - half * tile_of(from_behind, (), k))
        put_tile(h, (1, edge), k, tile_of(h, (1, edge), k) + COURANT * tile_of(from_ahead, (), tiles + k))
        put_tile(h, (2, edge), k, tile_of(h, (2, edge), k) - COURANT * tile_of(from_ahead, (), k))
    for k in range(tiles):
        hy, hz = (tile_of(h, (c, edge), k) for c in (1, 2))
        dhy_dz = z_backward(h, (1, edge), k, hy)
        curl_x = y_backward(hz) - dhy_dz
        if k == 0:
            memory = decay * psi_e[0, edge] + gain * dhy_dz
            psi_e[0, edge] = memory
            curl_x = curl_x - memory
        half = COURANT * tile_of(inv, (edge,), k)
        put_tile(e, (0, edge), k, tile_of(e, (0, edge), k) + half * curl_x)
        put_tile(e, (1, edge), k, tile_of(e, (1, edge), k) - half * hz)
        put_tile(e, (2, edge), k, tile_of(e, (2, edge), k) + half * hy)


def boundary(state, inv, from_ahead, from_behind, layers):
    e_now, h_now, polar, current, psi_h_now, psi_e_now = state
    planes, depth, width = e_now.shape[1:]
    tiles = depth // ROWS
    edge = planes - 1

    def body(e_in, h_in, ph_in, pe_in, inv, from_ahead, from_behind, e, h, psi_h, psi_e, back, ahead):
        coef_h = pml(layers, 0.5, width)
        coef_e = pml(layers, 0.0, width)
        close_edges(e, h, psi_e, inv, from_ahead, from_behind, edge, tiles, coef_e)

        def put_psi(value):
            psi_h[1, edge] = value

        for k in range(tiles):
            put_tile(back, (), k, tile_of(e, (1, 0), k))
            put_tile(back, (), tiles + k, tile_of(e, (2, 0), k))
            part_y, part_z = sent_ahead(
                e, h, psi_h[1, edge], put_psi, lambda c: (c, edge), lambda c: (c + 1, edge), k, tiles, coef_h
            )
            put_tile(h, (1, edge), k, part_y)
            put_tile(h, (2, edge), k, part_z)
            put_tile(ahead, (), k, part_y)
            put_tile(ahead, (), tiles + k, part_z)

    field, _, _, _, memory, _ = state_shapes(planes, depth, width)
    message = pltpu.VMEM((2 * depth, width), F32)
    e, h, psi_h, psi_e, back, ahead = pl.pallas_call(
        body,
        name="boundary",
        out_shape=(field, field, memory, memory, message, message),
        in_specs=[VMEM] * 7,
        out_specs=(VMEM,) * 6,
        input_output_aliases={0: 0, 1: 1, 2: 2, 3: 3},
        compiler_params=params(),
    )(e_now, h_now, psi_h_now, psi_e_now, inv, from_ahead, from_behind)
    return (e, h, polar, current, psi_h, psi_e), back, ahead


def spectral_rows(planes):
    return -(-(2 * planes + 3) // ROWS) * ROWS


def last_interior(state, mats, back, inv_ahead, inv_behind, table, layers):
    planes, depth, width = state[0].shape[1:]
    tiles = depth // ROWS
    edge = planes - 1
    count = spectral_rows(planes)
    at = layers
    inner = at % ROWS

    def body(*refs):
        mats_in = refs[6:10]
        back, inv_ahead, inv_behind, table = refs[10:14]
        e, h, polar, current, psi_h, psi_e, mixed = refs[14:21]
        e_out, h_out, p_out, c_out, ph_out, pe_out = refs[21:27]
        rows, sem = refs[27:]
        coef_h = pml(layers, 0.5, width)
        coef_e = pml(layers, 0.0, width)
        all_planes(e, h, polar, current, psi_h, psi_e, mats_in, planes, tiles, coef_h, coef_e)
        wanted = [
            (polar, p_out),
            (current, c_out),
            (e.at[:, 1:edge], e_out.at[:, 1:edge]),
            (e.at[0, 0], e_out.at[0, 0]),
            (h.at[:, 0:edge], h_out.at[:, 0:edge]),
            (h.at[0, edge], h_out.at[0, edge]),
            (psi_h.at[:, :, 0:layers], ph_out),
            (psi_e.at[:, 0:edge, 0:layers], pe_out.at[:, 0:edge]),
            (psi_e.at[1, edge, 0:layers], pe_out.at[1, edge]),
        ]
        copies = [pltpu.make_async_copy(s, d, sem.at[n]) for n, (s, d) in enumerate(wanted)]
        start_all(copies)

        def line(ref, lead, z):
            return ref[(*lead, slice(z, z + 1), slice(None))]

        rows[...] = jnp.zeros_like(rows)
        for c in range(2):
            for i in range(edge):
                rows[c * planes + i : c * planes + i + 1, :] = line(e, (c, i), at)
        inv = mats_in[0]
        half = COURANT * line(inv, (edge,), at)
        part_y, part_y_up, part_z = line(h, (1, edge), at), line(h, (1, edge), at - 1), line(h, (2, edge), at)
        rows[edge : edge + 1, :] = line(e, (0, edge), at) + half * (y_backward(part_z) - (part_y - part_y_up))
        rows[planes + edge : planes + edge + 1, :] = line(e, (1, edge), at) - half * part_z
        e_y, e_z, e_z_up = line(back, (), at), line(back, (), depth + at), line(back, (), depth + at - 1)
        quarter = COURANT * COURANT * line(inv_behind, (), inner)
        rows[2 * planes : 2 * planes + 1, :] = -quarter * (y_backward(e_y) + (e_z - e_z_up))
        rows[2 * planes + 1 : 2 * planes + 2, :] = quarter * e_y
        rows[2 * planes + 2 : 2 * planes + 3, :] = COURANT * line(inv_ahead, (), inner) * part_z
        mixed[...] = jnp.dot(rows[...], table[...], precision=lax.Precision.HIGHEST, preferred_element_type=F32)
        wait_all(copies)

    field = jax.ShapeDtypeStruct((3, planes, depth, width), F32)
    memory = jax.ShapeDtypeStruct((2, planes, layers, width), F32)
    found = pl.pallas_call(
        body,
        name="last_interior",
        out_shape=(
            *state_shapes(planes, depth, width),
            pltpu.VMEM((count, table.shape[1]), F32),
            *((field,) * 4),
            memory,
            memory,
        ),
        in_specs=[VMEM] * 14,
        out_specs=(*((VMEM,) * 7), *((HBM,) * 6)),
        input_output_aliases={n: n for n in range(6)},
        scratch_shapes=[pltpu.VMEM((count, width), F32), pltpu.SemaphoreType.DMA((9,))],
        compiler_params=params(),
    )(*state, *mats, back, inv_ahead, inv_behind, table)
    return found[:6], found[6], found[7:]


def last_boundary(state, inv, from_ahead, from_behind, outs, layers):
    e_now, h_now, _, _, _, psi_e_now = state
    planes, depth, width = e_now.shape[1:]
    tiles = depth // ROWS
    edge = planes - 1

    def body(e_in, h_in, pe_in, inv, from_ahead, from_behind, e_hbm, h_hbm, pe_hbm, e, h, psi_e, e_out, h_out, pe_out, sem):
        coef_e = pml(layers, 0.0, width)
        close_edges(e, h, psi_e, inv, from_ahead, from_behind, edge, tiles, coef_e)
        wanted = [
            (e.at[1:3, 0], e_out.at[1:3, 0]),
            (e.at[:, edge], e_out.at[:, edge]),
            (h.at[1:3, edge], h_out.at[1:3, edge]),
            (psi_e.at[0, edge, 0:layers], pe_out.at[0, edge]),
        ]
        copies = [pltpu.make_async_copy(s, d, sem.at[n]) for n, (s, d) in enumerate(wanted)]
        start_all(copies)
        wait_all(copies)

    field, _, _, _, memory, _ = state_shapes(planes, depth, width)
    shape = lambda x: jax.ShapeDtypeStruct(x.shape, x.dtype)
    e_out, h_out, p_out, c_out, ph_out, pe_out = outs
    found = pl.pallas_call(
        body,
        name="last_boundary",
        out_shape=(field, field, memory, shape(e_out), shape(h_out), shape(pe_out)),
        in_specs=[VMEM] * 6 + [HBM] * 3,
        out_specs=(VMEM, VMEM, VMEM, HBM, HBM, HBM),
        input_output_aliases={0: 0, 1: 1, 2: 2, 6: 3, 7: 4, 8: 5},
        scratch_shapes=[pltpu.SemaphoreType.DMA((4,))],
        compiler_params=params(),
    )(e_now, h_now, psi_e_now, inv, from_ahead, from_behind, e_out, h_out, pe_out)
    return (found[3], found[4], p_out, c_out, ph_out, found[5])


def y_table(cells):
    phase = np.arange(cells)[:, None] * (np.arange(KSPAN) - KSPAN // 2)[None, :] % cells
    phase = phase.astype(np.float64) * (2.0 * math.pi / cells)
    return np.concatenate([np.cos(phase), np.sin(phase)], axis=1).astype(np.float32)


def x_table(planes, count):
    rows = spectral_rows(planes)
    cells = planes * count
    comp = np.full(rows, -1)
    shift = np.zeros(rows, np.int64)
    comp[:planes], shift[:planes] = 0, np.arange(planes)
    comp[planes : 2 * planes], shift[planes : 2 * planes] = 1, np.arange(planes)
    comp[2 * planes : 2 * planes + 3] = [0, 1, 1]
    shift[2 * planes : 2 * planes + 3] = [-1, -1, planes]
    x = (np.arange(count)[:, None] * planes + shift[None, :]) % cells
    waves = np.arange(KSPAN) - KSPAN // 2
    phase = (waves[:, None, None] * x[None] % cells).astype(np.float64) * (2.0 * math.pi / cells)
    parts = []
    for c in range(2):
        for wave in (np.cos(phase), np.sin(phase)):
            parts.append(np.where(comp[None, None, :] == c, wave, 0.0).reshape(KSPAN, count * rows))
    return np.concatenate(parts, axis=0).astype(np.float32)


def gathered(block):
    count = lax.axis_size("gx")
    assert count & (count - 1) == 0
    pieces = [block]
    reach = 1
    while reach < count:
        ways = min(4, count // reach)
        held = pieces[0] if len(pieces) == 1 else jnp.concatenate(pieces, axis=0)
        pieces = [held] + [swapped(held, reach * way) for way in range(1, ways)]
        reach *= ways
    return pieces


def pick_orders(pieces, table, orders, cells_total):
    rows = spectral_rows_of = None
    count = lax.axis_size("gx")
    total = sum(piece.shape[0] for piece in pieces)
    rows = total // count
    wide = orders.shape[1]
    chunk = 512 if wide % 512 == 0 else wide
    scale = 1.0 / math.sqrt(cells_total)
    here = jnp.reshape(lax.axis_index("gx"), (1,)).astype(jnp.int32)

    def body(here, *refs):
        held = refs[: len(pieces)]
        table, orders, out, mixed = refs[len(pieces) :]
        at = 0
        for ref in held:
            for n in range(ref.shape[0] // rows):
                slot = jnp.bitwise_xor(here[0], at)
                mixed[pl.ds(pl.multiple_of(slot * rows, rows), rows), :] = ref[n * rows : n * rows + rows, :]
                at += 1
        both = jnp.dot(table[...], mixed[...], precision=lax.Precision.HIGHEST, preferred_element_type=F32)
        parts = []
        for c in range(2):
            cosine = both[2 * c * KSPAN : (2 * c + 1) * KSPAN]
            sine = both[(2 * c + 1) * KSPAN : (2 * c + 2) * KSPAN]
            parts.append((cosine[:, :KSPAN] - sine[:, KSPAN:]) * scale)
            parts.append((cosine[:, KSPAN:] + sine[:, :KSPAN]) * -scale)
        spectrum = jnp.concatenate(parts, axis=0)
        high = spectrum.astype(jnp.bfloat16)
        rest = spectrum - high.astype(F32)
        mid = rest.astype(jnp.bfloat16)
        low = (rest - mid.astype(F32)).astype(jnp.bfloat16)
        split = jnp.concatenate([high, mid, low], axis=1)
        for n in range(wide // chunk):
            span = slice(n * chunk, n * chunk + chunk)
            index_x = orders[0:1, span] + KSPAN // 2
            index_y = orders[1:2, span] + KSPAN // 2
            waves = lax.broadcasted_iota(jnp.int32, (KSPAN, chunk), 0)
            hit_y = (waves == index_y).astype(F32).astype(jnp.bfloat16)
            hit_x = waves == index_x
            hits = jnp.concatenate([hit_y] * 3, axis=0)
            lines = jnp.dot(split, hits, preferred_element_type=F32)
            for q in range(4):
                line = jnp.where(hit_x, lines[q * KSPAN : (q + 1) * KSPAN], 0.0)
                out[q : q + 1, span] = jnp.sum(line, axis=0, keepdims=True)

    return pl.pallas_call(
        body,
        name="pick_orders",
        out_shape=jax.ShapeDtypeStruct((4, wide), F32),
        in_specs=[SMEM] + [VMEM] * (len(pieces) + 2),
        out_specs=VMEM,
        scratch_shapes=[pltpu.VMEM((total, 2 * KSPAN), F32)],
        compiler_params=params(),
    )(here, *pieces, table, orders)


def shards(
    e_field,
    h_field,
    polar,
    current,
    psi_h,
    psi_e,
    material,
    inv_eps_table,
    decay_table,
    drive_table,
    strength_table,
    spring_table,
    orders,
):
    planes, depth, width = material.shape
    layers = psi_h.shape[2]
    count = lax.axis_size("gx")
    tables = (inv_eps_table, decay_table, drive_table, strength_table, spring_table)

    back, ahead, psi_edge = first_message(e_field, h_field, psi_h, material, inv_eps_table)
    from_ahead, from_behind = passed_along(back, -1), passed_along(ahead, 1)
    found = first_interior((e_field, h_field, polar, current), (psi_h, psi_e), material, tables, ahead, psi_edge)
    state, mats = found[:6], found[6:]
    inv_ahead = from_ahead[2 * depth :]
    inv_behind = from_behind[2 * depth :]
    for step in range(1, STEPS):
        state, back, ahead = boundary(state, mats[0], from_ahead, from_behind, layers)
        from_ahead, from_behind = passed_along(back, -1), passed_along(ahead, 1)
        if step < STEPS - 1:
            state = interior(state, mats, layers)
    state, mixed, outs = last_interior(
        state, mats, back, inv_ahead, inv_behind, jnp.asarray(y_table(width)), layers
    )
    pieces = gathered(mixed)
    outs = last_boundary(state, mats[0], from_ahead, from_behind, outs, layers)
    pupil = pick_orders(pieces, jnp.asarray(x_table(planes, count)), orders, planes * count * width)
    return (*outs, pupil)


def solution(mesh):
    split = P(None, ("mask", "gx"), None, None)
    in_specs = (split,) * 6 + (P(("mask", "gx"), None, None),) + (P(),) * 6
    out_specs = (split,) * 6 + (P(None, "mask"),)
    return jax.shard_map(shards, mesh=mesh, in_specs=in_specs, out_specs=out_specs, check_vma=False)
```

time: 216 us -> 64.5 us (0.30)
  waiting for transfers between devices: 116 us -> 12.7 us
  other arithmetic: 35.5 us -> 0 us
  local copies, waits for them, and re-layouts: 39 us -> 14.7 us
  Pallas kernels: 0 us -> 21.7 us
  between operations: 15 us -> 0.86 us
  starting transfers between devices: 6.09 us -> 13.9 us
    psum x1 -> x0, waiting for transfers between devices: 86.3 us -> none  [shards(): spectrum = lax.psum(partial_spectrum, 'gx')]
    pallas_call x0 -> x10, Pallas kernels: none -> 21.7 us  [the longest x1 6.42 us: first_interior(): pl.pallas_call(body, name='first_interior', out_shape=(*state_shapes(plan...]
    add x19 -> x0, other arithmetic: 19.5 us -> none  [the longest x3 14.6 us: lookup(): total = total + jnp.where(material == index, table[index], 0.0)]
    ppermute x8 -> x14, waiting for transfers between devices: 30.1 us -> 12.7 us  [the longest x8 10.9 us: passed_along(): return lax.ppermute(value, 'gx', pairs)]
    gather x1 -> x0, local copies, waits for them, and re-layouts: 14.2 us -> none  [pick_orders(): return jnp.take(flat, index, axis=1)]
    slice x57 -> x2, local copies, waits for them, and re-layouts: 8.26 us -> 0.01 us  [the longest x1 0.01 us: shards(): inv_behind = from_behind[2 * depth:]]
    ppermute x8 -> x14, starting transfers between devices: 6.06 us -> 13.9 us  [the longest x8 7.67 us: passed_along(): return lax.ppermute(value, 'gx', pairs)]
    sub x17 -> x0, other arithmetic: 5.42 us -> none  [the longest x1 1.73 us: h_update(): hz_new = h_z - COURANT * (ey_ahead - e_y - y_forward(e_x))]
  transfers between devices with their start and end apart: 9 -> 14, of which waited for: 8 -> 6; matrix products, arithmetic and copies ran while one was open for 15% -> 7% of each run, Pallas kernels for 0% -> 20%
where the time goes in v1:
time: 64.5 us; the launch traced here: 63.9 us
  Pallas kernels  21.7 us (34%)
  local copies, waits for them, and re-layouts  14.7 us (23%)
  starting transfers between devices  13.9 us (22%)
  waiting for transfers between devices  12.7 us (20%)
  between operations  0.86 us (1%)
    unnamed x43, local copies, waits for them, and re-layouts  14.1 us
    ppermute x8, waiting for transfers between devices, passed_along(): return lax.ppermute(value, 'gx', pairs)  10.9 us
    ppermute x8, starting transfers between devices, passed_along(): return lax.ppermute(value, 'gx', pairs)  7.67 us
    pallas_call x1, Pallas kernels, first_interior(): pl.pallas_call(body, name='first_interior', out_shape=(*state_shapes(plan...  6.42 us
    ppermute x6, starting transfers between devices, swapped(): lax.ppermute(value, 'gx', [(source, source ^ mask) for source in range(co...  6.25 us
    pallas_call x1, Pallas kernels, last_interior(): pl.pallas_call(body, name='last_interior', out_shape=(*state_shapes(plane...  4.75 us
    pallas_call x1, Pallas kernels, pick_orders(): pl.pallas_call(body, name='pick_orders', out_shape=jax.ShapeDtypeStruct((...  3.17 us
    pallas_call x2, Pallas kernels, interior(): pl.pallas_call(body, name='interior', out_shape=state_shapes(planes, dept...  3.16 us
  transfers between devices with their start and end apart: 14, of which 6 were waited for; matrix products, arithmetic and copies ran while one was open for 7% of the time, Pallas kernels for 20%

profile of v1, /device:TPU:0, one launch (start us, length us, event | category | flops | bytes accessed | tf_op | source)
XLA Modules:
  0.0 63.9 jit_solution(12553543016617159568)
XLA Ops:
  0.6 1.0 %copy.59.psi_in.ph_in = f32[2,6,6,768]{3,2,1,0:T(8,128)S(1)} copy(f32[2,6,6,768]{3,0,2,1:T(2,128)} %param.19) | data formatting | bytes 442368 | tf_op args[4]
  1.6 0.0 copy-start
  1.6 1.3 %copy-done = f32[3,6,24,768]{3,2,1,0:T(8,128)S(1)} copy-done((f32[3,6,24,768]{3,2,1,0:T(8,128)S(1)}, f32[3,6,24,768]{3,2,1,0:T(8,128)}, u32[]{:S(2)}) %copy-start) | copy-done | bytes 1327128
  2.9 1.3 %copy-done.1 = f32[3,6,24,768]{3,2,1,0:T(8,128)S(1)} copy-done((f32[3,6,24,768]{3,2,1,0:T(8,128)S(1)}, f32[3,6,24,768]{3,2,1,0:T(8,128)}, u32[]{:S(2)}) %copy-start.1) | copy-done | bytes 1327128
  4.3 1.0 %copy-done.2 = s32[6,24,768]{2,1,0:T(8,128)S(1)} copy-done((s32[6,24,768]{2,1,0:T(8,128)S(1)}, s32[6,24,768]{2,1,0:T(8,128)}, u32[]{:S(2)}) %copy-start.2) | copy-done | bytes 442392
  5.3 0.7 %copy-done.11 = f32[4]{0:T(128)S(1)} copy-done((f32[4]{0:T(128)S(1)}, f32[4]{0:T(128)}, u32[]{:S(2)}) %copy-start.11) | copy-done | bytes 40
  5.9 0.0 copy-start.13
  6.0 0.0 copy-start.14
  6.0 0.0 copy-start.15
  6.0 0.0 copy-start.16
  6.0 1.2 %first_message.1 = (f32[56,768]{1,0:T(8,128)S(1)}, f32[56,768]{1,0:T(8,128)S(1)}, f32[8,768]{1,0:T(8,128)S(1)}) custom-call(f32[3,6,24,768]{3,2,1,0:T(8,128)S(1)} %copy-done, f32[3,6,24,768]{3,2,1,0:T(8,128)S(1)} %copy-done.1, f32[2,6,6,768]{3,2,1,0:T(8,128)S(1)} %copy.59.psi_in.ph_in, s32[6,24,768]{2,1,0:T(8,128)S(1)} %copy-done.2, f32[4]{0:T(128)S(1)} %copy-done.11), custom_call_target="tpu_custom_call" | custom-call | tf_op jit(solution)/shard_map/first_message/pallas_call | solution.py:219
  7.2 0.5 collective-permute-start.1
  7.7 5.0 %collective-permute-start = (f32[56,768]{1,0:T(8,128)S(1)}, f32[56,768]{1,0:T(8,128)S(1)}, u32[]{:S(2)}, u32[]{:S(2)}) collective-permute-start(f32[56,768]{1,0:T(8,128)S(1)} %get-tuple-element.70), channel_id=1, source_target_pairs={{0,15},{1,0},{2,1},{3,2},{4,3},{5,4},{6,5},{7,6},{8,7},{9,8},{10,9... | collective-permute-start | bytes 516104 | tf_op jit(solution)/shard_map/ppermute | solution.py:34
  12.9 6.4 %first_interior.1 = (f32[3,6,24,768]{3,2,1,0:T(8,128)S(1)}, f32[3,6,24,768]{3,2,1,0:T(8,128)S(1)}, f32[3,6,24,768]{3,2,1,0:T(8,128)S(1)}, f32[3,6,24,768]{3,2,1,...) custom-call(f32[3,6,24,768]{3,2,1,0:T(8,128)S(1)} %copy-done, ...), custom_call_target="tpu_custom_call" | custom-call | tf_op jit(solution)/shard_map/first_interior/pallas_call | solution.py:320
  19.3 0.2 boundary.3
  19.5 1.0 %collective-permute-start.2 = (f32[48,768]{1,0:T(8,128)S(1)}, f32[48,768]{1,0:T(8,128)S(1)}, u32[]{:S(2)}, u32[]{:S(2)}) collective-permute-start(f32[48,768]{1,0:T(8,128)S(1)} %get-tuple-element.84), channel_id=1, source_target_pairs={{0,15},{1,0},{2,1},{3,2},{4,3},{5,4},{6,5},{7,6},{8,7},{9,8},{10,9... | collective-permute-start | bytes 442376 | tf_op jit(solution)/shard_map/ppermute | solution.py:34
  20.5 1.6 %interior.2 = (f32[3,6,24,768]{3,2,1,0:T(8,128)S(1)}, f32[3,6,24,768]{3,2,1,0:T(8,128)S(1)}, f32[3,6,24,768]{3,2,1,0:T(8,128)S(1)}, f32[3,6,24,768]{3,2,1,0:T(8,...) custom-call(f32[3,6,24,768]{3,2,1,0:T(8,128)S(1)} %get-tuple-element, ...), custom_call_target="tpu_custom_call", output_to_operand_aliasing={{0}: (0, {}), {1}: (1, {}), {2}: (2, {}), {3}: (3, {}), {4}... | custom-call | tf_op jit(solution)/shard_map/interior/pallas_call | solution.py:345
  22.1 1.1 %collective-permute-done.2.from_ahead = f32[48,768]{1,0:T(8,128)S(1)} collective-permute-done((f32[48,768]{1,0:T(8,128)S(1)}, f32[48,768]{1,0:T(8,128)S(1)}, u32[]{:S(2)}, u32[]{:S(2)}) %collective-permute-start.2) | collective-permute-done | bytes 147488 | tf_op jit(solution)/shard_map/ppermute | solution.py:34
  23.2 4.6 %collective-permute-done.3.from_behind = f32[48,768]{1,0:T(8,128)S(1)} collective-permute-done((f32[48,768]{1,0:T(8,128)S(1)}, f32[48,768]{1,0:T(8,128)S(1)}, u32[]{:S(2)}, u32[]{:S(2)}) %collective-permute-start.3) | collective-permute-done | bytes 147488 | tf_op jit(solution)/shard_map/ppermute | solution.py:34
  27.8 0.2 boundary.4
  28.0 0.1 collective-permute-start.4
  28.1 0.5 collective-permute-start.5
  28.6 1.6 %interior.3 = (f32[3,6,24,768]{3,2,1,0:T(8,128)S(1)}, f32[3,6,24,768]{3,2,1,0:T(8,128)S(1)}, f32[3,6,24,768]{3,2,1,0:T(8,128)S(1)}, f32[3,6,24,768]{3,2,1,0:T(8,...) custom-call(f32[3,6,24,768]{3,2,1,0:T(8,128)S(1)} %get-tuple-element, ...), custom_call_target="tpu_custom_call", output_to_operand_aliasing={{0}: (0, {}), {1}: (1, {}), {2}: (2, {}), {3}: (3, {}), {4}... | custom-call | tf_op jit(solution)/shard_map/interior/pallas_call | solution.py:345
  30.2 0.6 collective-permute-done.4.from_ahead
  30.7 4.6 %collective-permute-done.5.from_behind = f32[48,768]{1,0:T(8,128)S(1)} collective-permute-done((f32[48,768]{1,0:T(8,128)S(1)}, f32[48,768]{1,0:T(8,128)S(1)}, u32[]{:S(2)}, u32[]{:S(2)}) %collective-permute-start.5) | collective-permute-done | bytes 147488 | tf_op jit(solution)/shard_map/ppermute | solution.py:34
  35.4 0.9 %boundary.5 = (f32[3,6,24,768]{3,2,1,0:T(8,128)S(1)}, f32[3,6,24,768]{3,2,1,0:T(8,128)S(1)}, f32[2,6,8,768]{3,2,1,0:T(8,128)S(1)}, f32[2,6,8,768]{3,2,1,0:T(8,12...) custom-call(f32[3,6,24,768]{3,2,1,0:T(8,128)S(1)} %get-tuple-element, ...), custom_call_target="tpu_custom_call", output_to_operand_aliasing={{0}: (0, {}), {1}: (1, {}), {2}: (2, {}), {3}: (3, {})} | custom-call | tf_op jit(solution)/shard_map/boundary/pallas_call | solution.py:405
  36.3 0.1 copy-done.7
  36.4 4.8 %last_interior.1 = (f32[3,6,24,768]{3,2,1,0:T(8,128)S(1)}, f32[3,6,24,768]{3,2,1,0:T(8,128)S(1)}, f32[3,6,24,768]{3,2,1,0:T(8,128)S(1)}, f32[3,6,24,768]{3,2,1,0...) custom-call(f32[3,6,24,768]{3,2,1,0:T(8,128)S(1)} %get-tuple-element, ...), custom_call_target="tpu_custom_call", output_to_operand_aliasing={{0}: (0, {}), {1}: (1, {}), {2}: (2, {}), {3}: (3, {}), {4}... | custom-call | tf_op jit(solution)/shard_map/last_interior/pallas_call | solution.py:474
  41.2 0.7 %copy-done.5 = f32[2,6,6,768]{3,2,1,0:T(8,128)} copy-done((f32[2,6,6,768]{3,2,1,0:T(8,128)}, f32[2,6,6,768]{3,2,1,0:T(8,128)S(1)}, u32[]{:S(2)}) %copy-start.5) | copy-done | bytes 221208
  41.9 0.7 %copy-done.8 = f32[2,6,6,768]{3,2,1,0:T(8,128)} copy-done((f32[2,6,6,768]{3,2,1,0:T(8,128)}, f32[2,6,6,768]{3,2,1,0:T(8,128)S(1)}, u32[]{:S(2)}) %copy-start.8) | copy-done | bytes 221208
  42.6 0.6 constant_dynamic-update-slice_fusion.3
  43.2 1.9 %collective-permute-start.10 = (f32[16,128]{1,0:T(8,128)S(1)}, f32[16,128]{1,0:T(8,128)S(1)}, u32[]{:S(2)}, u32[]{:S(2)}) collective-permute-start(f32[16,128]{1,0:T(8,128)S(1)} %get-tuple-element.118), channel_id=1, source_target_pairs={{0,3},{1,2},{2,1},{3,0},{4,7},{5,6},{6,5},{7,4},{8,11},{9,10},{10,... | collective-permute-start | bytes 24584 | tf_op jit(solution)/shard_map/ppermute | solution.py:39
  45.0 0.2 collective-permute-start.6
  45.3 0.3 collective-permute-start.7
  45.6 0.6 constant_dynamic-update-slice_fusion.2
  46.1 0.7 %collective-permute-done.9 = f32[16,128]{1,0:T(8,128)S(1)} collective-permute-done((f32[16,128]{1,0:T(8,128)S(1)}, f32[16,128]{1,0:T(8,128)S(1)}, u32[]{:S(2)}, u32[]{:S(2)}) %collective-permute-start.9) | collective-permute-done | bytes 8224 | tf_op jit(solution)/shard_map/ppermute | solution.py:39
  46.8 0.6 constant_dynamic-update-slice_fusion.1
  47.4 0.6 constant_dynamic-update-slice_fusion.refs_0_
  48.0 0.3 collective-permute-start.11
  48.3 4.1 %collective-permute-start.13 = (f32[64,128]{1,0:T(8,128)}, f32[64,128]{1,0:T(8,128)}, u32[]{:S(2)}, u32[]{:S(2)}) collective-permute-start(f32[64,128]{1,0:T(8,128)} %constant_dynamic-update-slice_fusion.refs_0_), channel_id=1, source_target_pairs={{0,12},{1,13},{2,14},{3,15},{4,8},{5,9},{6,10},{7,11},{8,4},{9,5},... | collective-permute-start | bytes 98312 | tf_op jit(solution)/shard_map/ppermute | solution.py:39
  52.4 1.8 %copy.61 = f32[2,6,6,768]{3,0,2,1:T(2,128)} copy(f32[2,6,6,768]{3,2,1,0:T(8,128)} %copy-done.8) | data formatting | bytes 442368
  54.2 1.1 %collective-permute-done.13.refs_3_ = f32[64,128]{1,0:T(8,128)} collective-permute-done((f32[64,128]{1,0:T(8,128)}, f32[64,128]{1,0:T(8,128)}, u32[]{:S(2)}, u32[]{:S(2)}) %collective-permute-start.13) | collective-permute-done | bytes 32800 | tf_op jit(solution)/shard_map/ppermute | solution.py:39
  55.4 0.9 %copy-done.9 = f32[256,256]{1,0:T(8,128)S(1)} copy-done((f32[256,256]{1,0:T(8,128)S(1)}, f32[256,256]{1,0:T(8,128)}, u32[]{:S(2)}) %copy-start.9) | copy-done | bytes 262168
  56.3 0.8 %copy-done.10 = s32[2,4096]{1,0:T(2,128)S(1)} copy-done((s32[2,4096]{1,0:T(2,128)S(1)}, s32[2,4096]{1,0:T(2,128)}, u32[]{:S(2)}) %copy-start.10) | copy-done | bytes 32792
  57.1 3.2 %pick_orders.1 = f32[4,4096]{1,0:T(4,128)} custom-call(s32[1]{0:T(128)} %bitcast.here, f32[64,128]{1,0:T(8,128)} %constant_dynamic-update-slice_fusion.refs_0_, f32[64,128]{1,0:T(8,128)} %collective-permute-done.11.refs_1_, f32[64,128]{1,0:T(8,128)} %collective-permute-done.12.refs_2_, f32[64,128]{1,0:T(8,128)} %collective-permute-done.13.refs_3_, ...), custom_call_target="tpu_custom_call" | custom-call | tf_op jit(solution)/shard_map/pick_orders/pallas_call | solution.py:611
  60.3 1.0 %copy-done.6 = f32[2,6,6,768]{3,2,1,0:T(8,128)S(1)} copy-done((f32[2,6,6,768]{3,2,1,0:T(8,128)S(1)}, f32[2,6,6,768]{3,2,1,0:T(8,128)}, u32[]{:S(2)}) %copy-start.6) | copy-done | bytes 221208
  61.2 1.8 %last_boundary.1 = (f32[3,6,24,768]{3,2,1,0:T(8,128)S(1)}, f32[3,6,24,768]{3,2,1,0:T(8,128)S(1)}, f32[2,6,8,768]{3,2,1,0:T(8,128)S(1)}, f32[3,6,24,768]{3,2,1,0:...) custom-call(f32[3,6,24,768]{3,2,1,0:T(8,128)S(1)} %get-tuple-element, ...), custom_call_target="tpu_custom_call", output_to_operand_aliasing={{0}: (0, {}), {1}: (1, {}), {2}: (2, {}), {3}: (6, {}), {4}... | custom-call | tf_op jit(solution)/shard_map/last_boundary/pallas_call | solution.py:515
  63.1 0.9 %copy.62 = f32[2,6,6,768]{3,0,2,1:T(2,128)} copy(f32[2,6,6,768]{3,2,1,0:T(8,128)S(1)} %get-tuple-element.124) | data formatting | bytes 442368
  (36 shorter events, 0.1 us)
Async XLA Ops:
  1.6 1.3 %copy-start = (f32[3,6,24,768]{3,2,1,0:T(8,128)S(1)}, f32[3,6,24,768]{3,2,1,0:T(8,128)}, u32[]{:S(2)}) copy-start(f32[3,6,24,768]{3,2,1,0:T(8,128)} %e_in.3) | copy-start | bytes 3981316
  2.9 1.3 %copy-start.1 = (f32[3,6,24,768]{3,2,1,0:T(8,128)S(1)}, f32[3,6,24,768]{3,2,1,0:T(8,128)}, u32[]{:S(2)}) copy-start(f32[3,6,24,768]{3,2,1,0:T(8,128)} %h_in.3) | copy-start | bytes 3981316
  4.3 1.0 %copy-start.2 = (s32[6,24,768]{2,1,0:T(8,128)S(1)}, s32[6,24,768]{2,1,0:T(8,128)}, u32[]{:S(2)}) copy-start(s32[6,24,768]{2,1,0:T(8,128)} %mat_in.3) | copy-start | bytes 1327108
  5.3 0.7 %copy-start.11 = (f32[4]{0:T(128)S(1)}, f32[4]{0:T(128)}, u32[]{:S(2)}) copy-start(f32[4]{0:T(128)} %t0.1) | copy-start | bytes 52
  5.9 6.8 %copy-start.17 = (f32[2,6,6,768]{3,0,2,1:T(2,128)S(1)}, f32[2,6,6,768]{3,0,2,1:T(2,128)}, u32[]{:S(2)}) copy-start(f32[2,6,6,768]{3,0,2,1:T(2,128)} %param.20) | copy-start | bytes 663556
  5.9 6.9 %copy-start.3 = (f32[3,6,24,768]{3,2,1,0:T(8,128)S(1)}, f32[3,6,24,768]{3,2,1,0:T(8,128)}, u32[]{:S(2)}) copy-start(f32[3,6,24,768]{3,2,1,0:T(8,128)} %p_in.1) | copy-start | bytes 3981316
  5.9 6.9 %copy-start.4 = (f32[3,6,24,768]{3,2,1,0:T(8,128)S(1)}, f32[3,6,24,768]{3,2,1,0:T(8,128)}, u32[]{:S(2)}) copy-start(f32[3,6,24,768]{3,2,1,0:T(8,128)} %c_in.1) | copy-start | bytes 3981316
  5.9 6.9 %copy-start.12 = (f32[4]{0:T(128)S(1)}, f32[4]{0:T(128)}, u32[]{:S(2)}) copy-start(f32[4]{0:T(128)} %t0.1) | copy-start | bytes 52
  5.9 6.9 %copy-start.13 = (f32[4]{0:T(128)S(1)}, f32[4]{0:T(128)}, u32[]{:S(2)}) copy-start(f32[4]{0:T(128)} %t1.1) | copy-start | bytes 52
  6.0 6.9 %copy-start.14 = (f32[4]{0:T(128)S(1)}, f32[4]{0:T(128)}, u32[]{:S(2)}) copy-start(f32[4]{0:T(128)} %t2.1) | copy-start | bytes 52
  6.0 6.9 %copy-start.15 = (f32[4]{0:T(128)S(1)}, f32[4]{0:T(128)}, u32[]{:S(2)}) copy-start(f32[4]{0:T(128)} %t3.1) | copy-start | bytes 52
  6.0 6.9 %copy-start.16 = (f32[4]{0:T(128)S(1)}, f32[4]{0:T(128)}, u32[]{:S(2)}) copy-start(f32[4]{0:T(128)} %t4.1) | copy-start | bytes 52
  7.2 12.1 %collective-permute-start.1 = (f32[56,768]{1,0:T(8,128)S(1)}, f32[56,768]{1,0:T(8,128)S(1)}, u32[]{:S(2)}, u32[]{:S(2)}) collective-permute-start(f32[56,768]{1,0:T(8,128)S(1)} %get-tuple-element.63.ahead), channel_id=1, source_target_pairs={{0,1},{1,2},{2,3},{3,4},{4,5},{5,6},{6,7},{7,8},{8,9},{9,10},{10,1... | collective-permute-start | bytes 516104 | tf_op jit(solution)/shard_map/ppermute | solution.py:34
  7.7 11.6 %collective-permute-start = (f32[56,768]{1,0:T(8,128)S(1)}, f32[56,768]{1,0:T(8,128)S(1)}, u32[]{:S(2)}, u32[]{:S(2)}) collective-permute-start(f32[56,768]{1,0:T(8,128)S(1)} %get-tuple-element.70), channel_id=1, source_target_pairs={{0,15},{1,0},{2,1},{3,2},{4,3},{5,4},{6,5},{7,6},{8,7},{9,8},{10,9... | collective-permute-start | bytes 516104 | tf_op jit(solution)/shard_map/ppermute | solution.py:34
  19.5 3.7 %collective-permute-start.2 = (f32[48,768]{1,0:T(8,128)S(1)}, f32[48,768]{1,0:T(8,128)S(1)}, u32[]{:S(2)}, u32[]{:S(2)}) collective-permute-start(f32[48,768]{1,0:T(8,128)S(1)} %get-tuple-element.84), channel_id=1, source_target_pairs={{0,15},{1,0},{2,1},{3,2},{4,3},{5,4},{6,5},{7,6},{8,7},{9,8},{10,9... | collective-permute-start | bytes 442376 | tf_op jit(solution)/shard_map/ppermute | solution.py:34
  20.5 7.3 %collective-permute-start.3 = (f32[48,768]{1,0:T(8,128)S(1)}, f32[48,768]{1,0:T(8,128)S(1)}, u32[]{:S(2)}, u32[]{:S(2)}) collective-permute-start(f32[48,768]{1,0:T(8,128)S(1)} %get-tuple-element.85), channel_id=1, source_target_pairs={{0,1},{1,2},{2,3},{3,4},{4,5},{5,6},{6,7},{7,8},{8,9},{9,10},{10,1... | collective-permute-start | bytes 442376 | tf_op jit(solution)/shard_map/ppermute | solution.py:34
  28.0 2.7 %collective-permute-start.4 = (f32[48,768]{1,0:T(8,128)S(1)}, f32[48,768]{1,0:T(8,128)S(1)}, u32[]{:S(2)}, u32[]{:S(2)}) collective-permute-start(f32[48,768]{1,0:T(8,128)S(1)} %get-tuple-element.96), channel_id=1, source_target_pairs={{0,15},{1,0},{2,1},{3,2},{4,3},{5,4},{6,5},{7,6},{8,7},{9,8},{10,9... | collective-permute-start | bytes 442376 | tf_op jit(solution)/shard_map/ppermute | solution.py:34
  28.1 7.3 %collective-permute-start.5 = (f32[48,768]{1,0:T(8,128)S(1)}, f32[48,768]{1,0:T(8,128)S(1)}, u32[]{:S(2)}, u32[]{:S(2)}) collective-permute-start(f32[48,768]{1,0:T(8,128)S(1)} %get-tuple-element.97), channel_id=1, source_target_pairs={{0,1},{1,2},{2,3},{3,4},{4,5},{5,6},{6,7},{7,8},{8,9},{9,10},{10,1... | collective-permute-start | bytes 442376 | tf_op jit(solution)/shard_map/ppermute | solution.py:34
  35.4 1.0 %copy-start.7 = (f32[768,128]{1,0:T(8,128)S(1)}, f32[768,128]{1,0:T(8,128)}, u32[]{:S(2)}) copy-start(f32[768,128]{1,0:T(8,128)} %constant.8.clone.refs_13_) | copy-start | bytes 1179652
  41.2 0.7 %copy-start.5 = (f32[2,6,6,768]{3,2,1,0:T(8,128)}, f32[2,6,6,768]{3,2,1,0:T(8,128)S(1)}, u32[]{:S(2)}) copy-start(f32[2,6,6,768]{3,2,1,0:T(8,128)S(1)} %get-tuple-element.111.pe_hbm) | copy-start | bytes 663556
  41.9 0.7 %copy-start.8 = (f32[2,6,6,768]{3,2,1,0:T(8,128)}, f32[2,6,6,768]{3,2,1,0:T(8,128)S(1)}, u32[]{:S(2)}) copy-start(f32[2,6,6,768]{3,2,1,0:T(8,128)S(1)} %get-tuple-element.123) | copy-start | bytes 663556
  42.6 3.0 %collective-permute-start.8 = (f32[16,128]{1,0:T(8,128)S(1)}, f32[16,128]{1,0:T(8,128)S(1)}, u32[]{:S(2)}, u32[]{:S(2)}) collective-permute-start(f32[16,128]{1,0:T(8,128)S(1)} %get-tuple-element.118), channel_id=1, source_target_pairs={{0,1},{1,0},{2,3},{3,2},{4,5},{5,4},{6,7},{7,6},{8,9},{9,8},{10,11... | collective-permute-start | bytes 24584 | tf_op jit(solution)/shard_map/ppermute | solution.py:39
  43.2 3.7 %collective-permute-start.9 = (f32[16,128]{1,0:T(8,128)S(1)}, f32[16,128]{1,0:T(8,128)S(1)}, u32[]{:S(2)}, u32[]{:S(2)}) collective-permute-start(f32[16,128]{1,0:T(8,128)S(1)} %get-tuple-element.118), channel_id=1, source_target_pairs={{0,2},{1,3},{2,0},{3,1},{4,6},{5,7},{6,4},{7,5},{8,10},{9,11},{10,... | collective-permute-start | bytes 24584 | tf_op jit(solution)/shard_map/ppermute | solution.py:39
  43.2 4.3 %collective-permute-start.10 = (f32[16,128]{1,0:T(8,128)S(1)}, f32[16,128]{1,0:T(8,128)S(1)}, u32[]{:S(2)}, u32[]{:S(2)}) collective-permute-start(f32[16,128]{1,0:T(8,128)S(1)} %get-tuple-element.118), channel_id=1, source_target_pairs={{0,3},{1,2},{2,1},{3,0},{4,7},{5,6},{6,5},{7,4},{8,11},{9,10},{10,... | collective-permute-start | bytes 24584 | tf_op jit(solution)/shard_map/ppermute | solution.py:39
  45.0 15.2 %collective-permute-start.6 = (f32[48,768]{1,0:T(8,128)}, f32[48,768]{1,0:T(8,128)S(1)}, u32[]{:S(2)}, u32[]{:S(2)}) collective-permute-start(f32[48,768]{1,0:T(8,128)} %get-tuple-element.104.refs_10_), channel_id=1, source_target_pairs={{0,15},{1,0},{2,1},{3,2},{4,3},{5,4},{6,5},{7,6},{8,7},{9,8},{10,9... | collective-permute-start | bytes 442376 | tf_op jit(solution)/shard_map/ppermute | solution.py:34
  45.3 15.0 %collective-permute-start.7 = (f32[48,768]{1,0:T(8,128)}, f32[48,768]{1,0:T(8,128)}, u32[]{:S(2)}, u32[]{:S(2)}) collective-permute-start(f32[48,768]{1,0:T(8,128)} %get-tuple-element.108), channel_id=1, source_target_pairs={{0,1},{1,2},{2,3},{3,4},{4,5},{5,6},{6,7},{7,8},{8,9},{9,10},{10,1... | collective-permute-start | bytes 442376 | tf_op jit(solution)/shard_map/ppermute | solution.py:34
  48.0 6.2 %collective-permute-start.11 = (f32[64,128]{1,0:T(8,128)}, f32[64,128]{1,0:T(8,128)}, u32[]{:S(2)}, u32[]{:S(2)}) collective-permute-start(f32[64,128]{1,0:T(8,128)} %constant_dynamic-update-slice_fusion.refs_0_), channel_id=1, source_target_pairs={{0,4},{1,5},{2,6},{3,7},{4,0},{5,1},{6,2},{7,3},{8,12},{9,13},{10,... | collective-permute-start | bytes 98312 | tf_op jit(solution)/shard_map/ppermute | solution.py:39
  48.3 5.9 %collective-permute-start.12 = (f32[64,128]{1,0:T(8,128)}, f32[64,128]{1,0:T(8,128)}, u32[]{:S(2)}, u32[]{:S(2)}) collective-permute-start(f32[64,128]{1,0:T(8,128)} %constant_dynamic-update-slice_fusion.refs_0_), channel_id=1, source_target_pairs={{0,8},{1,9},{2,10},{3,11},{4,12},{5,13},{6,14},{7,15},{8,0},{9,1},... | collective-permute-start | bytes 98312 | tf_op jit(solution)/shard_map/ppermute | solution.py:39
  48.3 7.1 %collective-permute-start.13 = (f32[64,128]{1,0:T(8,128)}, f32[64,128]{1,0:T(8,128)}, u32[]{:S(2)}, u32[]{:S(2)}) collective-permute-start(f32[64,128]{1,0:T(8,128)} %constant_dynamic-update-slice_fusion.refs_0_), channel_id=1, source_target_pairs={{0,12},{1,13},{2,14},{3,15},{4,8},{5,9},{6,10},{7,11},{8,4},{9,5},... | collective-permute-start | bytes 98312 | tf_op jit(solution)/shard_map/ppermute | solution.py:39
  55.4 1.0 %copy-start.9 = (f32[256,256]{1,0:T(8,128)S(1)}, f32[256,256]{1,0:T(8,128)}, u32[]{:S(2)}) copy-start(f32[256,256]{1,0:T(8,128)} %constant.9.clone.refs_4_) | copy-start | bytes 786436
  56.3 0.8 %copy-start.10 = (s32[2,4096]{1,0:T(2,128)S(1)}, s32[2,4096]{1,0:T(2,128)}, u32[]{:S(2)}) copy-start(s32[2,4096]{1,0:T(2,128)} %refs_5_.1) | copy-start | bytes 98308
  60.3 1.0 %copy-start.6 = (f32[2,6,6,768]{3,2,1,0:T(8,128)S(1)}, f32[2,6,6,768]{3,2,1,0:T(8,128)}, u32[]{:S(2)}) copy-start(f32[2,6,6,768]{3,2,1,0:T(8,128)} %copy-done.5) | copy-start | bytes 663556

commit v2 on v1

--- a/solution.py
+++ b/solution.py
@@ -8,6 +8,7 @@
 from jax.experimental.pallas import tpu as pltpu
 from jax.sharding import PartitionSpec as P
 
+
 KSPAN = 64
 STEPS = 4
 
@@ -28,10 +29,47 @@
     return pltpu.CompilerParams(vmem_limit_bytes=24 << 20)
 
 
-def passed_along(value, steps):
+def in_hbm(value):
+    return pltpu.with_memory_space_constraint(value, pltpu.HBM)
+
+
+def exchanged(near, far):
     count = lax.axis_size("gx")
-    pairs = [(source, (source + steps) % count) for source in range(count)]
-    return lax.ppermute(value, "gx", pairs)
+    assert count % 2 == 0
+    odd = range(1, count, 2)
+    pairs = [(i, (i + 1) % count) for i in odd] + [((i + 1) % count, i) for i in odd]
+    far = lax.ppermute(far, "gx", pairs)
+    pairs = [(i, i - 1) for i in odd] + [(i - 1, i) for i in odd]
+    near = lax.ppermute(near, "gx", pairs)
+    return near, far
+
+
+def is_odd():
+    return lax.rem(lax.axis_index("gx"), 2) == 1
+
+
+def sort_out(back, ahead, near, far):
+    @pl.when(is_odd())
+    def _():
+        near[...] = back[...]
+        far[...] = ahead[...]
+
+    @pl.when(jnp.logical_not(is_odd()))
+    def _():
+        near[...] = ahead[...]
+        far[...] = back[...]
+
+
+def sort_in(near, far, from_ahead, from_behind):
+    @pl.when(is_odd())
+    def _():
+        from_behind[...] = near[...]
+        from_ahead[...] = far[...]
+
+    @pl.when(jnp.logical_not(is_odd()))
+    def _():
+        from_ahead[...] = near[...]
+        from_behind[...] = far[...]
 
 
 def swapped(value, mask):
@@ -94,7 +132,7 @@
     return total
 
 
-def h_plane(e, h, psi_h, i, tiles, coef, last):
+def h_plane(e, h_in, h, psi_h, i, tiles, coef, last):
     decay, gain = coef
     for k in range(tiles):
         ex, ey, ez = (tile_of(e, (c, i), k) for c in range(3))
@@ -104,7 +142,7 @@
             memory = decay * psi_h[0, i] + gain * dey_dz
             psi_h[0, i] = memory
             curl = curl - memory
-        put_tile(h, (0, i), k, tile_of(h, (0, i), k) - COURANT * curl)
+        put_tile(h, (0, i), k, tile_of(h_in, (0, i), k) - COURANT * curl)
         if last:
             continue
         dex_dz = z_forward(e, (0, i), k, tiles, ex)
@@ -113,18 +151,19 @@
             memory = decay * psi_h[1, i] + gain * dex_dz
             psi_h[1, i] = memory
             curl = curl + memory
-        put_tile(h, (1, i), k, tile_of(h, (1, i), k) - COURANT * curl)
+        put_tile(h, (1, i), k, tile_of(h_in, (1, i), k) - COURANT * curl)
         curl = tile_of(e, (1, i + 1), k) - ey - y_forward(ex)
-        put_tile(h, (2, i), k, tile_of(h, (2, i), k) - COURANT * curl)
-
-
-def e_plane(e, h, polar, current, psi_e, mats, i, tiles, coef, first=False, last=False):
-    inv_eps, decay_j, pull, spring = mats
+        put_tile(h, (2, i), k, tile_of(h_in, (2, i), k) - COURANT * curl)
+
+
+def e_plane(old_state, new_state, h, psi_e, mats, i, tiles, coef, first=False, last=False):
+    e_in, polar_in, current_in = old_state
+    e, polar, current = new_state
     decay, gain = coef
     for k in range(tiles):
         hx = tile_of(h, (0, i), k)
         dhx_dz = z_backward(h, (0, i), k, hx)
-        old = [tile_of(e, (c, i), k) for c in range(3)]
+        old = [tile_of(e_in, (c, i), k) for c in range(3)]
         curl_y = dhx_dz
         curl_z = -y_backward(hx)
         curl_x = None
@@ -150,8 +189,8 @@
             curl_z = curl_z - tile_of(h, (1, i - 1), k)
         inv, dec, drv, spr = (tile_of(m, (i,), k) for m in mats)
         for c, curl in enumerate((curl_x, curl_y, curl_z)):
-            pol = tile_of(polar, (c, i), k)
-            cur = dec * tile_of(current, (c, i), k) + (drv * old[c] - spr * pol)
+            pol = tile_of(polar_in, (c, i), k)
+            cur = dec * tile_of(current_in, (c, i), k) + (drv * old[c] - spr * pol)
             put_tile(current, (c, i), k, cur)
             put_tile(polar, (c, i), k, pol + cur)
             change = -cur if curl is None else COURANT * curl - cur
@@ -184,26 +223,28 @@
 
 def first_message(e_field, h_field, psi_h, material, inv_table):
     planes, depth, width = e_field.shape[1:]
-    layers = psi_h.shape[2]
+    layers = psi_h.shape[1]
     tiles = depth // ROWS
     edge = planes - 1
     probe = layers // ROWS * ROWS
 
-    def body(e_in, h_in, psi_in, mat_in, table, back, ahead, psi_out, e, h, psi, mat, sem):
+    def body(e_in, h_in, psi_in, mat_in, table, near, far, ahead, psi_out, back, e, h, psi_rows, psi, mat, sem):
         wanted = [
             (e_in.at[1, 0], back.at[0:depth]),
             (e_in.at[2, 0], back.at[depth : 2 * depth]),
             (e_in.at[:, edge], e),
             (h_in.at[1:3, edge], h),
-            (psi_in.at[1, edge], psi.at[0:layers]),
+            (psi_in.at[edge], psi_rows),
             (mat_in.at[0, probe : probe + ROWS], mat.at[0]),
             (mat_in.at[edge, probe : probe + ROWS], mat.at[1]),
         ]
-        psi[...] = jnp.zeros_like(psi)
         copies = [pltpu.make_async_copy(s, d, sem.at[n]) for n, (s, d) in enumerate(wanted)]
         start_all(copies)
+        psi[...] = jnp.zeros_like(psi)
         coef = pml(layers, 0.5, width)
         wait_all(copies)
+        for z in range(layers):
+            psi[z : z + 1, :] = psi_rows[z, 1:2, :]
         back[2 * depth : 2 * depth + ROWS, :] = lookup(mat[0], table)
         ahead[2 * depth : 2 * depth + ROWS, :] = lookup(mat[1], table)
 
@@ -214,37 +255,52 @@
             part_y, part_z = sent_ahead(e, h, psi[...], put_psi, lambda c: (c,), lambda c: (c,), k, tiles, coef)
             put_tile(ahead, (), k, part_y)
             put_tile(ahead, (), tiles + k, part_z)
+        sort_out(back, ahead, near, far)
 
     message = pltpu.VMEM((2 * depth + ROWS, width), F32)
     return pl.pallas_call(
         body,
         name="first_message",
-        out_shape=(message, message, pltpu.VMEM((ROWS, width), F32)),
+        out_shape=(message, message, message, pltpu.VMEM((ROWS, width), F32)),
         in_specs=[HBM, HBM, HBM, HBM, SMEM],
-        out_specs=(VMEM, VMEM, VMEM),
+        out_specs=(VMEM, VMEM, VMEM, VMEM),
         scratch_shapes=[
+            message,
             pltpu.VMEM((3, depth, width), F32),
             pltpu.VMEM((2, depth, width), F32),
+            pltpu.VMEM((layers, 2, width), F32),
             pltpu.VMEM((ROWS, width), F32),
             pltpu.VMEM((2, ROWS, width), jnp.int32),
             pltpu.SemaphoreType.DMA((7,)),
         ],
         compiler_params=params(),
-    )(e_field, h_field, psi_h, material, inv_table)
-
-
-def all_planes(e, h, polar, current, psi_h, psi_e, mats, planes, tiles, coef_h, coef_e):
-    h_plane(e, h, psi_h, 0, tiles, coef_h, False)
-    e_plane(e, h, polar, current, psi_e, mats, 0, tiles, coef_e, first=True)
+    )(*(in_hbm(x) for x in (e_field, h_field, psi_h, material)), inv_table)
+
+
+def all_planes(old_state, new_state, h_in, h, psi_h, psi_e, mats, planes, tiles, coef_h, coef_e, ahead=None, arrive=None):
+    e = old_state[0]
+    edge = planes - 1
+    if arrive is not None:
+        arrive(0)
+    h_plane(e, h_in, h, psi_h, 0, tiles, coef_h, False)
+    e_plane(old_state, new_state, h, psi_e, mats, 0, tiles, coef_e, first=True)
 
     def step(i, carry):
-        h_plane(e, h, psi_h, i, tiles, coef_h, False)
-        e_plane(e, h, polar, current, psi_e, mats, i, tiles, coef_e)
+        if arrive is not None:
+            arrive(i)
+        h_plane(e, h_in, h, psi_h, i, tiles, coef_h, False)
+        e_plane(old_state, new_state, h, psi_e, mats, i, tiles, coef_e)
         return carry
 
-    lax.fori_loop(1, planes - 1, step, 0)
-    h_plane(e, h, psi_h, planes - 1, tiles, coef_h, True)
-    e_plane(e, h, polar, current, psi_e, mats, planes - 1, tiles, coef_e, last=True)
+    lax.fori_loop(1, edge, step, 0)
+    if arrive is not None:
+        arrive(edge)
+    h_plane(e, h_in, h, psi_h, edge, tiles, coef_h, True)
+    if ahead is not None:
+        for k in range(tiles):
+            put_tile(h, (1, edge), k, tile_of(ahead, (), k))
+            put_tile(h, (2, edge), k, tile_of(ahead, (), tiles + k))
+    e_plane(old_state, new_state, h, psi_e, mats, edge, tiles, coef_e, last=True)
 
 
 def state_shapes(planes, depth, width):
@@ -255,34 +311,27 @@
 
 def first_interior(fields, memories, material, tables, ahead, psi_edge):
     planes, depth, width = material.shape
-    layers = memories[0].shape[2]
+    layers = memories[0].shape[1]
     tiles = depth // ROWS
     edge = planes - 1
 
-    def body(e_in, h_in, p_in, c_in, ph_in, pe_in, mat_in, t0, t1, t2, t3, t4, ahead, psi_edge, *rest):
-        e, h, polar, current, psi_h, psi_e, inv, dec, drv, spr, mat, sem = rest
+    def body(e_in, h_in, p_in, c_in, ph_in, pe_in, mat, t0, t1, t2, t3, t4, ahead, psi_edge, *rest):
+        e, h, polar, current, psi_h, psi_e, inv, dec, drv, spr = rest
         zero = jnp.zeros((ROWS, width), F32)
         for c in range(2):
             for i in range(planes):
                 psi_h[c, i] = zero
                 psi_e[c, i] = zero
-        pairs = [(e_in, e), (h_in, h), (p_in, polar), (c_in, current)]
-
-        def copies(i):
-            found = [pltpu.make_async_copy(s.at[:, i], d.at[:, i], sem.at[n, i]) for n, (s, d) in enumerate(pairs)]
-            found.append(pltpu.make_async_copy(ph_in.at[:, i], psi_h.at[:, i, 0:layers], sem.at[4, i]))
-            found.append(pltpu.make_async_copy(pe_in.at[:, i], psi_e.at[:, i, 0:layers], sem.at[5, i]))
-            found.append(pltpu.make_async_copy(mat_in.at[i], mat.at[i], sem.at[6, i]))
-            return found
-
-        for i in range(planes):
-            start_all(copies(i))
         coef_h = pml(layers, 0.5, width)
         coef_e = pml(layers, 0.0, width)
-        mats = (inv, dec, drv, spr)
 
         def arrive(i):
-            wait_all(copies(i))
+            for z in range(layers):
+                for c in range(2):
+                    psi_h[c, i, z : z + 1, :] = ph_in[i, z, c : c + 1, :]
+                    psi_e[c, i, z : z + 1, :] = pe_in[i, z, c : c + 1, :]
+            if isinstance(i, int) and i == edge:
+                psi_h[1, edge] = psi_edge[...]
             for k in range(tiles):
                 m = tile_of(mat, (i,), k)
                 put_tile(inv, (i,), k, lookup(m, t0))
@@ -291,42 +340,19 @@
                 put_tile(drv, (i,), k, drive * lookup(m, t3))
                 put_tile(spr, (i,), k, drive * lookup(m, t4))
 
-        arrive(0)
-
-        def step(i, carry):
-            arrive(i + 1)
-            h_plane(e, h, psi_h, i, tiles, coef_h, False)
-            return carry
-
-        arrive(1)
-        h_plane(e, h, psi_h, 0, tiles, coef_h, False)
-        e_plane(e, h, polar, current, psi_e, mats, 0, tiles, coef_e, first=True)
-
-        def step(i, carry):
-            arrive(i + 1)
-            h_plane(e, h, psi_h, i, tiles, coef_h, False)
-            e_plane(e, h, polar, current, psi_e, mats, i, tiles, coef_e)
-            return carry
-
-        lax.fori_loop(1, edge, step, 0)
-        h_plane(e, h, psi_h, edge, tiles, coef_h, True)
-        for k in range(tiles):
-            put_tile(h, (1, edge), k, tile_of(ahead, (), k))
-            put_tile(h, (2, edge), k, tile_of(ahead, (), tiles + k))
-        psi_h[1, edge] = psi_edge[...]
-        e_plane(e, h, polar, current, psi_e, mats, edge, tiles, coef_e, last=True)
+        old_state, new_state = (e_in, p_in, c_in), (e, polar, current)
+        mats = (inv, dec, drv, spr)
+        all_planes(
+            old_state, new_state, h_in, h, psi_h, psi_e, mats, planes, tiles, coef_h, coef_e, ahead, arrive
+        )
 
     coef = pltpu.VMEM((planes, depth, width), F32)
     return pl.pallas_call(
         body,
         name="first_interior",
         out_shape=(*state_shapes(planes, depth, width), coef, coef, coef, coef),
-        in_specs=[HBM] * 7 + [SMEM] * 5 + [VMEM, VMEM],
+        in_specs=[VMEM] * 7 + [SMEM] * 5 + [VMEM, VMEM],
         out_specs=(VMEM,) * 10,
-        scratch_shapes=[
-            pltpu.VMEM((planes, depth, width), jnp.int32),
-            pltpu.SemaphoreType.DMA((7, planes)),
-        ],
         compiler_params=params(),
     )(*fields, *memories, material, *tables, ahead, psi_edge)
 
@@ -340,7 +366,8 @@
         e, h, polar, current, psi_h, psi_e = refs[10:16]
         coef_h = pml(layers, 0.5, width)
         coef_e = pml(layers, 0.0, width)
-        all_planes(e, h, polar, current, psi_h, psi_e, mats_in, planes, tiles, coef_h, coef_e)
+        now = (e, polar, current)
+        all_planes(now, now, h, h, psi_h, psi_e, mats_in, planes, tiles, coef_h, coef_e)
 
     return pl.pallas_call(
         body,
@@ -375,16 +402,22 @@
         put_tile(e, (2, edge), k, tile_of(e, (2, edge), k) + half * hy)
 
 
-def boundary(state, inv, from_ahead, from_behind, layers):
+def message_scratch(depth, width):
+    message = pltpu.VMEM((2 * depth, width), F32)
+    return [message, message]
+
+
+def boundary(state, inv, near, far, layers):
     e_now, h_now, polar, current, psi_h_now, psi_e_now = state
     planes, depth, width = e_now.shape[1:]
     tiles = depth // ROWS
     edge = planes - 1
 
-    def body(e_in, h_in, ph_in, pe_in, inv, from_ahead, from_behind, e, h, psi_h, psi_e, back, ahead):
+    def body(e_in, h_in, ph_in, pe_in, inv, near_in, far_in, e, h, psi_h, psi_e, near, far, back, ahead, behind):
         coef_h = pml(layers, 0.5, width)
         coef_e = pml(layers, 0.0, width)
-        close_edges(e, h, psi_e, inv, from_ahead, from_behind, edge, tiles, coef_e)
+        sort_in(near_in.at[0 : 2 * depth], far_in.at[0 : 2 * depth], ahead, behind)
+        close_edges(e, h, psi_e, inv, ahead, behind, edge, tiles, coef_e)
 
         def put_psi(value):
             psi_h[1, edge] = value
@@ -399,26 +432,28 @@
             put_tile(h, (2, edge), k, part_z)
             put_tile(ahead, (), k, part_y)
             put_tile(ahead, (), tiles + k, part_z)
+        sort_out(back, ahead, near, far)
 
     field, _, _, _, memory, _ = state_shapes(planes, depth, width)
     message = pltpu.VMEM((2 * depth, width), F32)
-    e, h, psi_h, psi_e, back, ahead = pl.pallas_call(
+    e, h, psi_h, psi_e, near, far, back = pl.pallas_call(
         body,
         name="boundary",
-        out_shape=(field, field, memory, memory, message, message),
+        out_shape=(field, field, memory, memory, message, message, message),
         in_specs=[VMEM] * 7,
-        out_specs=(VMEM,) * 6,
+        out_specs=(VMEM,) * 7,
         input_output_aliases={0: 0, 1: 1, 2: 2, 3: 3},
-        compiler_params=params(),
-    )(e_now, h_now, psi_h_now, psi_e_now, inv, from_ahead, from_behind)
-    return (e, h, polar, current, psi_h, psi_e), back, ahead
+        scratch_shapes=message_scratch(depth, width),
+        compiler_params=params(),
+    )(e_now, h_now, psi_h_now, psi_e_now, inv, near, far)
+    return (e, h, polar, current, psi_h, psi_e), near, far, back
 
 
 def spectral_rows(planes):
     return -(-(2 * planes + 3) // ROWS) * ROWS
 
 
-def last_interior(state, mats, back, inv_ahead, inv_behind, table, layers):
+def last_interior(state, mats, back, inv_near, inv_far, table, layers):
     planes, depth, width = state[0].shape[1:]
     tiles = depth // ROWS
     edge = planes - 1
@@ -428,13 +463,21 @@
 
     def body(*refs):
         mats_in = refs[6:10]
-        back, inv_ahead, inv_behind, table = refs[10:14]
+        back, inv_near, inv_far, table = refs[10:14]
         e, h, polar, current, psi_h, psi_e, mixed = refs[14:21]
         e_out, h_out, p_out, c_out, ph_out, pe_out = refs[21:27]
-        rows, sem = refs[27:]
+        rows, inv_ahead, inv_behind, ph_rows, pe_rows, sem = refs[27:]
+        sort_in(inv_near, inv_far, inv_ahead, inv_behind)
         coef_h = pml(layers, 0.5, width)
         coef_e = pml(layers, 0.0, width)
-        all_planes(e, h, polar, current, psi_h, psi_e, mats_in, planes, tiles, coef_h, coef_e)
+        now = (e, polar, current)
+        all_planes(now, now, h, h, psi_h, psi_e, mats_in, planes, tiles, coef_h, coef_e)
+        for i in range(planes):
+            for z in range(layers):
+                for c in range(2):
+                    ph_rows[i, z, c : c + 1, :] = psi_h[c, i, z : z + 1, :]
+                    if i < edge:
+                        pe_rows[i, z, c : c + 1, :] = psi_e[c, i, z : z + 1, :]
         wanted = [
             (polar, p_out),
             (current, c_out),
@@ -442,9 +485,8 @@
             (e.at[0, 0], e_out.at[0, 0]),
             (h.at[:, 0:edge], h_out.at[:, 0:edge]),
             (h.at[0, edge], h_out.at[0, edge]),
-            (psi_h.at[:, :, 0:layers], ph_out),
-            (psi_e.at[:, 0:edge, 0:layers], pe_out.at[:, 0:edge]),
-            (psi_e.at[1, edge, 0:layers], pe_out.at[1, edge]),
+            (ph_rows, ph_out),
+            (pe_rows, pe_out.at[0:edge]),
         ]
         copies = [pltpu.make_async_copy(s, d, sem.at[n]) for n, (s, d) in enumerate(wanted)]
         start_all(copies)
@@ -470,7 +512,7 @@
         wait_all(copies)
 
     field = jax.ShapeDtypeStruct((3, planes, depth, width), F32)
-    memory = jax.ShapeDtypeStruct((2, planes, layers, width), F32)
+    memory = jax.ShapeDtypeStruct((planes, layers, 2, width), F32)
     found = pl.pallas_call(
         body,
         name="last_interior",
@@ -484,26 +526,38 @@
         in_specs=[VMEM] * 14,
         out_specs=(*((VMEM,) * 7), *((HBM,) * 6)),
         input_output_aliases={n: n for n in range(6)},
-        scratch_shapes=[pltpu.VMEM((count, width), F32), pltpu.SemaphoreType.DMA((9,))],
-        compiler_params=params(),
-    )(*state, *mats, back, inv_ahead, inv_behind, table)
+        scratch_shapes=[
+            pltpu.VMEM((count, width), F32),
+            pltpu.VMEM((ROWS, width), F32),
+            pltpu.VMEM((ROWS, width), F32),
+            pltpu.VMEM((planes, layers, 2, width), F32),
+            pltpu.VMEM((edge, layers, 2, width), F32),
+            pltpu.SemaphoreType.DMA((9,)),
+        ],
+        compiler_params=params(),
+    )(*state, *mats, back, inv_near, inv_far, table)
     return found[:6], found[6], found[7:]
 
 
-def last_boundary(state, inv, from_ahead, from_behind, outs, layers):
+def last_boundary(state, inv, near, far, outs, layers):
     e_now, h_now, _, _, _, psi_e_now = state
     planes, depth, width = e_now.shape[1:]
     tiles = depth // ROWS
     edge = planes - 1
 
-    def body(e_in, h_in, pe_in, inv, from_ahead, from_behind, e_hbm, h_hbm, pe_hbm, e, h, psi_e, e_out, h_out, pe_out, sem):
+    def body(e_in, h_in, pe_in, inv, near, far, e_hbm, h_hbm, pe_hbm, *refs):
+        e, h, psi_e, e_out, h_out, pe_out, ahead, behind, rows, sem = refs
         coef_e = pml(layers, 0.0, width)
-        close_edges(e, h, psi_e, inv, from_ahead, from_behind, edge, tiles, coef_e)
+        sort_in(near, far, ahead, behind)
+        close_edges(e, h, psi_e, inv, ahead, behind, edge, tiles, coef_e)
+        for z in range(layers):
+            for c in range(2):
+                rows[z, c : c + 1, :] = psi_e[c, edge, z : z + 1, :]
         wanted = [
             (e.at[1:3, 0], e_out.at[1:3, 0]),
             (e.at[:, edge], e_out.at[:, edge]),
             (h.at[1:3, edge], h_out.at[1:3, edge]),
-            (psi_e.at[0, edge, 0:layers], pe_out.at[0, edge]),
+            (rows, pe_out.at[edge]),
         ]
         copies = [pltpu.make_async_copy(s, d, sem.at[n]) for n, (s, d) in enumerate(wanted)]
         start_all(copies)
@@ -519,9 +573,13 @@
         in_specs=[VMEM] * 6 + [HBM] * 3,
         out_specs=(VMEM, VMEM, VMEM, HBM, HBM, HBM),
         input_output_aliases={0: 0, 1: 1, 2: 2, 6: 3, 7: 4, 8: 5},
-        scratch_shapes=[pltpu.SemaphoreType.DMA((4,))],
-        compiler_params=params(),
-    )(e_now, h_now, psi_e_now, inv, from_ahead, from_behind, e_out, h_out, pe_out)
+        scratch_shapes=[
+            *message_scratch(depth, width),
+            pltpu.VMEM((layers, 2, width), F32),
+            pltpu.SemaphoreType.DMA((4,)),
+        ],
+        compiler_params=params(),
+    )(e_now, h_now, psi_e_now, inv, near, far, *(in_hbm(x) for x in (e_out, h_out, pe_out)))
     return (found[3], found[4], p_out, c_out, ph_out, found[5])
 
 
@@ -550,6 +608,23 @@
     return np.concatenate(parts, axis=0).astype(np.float32)
 
 
+def packed(pieces):
+    rows, width = pieces[0].shape
+
+    def body(*refs):
+        for n in range(len(pieces)):
+            refs[-1][n * rows : n * rows + rows, :] = refs[n][...]
+
+    return pl.pallas_call(
+        body,
+        name="packed",
+        out_shape=pltpu.VMEM((rows * len(pieces), width), F32),
+        in_specs=[VMEM] * len(pieces),
+        out_specs=VMEM,
+        compiler_params=params(),
+    )(*pieces)
+
+
 def gathered(block):
     count = lax.axis_size("gx")
     assert count & (count - 1) == 0
@@ -557,29 +632,61 @@
     reach = 1
     while reach < count:
         ways = min(4, count // reach)
-        held = pieces[0] if len(pieces) == 1 else jnp.concatenate(pieces, axis=0)
+        held = pieces[0] if len(pieces) == 1 else packed(pieces)
         pieces = [held] + [swapped(held, reach * way) for way in range(1, ways)]
         reach *= ways
     return pieces
 
 
-def pick_orders(pieces, table, orders, cells_total):
-    rows = spectral_rows_of = None
+def prepared(orders, table_y, table_x):
+    wide = orders.shape[1]
+    chunk = 512 if wide % 512 == 0 else wide
+
+    def body(orders_in, y_in, x_in, hit_y, hit_x, table_y, table_x, orders, sem):
+        wanted = [(orders_in, orders), (y_in, table_y), (x_in, table_x)]
+        copies = [pltpu.make_async_copy(s, d, sem.at[n]) for n, (s, d) in enumerate(wanted)]
+        start_all(copies)
+        wait_all(copies)
+        for n in range(wide // chunk):
+            span = slice(n * chunk, n * chunk + chunk)
+            waves = lax.broadcasted_iota(jnp.int32, (KSPAN, chunk), 0) - KSPAN // 2
+            hit = jnp.where(waves == orders[1:2, span], 1.0, 0.0).astype(jnp.bfloat16)
+            for part in range(3):
+                hit_y[part * KSPAN : (part + 1) * KSPAN, span] = hit
+            hit_x[:, span] = jnp.where(waves == orders[0:1, span], 1.0, 0.0)
+
+    return pl.pallas_call(
+        body,
+        name="prepared",
+        out_shape=(
+            pltpu.VMEM((3 * KSPAN, wide), jnp.bfloat16),
+            pltpu.VMEM((KSPAN, wide), F32),
+            pltpu.VMEM(table_y.shape, F32),
+            pltpu.VMEM(table_x.shape, F32),
+        ),
+        in_specs=[HBM] * 3,
+        out_specs=(VMEM,) * 4,
+        scratch_shapes=[pltpu.VMEM(orders.shape, jnp.int32), pltpu.SemaphoreType.DMA((3,))],
+        compiler_params=params(),
+    )(in_hbm(orders), in_hbm(table_y), in_hbm(table_x))
+
+
+def pick_orders(pieces, table, hit_y, hit_x, cells_total):
     count = lax.axis_size("gx")
     total = sum(piece.shape[0] for piece in pieces)
     rows = total // count
-    wide = orders.shape[1]
+    wide = hit_x.shape[1]
     chunk = 512 if wide % 512 == 0 else wide
     scale = 1.0 / math.sqrt(cells_total)
-    here = jnp.reshape(lax.axis_index("gx"), (1,)).astype(jnp.int32)
-
-    def body(here, *refs):
+
+    def body(*refs):
         held = refs[: len(pieces)]
-        table, orders, out, mixed = refs[len(pieces) :]
+        table, hit_y, hit_x, out, mixed = refs[len(pieces) :]
+        here = lax.axis_index("gx")
         at = 0
         for ref in held:
             for n in range(ref.shape[0] // rows):
-                slot = jnp.bitwise_xor(here[0], at)
+                slot = jnp.bitwise_xor(here, at)
                 mixed[pl.ds(pl.multiple_of(slot * rows, rows), rows), :] = ref[n * rows : n * rows + rows, :]
                 at += 1
         both = jnp.dot(table[...], mixed[...], precision=lax.Precision.HIGHEST, preferred_element_type=F32)
@@ -597,26 +704,21 @@
         split = jnp.concatenate([high, mid, low], axis=1)
         for n in range(wide // chunk):
             span = slice(n * chunk, n * chunk + chunk)
-            index_x = orders[0:1, span] + KSPAN // 2
-            index_y = orders[1:2, span] + KSPAN // 2
-            waves = lax.broadcasted_iota(jnp.int32, (KSPAN, chunk), 0)
-            hit_y = (waves == index_y).astype(F32).astype(jnp.bfloat16)
-            hit_x = waves == index_x
-            hits = jnp.concatenate([hit_y] * 3, axis=0)
-            lines = jnp.dot(split, hits, preferred_element_type=F32)
+            lines = jnp.dot(split, hit_y[:, span], preferred_element_type=F32)
+            hit = hit_x[:, span]
             for q in range(4):
-                line = jnp.where(hit_x, lines[q * KSPAN : (q + 1) * KSPAN], 0.0)
+                line = lines[q * KSPAN : (q + 1) * KSPAN] * hit
                 out[q : q + 1, span] = jnp.sum(line, axis=0, keepdims=True)
 
     return pl.pallas_call(
         body,
         name="pick_orders",
         out_shape=jax.ShapeDtypeStruct((4, wide), F32),
-        in_specs=[SMEM] + [VMEM] * (len(pieces) + 2),
+        in_specs=[VMEM] * (len(pieces) + 3),
         out_specs=VMEM,
         scratch_shapes=[pltpu.VMEM((total, 2 * KSPAN), F32)],
         compiler_params=params(),
-    )(here, *pieces, table, orders)
+    )(*pieces, table, hit_y, hit_x)
 
 
 def shards(
@@ -638,24 +740,25 @@
     layers = psi_h.shape[2]
     count = lax.axis_size("gx")
     tables = (inv_eps_table, decay_table, drive_table, strength_table, spring_table)
-
-    back, ahead, psi_edge = first_message(e_field, h_field, psi_h, material, inv_eps_table)
-    from_ahead, from_behind = passed_along(back, -1), passed_along(ahead, 1)
+    psi_h, psi_e = (jnp.transpose(psi, (1, 2, 0, 3)) for psi in (psi_h, psi_e))
+
+    near, far, ahead, psi_edge = first_message(e_field, h_field, psi_h, material, inv_eps_table)
+    near, far = exchanged(near, far)
     found = first_interior((e_field, h_field, polar, current), (psi_h, psi_e), material, tables, ahead, psi_edge)
     state, mats = found[:6], found[6:]
-    inv_ahead = from_ahead[2 * depth :]
-    inv_behind = from_behind[2 * depth :]
+    inv_near, inv_far = near[2 * depth :], far[2 * depth :]
+    hit_y, hit_x, table_y, table_x = prepared(orders, jnp.asarray(y_table(width)), jnp.asarray(x_table(planes, count)))
     for step in range(1, STEPS):
-        state, back, ahead = boundary(state, mats[0], from_ahead, from_behind, layers)
-        from_ahead, from_behind = passed_along(back, -1), passed_along(ahead, 1)
+        state, near, far, back = boundary(state, mats[0], near, far, layers)
+        near, far = exchanged(near, far)
         if step < STEPS - 1:
             state = interior(state, mats, layers)
-    state, mixed, outs = last_interior(
-        state, mats, back, inv_ahead, inv_behind, jnp.asarray(y_table(width)), layers
-    )
+        else:
+            state, mixed, outs = last_interior(state, mats, back, inv_near, inv_far, table_y, layers)
     pieces = gathered(mixed)
-    outs = last_boundary(state, mats[0], from_ahead, from_behind, outs, layers)
-    pupil = pick_orders(pieces, jnp.asarray(x_table(planes, count)), orders, planes * count * width)
+    outs = last_boundary(state, mats[0], near, far, outs, layers)
+    pupil = pick_orders(pieces, table_x, hit_y, hit_x, planes * count * width)
+    outs = (*outs[:4], *(jnp.transpose(psi, (2, 0, 1, 3)) for psi in outs[4:]))
     return (*outs, pupil)
 
 

time: 64.5 us -> 55.1 us (0.85)
  local copies, waits for them, and re-layouts: 14.7 us -> 4.26 us
  Pallas kernels: 21.7 us -> 18.5 us
  starting transfers between devices: 13.9 us -> 17 us
  waiting for transfers between devices: 12.7 us -> 14.3 us
    unnamed x43 -> x24, local copies, waits for them, and re-layouts: 14.1 us -> 4.25 us
    pallas_call x1, Pallas kernels: 6.42 us -> 2.39 us  [first_interior(): pl.pallas_call(body, name='first_interior', out_shape=(*state_shapes(plan...]
    ppermute x6, waiting for transfers between devices: 1.81 us -> 5.8 us  [swapped(): lax.ppermute(value, 'gx', [(source, source ^ mask) for source in range(co...]
    ppermute x8, starting transfers between devices: 7.67 us -> 10.7 us  [the longest x4 10 us: exchanged(): far = lax.ppermute(far, 'gx', pairs)]
    ppermute x8, waiting for transfers between devices: 10.9 us -> 8.46 us  [the longest x4 8.45 us: exchanged(): far = lax.ppermute(far, 'gx', pairs)]
    pallas_call x1 -> x3, Pallas kernels: 1.18 us -> 3.42 us  [the longest x1 2.11 us: first_message(): pl.pallas_call(body, name='first_message', out_shape=(message, message, m...]
    pallas_call x3, Pallas kernels: 1.23 us -> 2.09 us  [boundary(): pl.pallas_call(body, name='boundary', out_shape=(field, field, memory, me...]
    pallas_call x1, Pallas kernels: 3.17 us -> 2.31 us  [pick_orders(): pl.pallas_call(body, name='pick_orders', out_shape=jax.ShapeDtypeStruct((...]
  transfers between devices with their start and end apart: 14 -> 14, of which waited for: 6 -> 6; matrix products, arithmetic and copies ran while one was open for 7% -> 0% of each run, Pallas kernels for 20% -> 24%
where the time goes in v2:
time: 55.1 us; the launch traced here: 54.9 us
  Pallas kernels  18.5 us (34%)
  starting transfers between devices  17 us (31%)
  waiting for transfers between devices  14.3 us (26%)
  local copies, waits for them, and re-layouts  4.26 us (8%)
  between operations  0.85 us (2%)
    ppermute x4, starting transfers between devices, exchanged(): far = lax.ppermute(far, 'gx', pairs)  10 us
    ppermute x4, waiting for transfers between devices, exchanged(): far = lax.ppermute(far, 'gx', pairs)  8.45 us
    ppermute x6, starting transfers between devices, swapped(): lax.ppermute(value, 'gx', [(source, source ^ mask) for source in range(co...  6.31 us
    ppermute x6, waiting for transfers between devices, swapped(): lax.ppermute(value, 'gx', [(source, source ^ mask) for source in range(co...  5.8 us
    unnamed x24, local copies, waits for them, and re-layouts  4.25 us
    pallas_call x1, Pallas kernels, last_interior(): pl.pallas_call(body, name='last_interior', out_shape=(*state_shapes(plane...  4.18 us
    pallas_call x2, Pallas kernels, interior(): pl.pallas_call(body, name='interior', out_shape=state_shapes(planes, dept...  3.17 us
    pallas_call x1, Pallas kernels, first_interior(): pl.pallas_call(body, name='first_interior', out_shape=(*state_shapes(plan...  2.39 us
  transfers between devices with their start and end apart: 14, of which 6 were waited for; matrix products, arithmetic and copies ran while one was open for 0% of the time, Pallas kernels for 24%

profile of v2, /device:TPU:0, one launch (start us, length us, event | category | flops | bytes accessed | tf_op | source)
XLA Modules:
  0.0 54.9 jit_solution(3142104519307181349)
XLA Ops:
  0.6 0.0 copy-start.7
  0.6 0.6 %copy-done.7 = f32[4]{0:T(128)S(1)} copy-done((f32[4]{0:T(128)S(1)}, f32[4]{0:T(128)}, u32[]{:S(2)}) %copy-start.7) | copy-done | bytes 40
  1.3 2.1 %first_message.1 = (f32[56,768]{1,0:T(8,128)S(1)}, f32[56,768]{1,0:T(8,128)S(1)}, f32[56,768]{1,0:T(8,128)S(1)}, f32[8,768]{1,0:T(8,128)S(1)}) custom-call(f32[3,6,24,768]{3,2,1,0:T(8,128)} %e_in.3, f32[3,6,24,768]{3,2,1,0:T(8,128)} %h_in.3, f32[6,6,2,768]{3,2,1,0:T(2,128)} %bitcast.4, s32[6,24,768]{2,1,0:T(8,128)} %mat.1, f32[4]{0:T(128)S(1)} %copy-done.7), custom_call_target="tpu_custom_call" | custom-call | tf_op jit(solution)/shard_map/first_message/pallas_call | solution.py:261
  3.5 0.6 %collective-permute-start = (f32[56,768]{1,0:T(8,128)S(1)}, f32[56,768]{1,0:T(8,128)S(1)}, u32[]{:S(2)}, u32[]{:S(2)}) collective-permute-start(f32[56,768]{1,0:T(8,128)S(1)} %get-tuple-element.76), channel_id=1, source_target_pairs={{1,0},{3,2},{5,4},{7,6},{9,8},{11,10},{13,12},{15,14},{0,1},{2,3},... | collective-permute-start | bytes 516104 | tf_op jit(solution)/shard_map/ppermute | solution.py:43
  4.0 5.7 %collective-permute-start.1 = (f32[56,768]{1,0:T(8,128)S(1)}, f32[56,768]{1,0:T(8,128)S(1)}, u32[]{:S(2)}, u32[]{:S(2)}) collective-permute-start(f32[56,768]{1,0:T(8,128)S(1)} %get-tuple-element.77), channel_id=1, source_target_pairs={{1,2},{3,4},{5,6},{7,8},{9,10},{11,12},{13,14},{15,0},{2,1},{4,3},... | collective-permute-start | bytes 516104 | tf_op jit(solution)/shard_map/ppermute | solution.py:41
  9.7 0.0 copy-done
  9.7 0.0 copy-done.8
  9.7 0.0 copy-done.9
  9.7 0.0 copy-start.3
  9.7 1.3 %copy-done.3 = f32[3,6,24,768]{3,2,1,0:T(8,128)S(1)} copy-done((f32[3,6,24,768]{3,2,1,0:T(8,128)S(1)}, f32[3,6,24,768]{3,2,1,0:T(8,128)}, u32[]{:S(2)}) %copy-start.3) | copy-done | bytes 1327128
  11.1 1.3 %copy-done.4 = f32[3,6,24,768]{3,2,1,0:T(8,128)S(1)} copy-done((f32[3,6,24,768]{3,2,1,0:T(8,128)S(1)}, f32[3,6,24,768]{3,2,1,0:T(8,128)}, u32[]{:S(2)}) %copy-start.4) | copy-done | bytes 1327128
  12.4 0.9 %copy-done.6 = f32[2,6,6,768]{3,0,2,1:T(2,128)S(1)} copy-done((f32[2,6,6,768]{3,0,2,1:T(2,128)S(1)}, f32[2,6,6,768]{3,0,2,1:T(2,128)}, u32[]{:S(2)}) %copy-start.6) | copy-done | bytes 221208
  13.3 2.4 %first_interior.1 = (f32[3,6,24,768]{3,2,1,0:T(8,128)S(1)}, f32[3,6,24,768]{3,2,1,0:T(8,128)S(1)}, f32[3,6,24,768]{3,2,1,0:T(8,128)S(1)}, f32[3,6,24,768]{3,2,1,...) custom-call(f32[3,6,24,768]{3,2,1,0:T(8,128)S(1)} %copy-done, ...), custom_call_target="tpu_custom_call" | custom-call | tf_op jit(solution)/shard_map/first_interior/pallas_call | solution.py:350
  15.7 0.0 collective-permute-done.near_in
  15.7 0.0 collective-permute-done.1.far_in
  15.7 0.9 %boundary.3 = (f32[3,6,24,768]{3,2,1,0:T(8,128)S(1)}, f32[3,6,24,768]{3,2,1,0:T(8,128)S(1)}, f32[2,6,8,768]{3,2,1,0:T(8,128)S(1)}, f32[2,6,8,768]{3,2,1,0:T(8,12...) custom-call(f32[3,6,24,768]{3,2,1,0:T(8,128)S(1)} %get-tuple-element, ...), custom_call_target="tpu_custom_call", output_to_operand_aliasing={{0}: (0, {}), {1}: (1, {}), {2}: (2, {}), {3}: (3, {})} | custom-call | tf_op jit(solution)/shard_map/boundary/pallas_call | solution.py:439
  16.7 0.0 collective-permute-start.2
  16.7 1.5 %collective-permute-start.3 = (f32[48,768]{1,0:T(8,128)S(1)}, f32[48,768]{1,0:T(8,128)S(1)}, u32[]{:S(2)}, u32[]{:S(2)}) collective-permute-start(f32[48,768]{1,0:T(8,128)S(1)} %get-tuple-element.92), channel_id=1, source_target_pairs={{1,2},{3,4},{5,6},{7,8},{9,10},{11,12},{13,14},{15,0},{2,1},{4,3},... | collective-permute-start | bytes 442376 | tf_op jit(solution)/shard_map/ppermute | solution.py:41
  18.1 1.6 %interior.2 = (f32[3,6,24,768]{3,2,1,0:T(8,128)S(1)}, f32[3,6,24,768]{3,2,1,0:T(8,128)S(1)}, f32[3,6,24,768]{3,2,1,0:T(8,128)S(1)}, f32[3,6,24,768]{3,2,1,0:T(8,...) custom-call(f32[3,6,24,768]{3,2,1,0:T(8,128)S(1)} %get-tuple-element, ...), custom_call_target="tpu_custom_call", output_to_operand_aliasing={{0}: (0, {}), {1}: (1, {}), {2}: (2, {}), {3}: (3, {}), {4}... | custom-call | tf_op jit(solution)/shard_map/interior/pallas_call | solution.py:372
  19.7 0.0 collective-permute-done.2.near_in
  19.7 4.2 %collective-permute-done.3.far_in = f32[48,768]{1,0:T(8,128)S(1)} collective-permute-done((f32[48,768]{1,0:T(8,128)S(1)}, f32[48,768]{1,0:T(8,128)S(1)}, u32[]{:S(2)}, u32[]{:S(2)}) %collective-permute-start.3) | collective-permute-done | bytes 147488 | tf_op jit(solution)/shard_map/ppermute | solution.py:41
  23.9 0.9 %boundary.4 = (f32[3,6,24,768]{3,2,1,0:T(8,128)S(1)}, f32[3,6,24,768]{3,2,1,0:T(8,128)S(1)}, f32[2,6,8,768]{3,2,1,0:T(8,128)S(1)}, f32[2,6,8,768]{3,2,1,0:T(8,12...) custom-call(f32[3,6,24,768]{3,2,1,0:T(8,128)S(1)} %get-tuple-element, ...), custom_call_target="tpu_custom_call", output_to_operand_aliasing={{0}: (0, {}), {1}: (1, {}), {2}: (2, {}), {3}: (3, {})} | custom-call | tf_op jit(solution)/shard_map/boundary/pallas_call | solution.py:439
  24.8 0.0 collective-permute-start.4
  24.8 1.4 %collective-permute-start.5 = (f32[48,768]{1,0:T(8,128)S(1)}, f32[48,768]{1,0:T(8,128)S(1)}, u32[]{:S(2)}, u32[]{:S(2)}) collective-permute-start(f32[48,768]{1,0:T(8,128)S(1)} %get-tuple-element.104), channel_id=1, source_target_pairs={{1,2},{3,4},{5,6},{7,8},{9,10},{11,12},{13,14},{15,0},{2,1},{4,3},... | collective-permute-start | bytes 442376 | tf_op jit(solution)/shard_map/ppermute | solution.py:41
  26.3 1.6 %interior.3 = (f32[3,6,24,768]{3,2,1,0:T(8,128)S(1)}, f32[3,6,24,768]{3,2,1,0:T(8,128)S(1)}, f32[3,6,24,768]{3,2,1,0:T(8,128)S(1)}, f32[3,6,24,768]{3,2,1,0:T(8,...) custom-call(f32[3,6,24,768]{3,2,1,0:T(8,128)S(1)} %get-tuple-element, ...), custom_call_target="tpu_custom_call", output_to_operand_aliasing={{0}: (0, {}), {1}: (1, {}), {2}: (2, {}), {3}: (3, {}), {4}... | custom-call | tf_op jit(solution)/shard_map/interior/pallas_call | solution.py:372
  27.9 0.0 collective-permute-done.4.near_in
  27.9 4.2 %collective-permute-done.5.far_in = f32[48,768]{1,0:T(8,128)S(1)} collective-permute-done((f32[48,768]{1,0:T(8,128)S(1)}, f32[48,768]{1,0:T(8,128)S(1)}, u32[]{:S(2)}, u32[]{:S(2)}) %collective-permute-start.5) | collective-permute-done | bytes 147488 | tf_op jit(solution)/shard_map/ppermute | solution.py:41
  32.1 0.3 boundary.5
  32.4 0.1 collective-permute-start.6
  32.5 1.5 %collective-permute-start.7 = (f32[48,768]{1,0:T(8,128)S(1)}, f32[48,768]{1,0:T(8,128)S(1)}, u32[]{:S(2)}, u32[]{:S(2)}) collective-permute-start(f32[48,768]{1,0:T(8,128)S(1)} %get-tuple-element.117), channel_id=1, source_target_pairs={{1,2},{3,4},{5,6},{7,8},{9,10},{11,12},{13,14},{15,0},{2,1},{4,3},... | collective-permute-start | bytes 442376 | tf_op jit(solution)/shard_map/ppermute | solution.py:41
  33.9 1.3 %prepared.1 = (bf16[192,4096]{1,0:T(8,128)(2,1)S(1)}, f32[64,4096]{1,0:T(8,128)S(1)}, f32[768,128]{1,0:T(8,128)S(1)}, f32[256,256]{1,0:T(8,128)S(1)}) custom-call(s32[2,4096]{1,0:T(2,128)} %orders_in.1, f32[768,128]{1,0:T(8,128)} %constant.4.clone.y_in, f32[256,256]{1,0:T(8,128)} %constant.5.clone.x_in), custom_call_target="tpu_custom_call" | custom-call | tf_op jit(solution)/shard_map/prepared/pallas_call | solution.py:658
  35.3 4.2 %last_interior.1 = (f32[3,6,24,768]{3,2,1,0:T(8,128)S(1)}, f32[3,6,24,768]{3,2,1,0:T(8,128)S(1)}, f32[3,6,24,768]{3,2,1,0:T(8,128)S(1)}, f32[3,6,24,768]{3,2,1,0...) custom-call(f32[3,6,24,768]{3,2,1,0:T(8,128)S(1)} %get-tuple-element, ...), custom_call_target="tpu_custom_call", output_to_operand_aliasing={{0}: (0, {}), {1}: (1, {}), {2}: (2, {}), {3}: (3, {}), {4}... | custom-call | tf_op jit(solution)/shard_map/last_interior/pallas_call | solution.py:516
  39.5 0.1 collective-permute-start.10
  39.5 0.7 %collective-permute-start.9 = (f32[16,128]{1,0:T(8,128)S(1)}, f32[16,128]{1,0:T(8,128)S(1)}, u32[]{:S(2)}, u32[]{:S(2)}) collective-permute-start(f32[16,128]{1,0:T(8,128)S(1)} %get-tuple-element.127.refs_0_), channel_id=1, source_target_pairs={{0,2},{1,3},{2,0},{3,1},{4,6},{5,7},{6,4},{7,5},{8,10},{9,11},{10,... | collective-permute-start | bytes 24584 | tf_op jit(solution)/shard_map/ppermute | solution.py:77
  40.2 1.1 %collective-permute-start.8 = (f32[16,128]{1,0:T(8,128)S(1)}, f32[16,128]{1,0:T(8,128)S(1)}, u32[]{:S(2)}, u32[]{:S(2)}) collective-permute-start(f32[16,128]{1,0:T(8,128)S(1)} %get-tuple-element.127.refs_0_), channel_id=1, source_target_pairs={{0,1},{1,0},{2,3},{3,2},{4,5},{5,4},{6,7},{7,6},{8,9},{9,8},{10,11... | collective-permute-start | bytes 24584 | tf_op jit(solution)/shard_map/ppermute | solution.py:77
  41.4 1.2 %collective-permute-done.10.refs_3_ = f32[16,128]{1,0:T(8,128)S(1)} collective-permute-done((f32[16,128]{1,0:T(8,128)S(1)}, f32[16,128]{1,0:T(8,128)S(1)}, u32[]{:S(2)}, u32[]{:S(2)}) %collective-permute-start.10) | collective-permute-done | bytes 8224 | tf_op jit(solution)/shard_map/ppermute | solution.py:77
  42.6 0.7 %collective-permute-done.9.refs_2_ = f32[16,128]{1,0:T(8,128)S(1)} collective-permute-done((f32[16,128]{1,0:T(8,128)S(1)}, f32[16,128]{1,0:T(8,128)S(1)}, u32[]{:S(2)}, u32[]{:S(2)}) %collective-permute-start.9) | collective-permute-done | bytes 8224 | tf_op jit(solution)/shard_map/ppermute | solution.py:77
  43.3 0.0 collective-permute-done.8.refs_1_
  43.3 3.5 %collective-permute-start.13 = (f32[64,128]{1,0:T(8,128)S(1)}, f32[64,128]{1,0:T(8,128)S(1)}, u32[]{:S(2)}, u32[]{:S(2)}) collective-permute-start(f32[64,128]{1,0:T(8,128)S(1)} %packed.1.refs_0_), channel_id=1, source_target_pairs={{0,12},{1,13},{2,14},{3,15},{4,8},{5,9},{6,10},{7,11},{8,4},{9,5},... | collective-permute-start | bytes 98312 | tf_op jit(solution)/shard_map/ppermute | solution.py:77
  46.8 0.0 collective-permute-start.12
  46.8 0.9 %collective-permute-start.11 = (f32[64,128]{1,0:T(8,128)S(1)}, f32[64,128]{1,0:T(8,128)S(1)}, u32[]{:S(2)}, u32[]{:S(2)}) collective-permute-start(f32[64,128]{1,0:T(8,128)S(1)} %packed.1.refs_0_), channel_id=1, source_target_pairs={{0,4},{1,5},{2,6},{3,7},{4,0},{5,1},{6,2},{7,3},{8,12},{9,13},{10,... | collective-permute-start | bytes 98312 | tf_op jit(solution)/shard_map/ppermute | solution.py:77
  47.7 1.3 %collective-permute-done.13.refs_3_ = f32[64,128]{1,0:T(8,128)S(1)} collective-permute-done((f32[64,128]{1,0:T(8,128)S(1)}, f32[64,128]{1,0:T(8,128)S(1)}, u32[]{:S(2)}, u32[]{:S(2)}) %collective-permute-start.13) | collective-permute-done | bytes 32800 | tf_op jit(solution)/shard_map/ppermute | solution.py:77
  49.0 2.6 %collective-permute-done.12.refs_2_ = f32[64,128]{1,0:T(8,128)S(1)} collective-permute-done((f32[64,128]{1,0:T(8,128)S(1)}, f32[64,128]{1,0:T(8,128)S(1)}, u32[]{:S(2)}, u32[]{:S(2)}) %collective-permute-start.12) | collective-permute-done | bytes 32800 | tf_op jit(solution)/shard_map/ppermute | solution.py:77
  51.6 0.0 collective-permute-done.11.refs_1_
  51.6 2.3 %pick_orders.1 = f32[4,4096]{1,0:T(4,128)} custom-call(f32[64,128]{1,0:T(8,128)S(1)} %packed.1.refs_0_, f32[64,128]{1,0:T(8,128)S(1)} %collective-permute-done.11.refs_1_, f32[64,128]{1,0:T(8,128)S(1)} %collective-permute-done.12.refs_2_, f32[64,128]{1,0:T(8,128)S(1)} %collective-permute-done.13.refs_3_, f32[256,256]{1,0:T(8,128)S(1)} %get-tuple-element.128.refs_4_, ...), custom_call_target="tpu_custom_call" | custom-call | tf_op jit(solution)/shard_map/pick_orders/pallas_call | solution.py:713
  53.9 0.0 collective-permute-done.6.near
  53.9 0.0 collective-permute-done.7.far
  53.9 1.0 %last_boundary.1 = (f32[3,6,24,768]{3,2,1,0:T(8,128)S(1)}, f32[3,6,24,768]{3,2,1,0:T(8,128)S(1)}, f32[2,6,8,768]{3,2,1,0:T(8,128)S(1)}, f32[3,6,24,768]{3,2,1,0:...) custom-call(f32[3,6,24,768]{3,2,1,0:T(8,128)S(1)} %get-tuple-element, ...), custom_call_target="tpu_custom_call", output_to_operand_aliasing={{0}: (0, {}), {1}: (1, {}), {2}: (2, {}), {3}: (6, {}), {4}... | custom-call | tf_op jit(solution)/shard_map/last_boundary/pallas_call | solution.py:569
  (18 shorter events, 0.0 us)
Async XLA Ops:
  0.6 0.7 %copy-start.7 = (f32[4]{0:T(128)S(1)}, f32[4]{0:T(128)}, u32[]{:S(2)}) copy-start(f32[4]{0:T(128)} %t0.1) | copy-start | bytes 52
  1.3 8.4 %copy-start = (f32[3,6,24,768]{3,2,1,0:T(8,128)S(1)}, f32[3,6,24,768]{3,2,1,0:T(8,128)}, u32[]{:S(2)}) copy-start(f32[3,6,24,768]{3,2,1,0:T(8,128)} %e_in.3) | copy-start | bytes 3981316
  1.3 8.4 %copy-start.1 = (f32[3,6,24,768]{3,2,1,0:T(8,128)S(1)}, f32[3,6,24,768]{3,2,1,0:T(8,128)}, u32[]{:S(2)}) copy-start(f32[3,6,24,768]{3,2,1,0:T(8,128)} %h_in.3) | copy-start | bytes 3981316
  1.3 8.4 %copy-start.2 = (s32[6,24,768]{2,1,0:T(8,128)S(1)}, s32[6,24,768]{2,1,0:T(8,128)}, u32[]{:S(2)}) copy-start(s32[6,24,768]{2,1,0:T(8,128)} %mat.1) | copy-start | bytes 1327108
  1.3 8.4 %copy-start.5 = (f32[2,6,6,768]{3,0,2,1:T(2,128)S(1)}, f32[2,6,6,768]{3,0,2,1:T(2,128)}, u32[]{:S(2)}) copy-start(f32[2,6,6,768]{3,0,2,1:T(2,128)} %param.19) | copy-start | bytes 663556
  1.3 8.4 %copy-start.8 = (f32[4]{0:T(128)S(1)}, f32[4]{0:T(128)}, u32[]{:S(2)}) copy-start(f32[4]{0:T(128)} %t1.1) | copy-start | bytes 52
  1.3 8.4 %copy-start.9 = (f32[4]{0:T(128)S(1)}, f32[4]{0:T(128)}, u32[]{:S(2)}) copy-start(f32[4]{0:T(128)} %t2.1) | copy-start | bytes 52
  1.3 8.4 %copy-start.10 = (f32[4]{0:T(128)S(1)}, f32[4]{0:T(128)}, u32[]{:S(2)}) copy-start(f32[4]{0:T(128)} %t3.1) | copy-start | bytes 52
  1.3 8.4 %copy-start.11 = (f32[4]{0:T(128)S(1)}, f32[4]{0:T(128)}, u32[]{:S(2)}) copy-start(f32[4]{0:T(128)} %t4.1) | copy-start | bytes 52
  3.5 12.3 %collective-permute-start = (f32[56,768]{1,0:T(8,128)S(1)}, f32[56,768]{1,0:T(8,128)S(1)}, u32[]{:S(2)}, u32[]{:S(2)}) collective-permute-start(f32[56,768]{1,0:T(8,128)S(1)} %get-tuple-element.76), channel_id=1, source_target_pairs={{1,0},{3,2},{5,4},{7,6},{9,8},{11,10},{13,12},{15,14},{0,1},{2,3},... | collective-permute-start | bytes 516104 | tf_op jit(solution)/shard_map/ppermute | solution.py:43
  4.0 11.7 %collective-permute-start.1 = (f32[56,768]{1,0:T(8,128)S(1)}, f32[56,768]{1,0:T(8,128)S(1)}, u32[]{:S(2)}, u32[]{:S(2)}) collective-permute-start(f32[56,768]{1,0:T(8,128)S(1)} %get-tuple-element.77), channel_id=1, source_target_pairs={{1,2},{3,4},{5,6},{7,8},{9,10},{11,12},{13,14},{15,0},{2,1},{4,3},... | collective-permute-start | bytes 516104 | tf_op jit(solution)/shard_map/ppermute | solution.py:41
  9.7 1.3 %copy-start.3 = (f32[3,6,24,768]{3,2,1,0:T(8,128)S(1)}, f32[3,6,24,768]{3,2,1,0:T(8,128)}, u32[]{:S(2)}) copy-start(f32[3,6,24,768]{3,2,1,0:T(8,128)} %p_in.1) | copy-start | bytes 3981316
  11.1 1.3 %copy-start.4 = (f32[3,6,24,768]{3,2,1,0:T(8,128)S(1)}, f32[3,6,24,768]{3,2,1,0:T(8,128)}, u32[]{:S(2)}) copy-start(f32[3,6,24,768]{3,2,1,0:T(8,128)} %c_in.1) | copy-start | bytes 3981316
  12.4 0.9 %copy-start.6 = (f32[2,6,6,768]{3,0,2,1:T(2,128)S(1)}, f32[2,6,6,768]{3,0,2,1:T(2,128)}, u32[]{:S(2)}) copy-start(f32[2,6,6,768]{3,0,2,1:T(2,128)} %param.20) | copy-start | bytes 663556
  16.7 3.0 %collective-permute-start.2 = (f32[48,768]{1,0:T(8,128)S(1)}, f32[48,768]{1,0:T(8,128)S(1)}, u32[]{:S(2)}, u32[]{:S(2)}) collective-permute-start(f32[48,768]{1,0:T(8,128)S(1)} %get-tuple-element.91), channel_id=1, source_target_pairs={{1,0},{3,2},{5,4},{7,6},{9,8},{11,10},{13,12},{15,14},{0,1},{2,3},... | collective-permute-start | bytes 442376 | tf_op jit(solution)/shard_map/ppermute | solution.py:43
  16.7 7.3 %collective-permute-start.3 = (f32[48,768]{1,0:T(8,128)S(1)}, f32[48,768]{1,0:T(8,128)S(1)}, u32[]{:S(2)}, u32[]{:S(2)}) collective-permute-start(f32[48,768]{1,0:T(8,128)S(1)} %get-tuple-element.92), channel_id=1, source_target_pairs={{1,2},{3,4},{5,6},{7,8},{9,10},{11,12},{13,14},{15,0},{2,1},{4,3},... | collective-permute-start | bytes 442376 | tf_op jit(solution)/shard_map/ppermute | solution.py:41
  24.8 3.0 %collective-permute-start.4 = (f32[48,768]{1,0:T(8,128)S(1)}, f32[48,768]{1,0:T(8,128)S(1)}, u32[]{:S(2)}, u32[]{:S(2)}) collective-permute-start(f32[48,768]{1,0:T(8,128)S(1)} %get-tuple-element.103), channel_id=1, source_target_pairs={{1,0},{3,2},{5,4},{7,6},{9,8},{11,10},{13,12},{15,14},{0,1},{2,3},... | collective-permute-start | bytes 442376 | tf_op jit(solution)/shard_map/ppermute | solution.py:43
  24.8 7.3 %collective-permute-start.5 = (f32[48,768]{1,0:T(8,128)S(1)}, f32[48,768]{1,0:T(8,128)S(1)}, u32[]{:S(2)}, u32[]{:S(2)}) collective-permute-start(f32[48,768]{1,0:T(8,128)S(1)} %get-tuple-element.104), channel_id=1, source_target_pairs={{1,2},{3,4},{5,6},{7,8},{9,10},{11,12},{13,14},{15,0},{2,1},{4,3},... | collective-permute-start | bytes 442376 | tf_op jit(solution)/shard_map/ppermute | solution.py:41
  32.4 21.5 %collective-permute-start.6 = (f32[48,768]{1,0:T(8,128)S(1)}, f32[48,768]{1,0:T(8,128)S(1)}, u32[]{:S(2)}, u32[]{:S(2)}) collective-permute-start(f32[48,768]{1,0:T(8,128)S(1)} %get-tuple-element.116), channel_id=1, source_target_pairs={{1,0},{3,2},{5,4},{7,6},{9,8},{11,10},{13,12},{15,14},{0,1},{2,3},... | collective-permute-start | bytes 442376 | tf_op jit(solution)/shard_map/ppermute | solution.py:43
  32.5 21.5 %collective-permute-start.7 = (f32[48,768]{1,0:T(8,128)S(1)}, f32[48,768]{1,0:T(8,128)S(1)}, u32[]{:S(2)}, u32[]{:S(2)}) collective-permute-start(f32[48,768]{1,0:T(8,128)S(1)} %get-tuple-element.117), channel_id=1, source_target_pairs={{1,2},{3,4},{5,6},{7,8},{9,10},{11,12},{13,14},{15,0},{2,1},{4,3},... | collective-permute-start | bytes 442376 | tf_op jit(solution)/shard_map/ppermute | solution.py:41
  39.5 3.1 %collective-permute-start.10 = (f32[16,128]{1,0:T(8,128)S(1)}, f32[16,128]{1,0:T(8,128)S(1)}, u32[]{:S(2)}, u32[]{:S(2)}) collective-permute-start(f32[16,128]{1,0:T(8,128)S(1)} %get-tuple-element.127.refs_0_), channel_id=1, source_target_pairs={{0,3},{1,2},{2,1},{3,0},{4,7},{5,6},{6,5},{7,4},{8,11},{9,10},{10,... | collective-permute-start | bytes 24584 | tf_op jit(solution)/shard_map/ppermute | solution.py:77
  39.5 3.7 %collective-permute-start.9 = (f32[16,128]{1,0:T(8,128)S(1)}, f32[16,128]{1,0:T(8,128)S(1)}, u32[]{:S(2)}, u32[]{:S(2)}) collective-permute-start(f32[16,128]{1,0:T(8,128)S(1)} %get-tuple-element.127.refs_0_), channel_id=1, source_target_pairs={{0,2},{1,3},{2,0},{3,1},{4,6},{5,7},{6,4},{7,5},{8,10},{9,11},{10,... | collective-permute-start | bytes 24584 | tf_op jit(solution)/shard_map/ppermute | solution.py:77
  40.2 3.0 %collective-permute-start.8 = (f32[16,128]{1,0:T(8,128)S(1)}, f32[16,128]{1,0:T(8,128)S(1)}, u32[]{:S(2)}, u32[]{:S(2)}) collective-permute-start(f32[16,128]{1,0:T(8,128)S(1)} %get-tuple-element.127.refs_0_), channel_id=1, source_target_pairs={{0,1},{1,0},{2,3},{3,2},{4,5},{5,4},{6,7},{7,6},{8,9},{9,8},{10,11... | collective-permute-start | bytes 24584 | tf_op jit(solution)/shard_map/ppermute | solution.py:77
  43.3 5.7 %collective-permute-start.13 = (f32[64,128]{1,0:T(8,128)S(1)}, f32[64,128]{1,0:T(8,128)S(1)}, u32[]{:S(2)}, u32[]{:S(2)}) collective-permute-start(f32[64,128]{1,0:T(8,128)S(1)} %packed.1.refs_0_), channel_id=1, source_target_pairs={{0,12},{1,13},{2,14},{3,15},{4,8},{5,9},{6,10},{7,11},{8,4},{9,5},... | collective-permute-start | bytes 98312 | tf_op jit(solution)/shard_map/ppermute | solution.py:77
  46.8 4.8 %collective-permute-start.12 = (f32[64,128]{1,0:T(8,128)S(1)}, f32[64,128]{1,0:T(8,128)S(1)}, u32[]{:S(2)}, u32[]{:S(2)}) collective-permute-start(f32[64,128]{1,0:T(8,128)S(1)} %packed.1.refs_0_), channel_id=1, source_target_pairs={{0,8},{1,9},{2,10},{3,11},{4,12},{5,13},{6,14},{7,15},{8,0},{9,1},... | collective-permute-start | bytes 98312 | tf_op jit(solution)/shard_map/ppermute | solution.py:77
  46.8 4.8 %collective-permute-start.11 = (f32[64,128]{1,0:T(8,128)S(1)}, f32[64,128]{1,0:T(8,128)S(1)}, u32[]{:S(2)}, u32[]{:S(2)}) collective-permute-start(f32[64,128]{1,0:T(8,128)S(1)} %packed.1.refs_0_), channel_id=1, source_target_pairs={{0,4},{1,5},{2,6},{3,7},{4,0},{5,1},{6,2},{7,3},{8,12},{9,13},{10,... | collective-permute-start | bytes 98312 | tf_op jit(solution)/shard_map/ppermute | solution.py:77

commit v3 on v2

v3 whole, which is shorter than its diff:
```python
import math

import jax
import jax.numpy as jnp
import numpy as np
from jax import lax
from jax.experimental import pallas as pl
from jax.experimental.pallas import tpu as pltpu
from jax.sharding import PartitionSpec as P


KSPAN = 64

COURANT = 0.5
SIGMA_MAX = 0.8
PML_ALPHA = 0.05

ROWS = 8
LANES = 128
F32 = jnp.float32

HBM = pl.BlockSpec(memory_space=pltpu.HBM)
VMEM = pl.BlockSpec(memory_space=pltpu.VMEM)
SMEM = pl.BlockSpec(memory_space=pltpu.SMEM)


def params():
    return pltpu.CompilerParams(vmem_limit_bytes=24 << 20)


def in_hbm(value):
    return pltpu.with_memory_space_constraint(value, pltpu.HBM)


def exchanged(near, far):
    count = lax.axis_size("gx")
    assert count % 2 == 0
    odd = range(1, count, 2)
    pairs = [(i, (i + 1) % count) for i in odd] + [((i + 1) % count, i) for i in odd]
    far = lax.ppermute(far, "gx", pairs)
    pairs = [(i, i - 1) for i in odd] + [(i - 1, i) for i in odd]
    near = lax.ppermute(near, "gx", pairs)
    return near, far


def is_odd():
    return lax.rem(lax.axis_index("gx"), 2) == 1


def sort_out(back, ahead, near, far):
    @pl.when(is_odd())
    def _():
        near[...] = back[...]
        far[...] = ahead[...]

    @pl.when(jnp.logical_not(is_odd()))
    def _():
        near[...] = ahead[...]
        far[...] = back[...]


def sort_in(near, far, from_ahead, from_behind):
    @pl.when(is_odd())
    def _():
        from_behind[...] = near[...]
        from_ahead[...] = far[...]

    @pl.when(jnp.logical_not(is_odd()))
    def _():
        from_ahead[...] = near[...]
        from_behind[...] = far[...]


def swapped(value, mask):
    count = lax.axis_size("gx")
    return lax.ppermute(value, "gx", [(source, source ^ mask) for source in range(count)])


def pml(layers, offset, width):
    row = lax.broadcasted_iota(jnp.int32, (ROWS, LANES), 0)
    depth = (layers - row.astype(F32) - offset) / layers
    sigma = SIGMA_MAX * depth * depth * depth
    decay = jnp.exp(-(sigma + PML_ALPHA))
    gain = sigma / (sigma + PML_ALPHA) * (decay - 1.0)
    inside = row < layers
    wide = lambda v: jnp.concatenate([jnp.where(inside, v, 0.0)] * (width // LANES), axis=1)
    return wide(decay), wide(gain)


def tile_of(ref, lead, k):
    return ref[(*lead, slice(ROWS * k, ROWS * k + ROWS), slice(None))]


def put_tile(ref, lead, k, value):
    ref[(*lead, slice(ROWS * k, ROWS * k + ROWS), slice(None))] = value


def row_ids(value):
    return lax.broadcasted_iota(jnp.int32, value.shape, 0)


def up(ref, lead, k, tiles, here):
    if k + 1 < tiles:
        return ref[(*lead, slice(ROWS * k + 1, ROWS * k + ROWS + 1), slice(None))]
    return jnp.where(row_ids(here) < ROWS - 1, pltpu.roll(here, ROWS - 1, 0), 0.0)


def down(ref, lead, k, here):
    if k > 0:
        return ref[(*lead, slice(ROWS * k - 1, ROWS * k + ROWS - 1), slice(None))]
    return jnp.where(row_ids(here) > 0, pltpu.roll(here, 1, 0), 0.0)


def y_forward(value):
    return pltpu.roll(value, value.shape[-1] - 1, 1) - value


def y_backward(value):
    return value - pltpu.roll(value, 1, 1)


def lookup(material, table):
    count = table.shape[0]
    total = jnp.full(material.shape, table[count - 1], F32)
    for index in range(count - 1):
        total = jnp.where(material == index, table[index], total)
    return total


def h_values(here, above, ahead, old, psi, coef):
    decay, gain = coef
    ex, ey, ez = here
    dex_dz, dey_dz = above[0] - ex, above[1] - ey
    curl_x = y_forward(ez) - dey_dz
    curl_y = dex_dz + ez
    curl_z = -ey - y_forward(ex)
    memory = None
    if psi is not None:
        memory = (decay * psi[0] + gain * dey_dz, decay * psi[1] + gain * dex_dz)
        curl_x = curl_x - memory[0]
        curl_y = curl_y + memory[1]
    if ahead is not None:
        curl_y = curl_y - ahead[1]
        curl_z = curl_z + ahead[0]
    return tuple(o - COURANT * c for o, c in zip(old, (curl_x, curl_y, curl_z))), memory


def curl_of_h(here, below, behind, psi, coef):
    decay, gain = coef
    hx, hy, hz = here
    dhx_dz, dhy_dz = hx - below[0], hy - below[1]
    curl_x = y_backward(hz) - dhy_dz
    curl_y = dhx_dz - hz
    curl_z = hy - y_backward(hx)
    memory = None
    if psi is not None:
        memory = (decay * psi[0] + gain * dhy_dz, decay * psi[1] + gain * dhx_dz)
        curl_x = curl_x - memory[0]
        curl_y = curl_y + memory[1]
    if behind is not None:
        curl_y = curl_y + behind[1]
        curl_z = curl_z - behind[0]
    return (curl_x, curl_y, curl_z), memory


def material_step(old, curl, pol, cur, mats):
    inv, dec, drv, spr = mats
    cur = dec * cur + (drv * old - spr * pol)
    return old + inv * (COURANT * curl - cur), pol + cur, cur


def response(hy, hz, hy_below, half, gain):
    step = hy - hy_below
    curl_x = y_backward(hz) - step
    memory = None
    if gain is not None:
        memory = gain * step
        curl_x = curl_x - memory
    return (half * curl_x, -half * hz, half * hy), memory


def three(ref, i, k):
    return tuple(tile_of(ref, (c, i), k) for c in range(3))


def h_plane(e, h, psi_h, i, tiles, coef, ahead):
    for k in range(tiles):
        here = three(e, i, k)
        above = tuple(up(e, (c, i), k, tiles, here[c]) for c in range(2))
        psi = (psi_h[0, i], psi_h[1, i]) if k == 0 else None
        new, memory = h_values(here, above, ahead(k), three(h, i, k), psi, coef)
        for c in range(3):
            put_tile(h, (c, i), k, new[c])
        if k == 0:
            psi_h[0, i], psi_h[1, i] = memory


def e_plane(e, h, polar, current, psi_e, mats, i, tiles, coef, behind):
    for k in range(tiles):
        here = three(h, i, k)
        below = tuple(down(h, (c, i), k, here[c]) for c in range(2))
        psi = (psi_e[0, i], psi_e[1, i]) if k == 0 else None
        curl, memory = curl_of_h(here, below, behind(k), psi, coef)
        if k == 0:
            psi_e[0, i], psi_e[1, i] = memory
        values = tuple(tile_of(m, (i,), k) for m in mats)
        for c in range(3):
            found = material_step(
                tile_of(e, (c, i), k), curl[c], tile_of(polar, (c, i), k), tile_of(current, (c, i), k), values
            )
            for ref, value in zip((e, polar, current), found):
                put_tile(ref, (c, i), k, value)


def nothing(k):
    return None


def full_step(state, mats, planes, tiles, coef_h, coef_e, ahead, behind, before=None, after=None):
    e, h, polar, current, psi_h, psi_e = state

    def plane(i, ahead, behind):
        if before is not None:
            before(i)
        h_plane(e, h, psi_h, i, tiles, coef_h, ahead)
        e_plane(e, h, polar, current, psi_e, mats, i, tiles, coef_e, behind)
        if after is not None:
            after(i)

    def next_e(i):
        return lambda k: (tile_of(e, (1, i + 1), k), tile_of(e, (2, i + 1), k))

    def past_h(i):
        return lambda k: (tile_of(h, (1, i - 1), k), tile_of(h, (2, i - 1), k))

    def step(i, carry):
        plane(i, next_e(i), past_h(i))
        return carry

    plane(0, next_e(0), behind)
    lax.fori_loop(1, planes - 1, step, 0)
    plane(planes - 1, ahead, past_h(planes - 1))


def pair_of(ref, row, tiles):
    return lambda k: (tile_of(ref, (), row + k), tile_of(ref, (), row + tiles + k))


def outlook(state, mats, scratch, planes, tiles, coef_h, coef_e, back, ahead):
    e, h, polar, current, psi_h, psi_e = state
    h_first, h_last, h_past, e_last = scratch
    edge = planes - 1
    kept = None
    for k in range(tiles):
        for i in (0, edge - 1, edge):
            here = three(e, i, k)
            above = tuple(up(e, (c, i), k, tiles, here[c]) for c in range(2))
            psi = (psi_h[0, i], psi_h[1, i]) if k == 0 else None
            ey_ez = None if i == edge else (tile_of(e, (1, i + 1), k), tile_of(e, (2, i + 1), k))
            new, memory = h_values(here, above, ey_ez, three(h, i, k), psi, coef_h)
            if i == 0:
                put_tile(back, (), k, here[1])
                put_tile(back, (), tiles + k, here[2])
                for c in range(3):
                    put_tile(h_first, (c,), k, new[c])
            elif i == edge:
                put_tile(ahead, (), k, new[1])
                put_tile(ahead, (), tiles + k, new[2])
                for c in range(3):
                    put_tile(h_last, (c,), k, new[c])
                if k == 0:
                    kept = memory
            else:
                put_tile(h_past, (0,), k, new[1])
                put_tile(h_past, (1,), k, new[2])
    for i, ref in ((edge, h_last), (0, h_first)):
        for k in range(tiles):
            here = tuple(tile_of(ref, (c,), k) for c in range(3))
            below = tuple(down(ref, (c,), k, here[c]) for c in range(2))
            psi = (psi_e[0, i], psi_e[1, i]) if k == 0 else None
            behind = (tile_of(h_past, (0,), k), tile_of(h_past, (1,), k)) if i == edge else None
            curl, _ = curl_of_h(here, below, behind, psi, coef_e)
            values = tuple(tile_of(m, (i,), k) for m in mats)
            for c in range(3):
                new, _, _ = material_step(
                    tile_of(e, (c, i), k), curl[c], tile_of(polar, (c, i), k), tile_of(current, (c, i), k), values
                )
                if i == edge:
                    put_tile(e_last, (c,), k, new)
                elif c > 0:
                    put_tile(back, (), (c + 1) * tiles + k, new)
    for k in range(tiles):
        here = tuple(tile_of(e_last, (c,), k) for c in range(3))
        above = tuple(up(e_last, (c,), k, tiles, here[c]) for c in range(2))
        old = tuple(tile_of(h_last, (c,), k) for c in range(3))
        new, _ = h_values(here, above, None, old, kept if k == 0 else None, coef_h)
        put_tile(ahead, (), 2 * tiles + k, new[1])
        put_tile(ahead, (), 3 * tiles + k, new[2])


def outlook_scratch(depth, width):
    field = pltpu.VMEM((3, depth, width), F32)
    return [field, field, pltpu.VMEM((2, depth, width), F32), field]


def start_all(copies):
    for copy in copies:
        copy.start()


def wait_all(copies):
    for copy in copies:
        copy.wait()


def state_shapes(planes, depth, width):
    field = pltpu.VMEM((3, planes, depth, width), F32)
    memory = pltpu.VMEM((2, planes, ROWS, width), F32)
    return (field, field, field, field, memory, memory)


def fill_mats(mats, material, tables, i, tiles):
    t0, t1, t2, t3, t4 = tables
    inv, dec, drv, spr = mats
    for k in range(tiles):
        m = tile_of(material, (i,), k)
        drive = lookup(m, t2)
        put_tile(inv, (i,), k, lookup(m, t0))
        put_tile(dec, (i,), k, lookup(m, t1))
        put_tile(drv, (i,), k, drive * lookup(m, t3))
        put_tile(spr, (i,), k, drive * lookup(m, t4))


def begin(fields, memories, material, tables):
    planes, depth, width = material.shape
    layers = memories[0].shape[1]
    tiles = depth // ROWS
    edge = planes - 1
    rows = 4 * depth + depth + 2 * ROWS
    order = list(dict.fromkeys([0, edge, edge - 1, 1, *range(planes)]))
    first = order[:4]

    def body(*refs):
        sources, tables_in = refs[:7], refs[7:12]
        state = refs[12:18]
        mat, inv, dec, drv, spr, near, far, back = refs[18:26]
        ahead = refs[26]
        scratch = refs[27:31]
        tables = refs[31:36]
        sem, sem_psi, sem_table = refs[36:39]
        zero = jnp.zeros((ROWS, width), F32)
        for ref in state[4:]:
            for c in range(2):
                for i in range(planes):
                    ref[c, i] = zero

        def copies(i):
            found = [
                pltpu.make_async_copy(sources[n].at[:, i], state[n].at[:, i], sem.at[n, i]) for n in range(4)
            ]
            for n in range(2):
                for c in range(2):
                    source = sources[4 + n].at[i, :, c]
                    target = state[4 + n].at[c, i, 0:layers]
                    found.append(pltpu.make_async_copy(source, target, sem_psi.at[2 * n + c, i]))
            found.append(pltpu.make_async_copy(sources[6].at[i], mat.at[i], sem.at[4, i]))
            return found

        small = [pltpu.make_async_copy(s, d, sem_table.at[n]) for n, (s, d) in enumerate(zip(tables_in, tables))]
        start_all(small)
        for i in order:
            start_all(copies(i))
        coef_h = pml(layers, 0.5, width)
        coef_e = pml(layers, 0.0, width)
        wait_all(small)
        for i in first:
            wait_all(copies(i))
        mats = (inv, dec, drv, spr)
        for i in (0, edge):
            fill_mats(mats, mat, tables, i, tiles)
        outlook(state, mats, scratch, planes, tiles, coef_h, coef_e, back, ahead)
        for i, inner, ref in ((0, 1, back), (edge, edge - 1, ahead)):
            for k in range(tiles):
                put_tile(ref, (), 4 * tiles + k, tile_of(inv, (i,), k))
            put_tile(ref, (), 5 * tiles, lookup(tile_of(mat, (inner,), 0), tables[0]))
            put_tile(ref, (), 5 * tiles + 1, tile_of(drv, (i,), 0))
        sort_out(back, ahead, near, far)
        for i in order[4:]:
            wait_all(copies(i))

    message = pltpu.VMEM((rows, width), F32)
    coef = pltpu.VMEM((planes, depth, width), F32)
    found = pl.pallas_call(
        body,
        name="begin",
        out_shape=(
            *state_shapes(planes, depth, width),
            pltpu.VMEM((planes, depth, width), jnp.int32),
            coef,
            coef,
            coef,
            coef,
            message,
            message,
            message,
        ),
        in_specs=[HBM] * 12,
        out_specs=(VMEM,) * 14,
        scratch_shapes=[
            message,
            *outlook_scratch(depth, width),
            *(pltpu.SMEM(table.shape, F32) for table in tables),
            pltpu.SemaphoreType.DMA((5, planes)),
            pltpu.SemaphoreType.DMA((4, planes)),
            pltpu.SemaphoreType.DMA((len(tables),)),
        ],
        compiler_params=params(),
    )(*(in_hbm(x) for x in (*fields, *memories, material, *tables)))
    return found[:6], found[6], found[7:11], found[11], found[12], found[13]


def interior(state, mats, layers, material=None, tables=()):
    planes, depth, width = state[0].shape[1:]
    tiles = depth // ROWS
    fill = material is not None
    extra = (material, *tables) if fill else ()
    count = 10 if fill else 6

    def body(*refs):
        inputs, outputs = refs[: 10 + len(extra)], refs[10 + len(extra) :]
        state = outputs[:6]
        mats = outputs[6:10] if fill else inputs[6:10]
        coef_h = pml(layers, 0.5, width)
        coef_e = pml(layers, 0.0, width)
        if fill:

            def step(i, carry):
                fill_mats(mats, inputs[10], inputs[11:], i, tiles)
                return carry

            lax.fori_loop(1, planes - 1, step, 0)
        full_step(state, mats, planes, tiles, coef_h, coef_e, nothing, nothing)

    coef = pltpu.VMEM((planes, depth, width), F32)
    shapes = (*state_shapes(planes, depth, width), coef, coef, coef, coef)
    found = pl.pallas_call(
        body,
        name="first_interior" if fill else "interior",
        out_shape=shapes[:count],
        in_specs=[VMEM] * 10 + ([VMEM] + [SMEM] * len(tables) if fill else []),
        out_specs=(VMEM,) * count,
        input_output_aliases={n: n for n in range(count)},
        compiler_params=params(),
    )(*state, *mats, *extra)
    return found[:6], (found[6:] if fill else mats)


def close_step(state, mats, back, ahead, behind, around, scratch, planes, tiles, coef_h, coef_e):
    e, h, _, _, _, psi_e = state
    inv = mats[0]
    e_ahead, h_behind, e_turn = scratch
    edge = planes - 1
    gain_h, gain_e = coef_h[1], coef_e[1]
    for k in range(tiles):
        old_y, old_z = tile_of(back, (), k), tile_of(back, (), tiles + k)
        half = COURANT * tile_of(inv, (0,), k)
        hy = tile_of(behind, (), k) + COURANT * old_z
        hz = tile_of(behind, (), tiles + k) - COURANT * old_y
        put_tile(e, (1, 0), k, tile_of(e, (1, 0), k) + half * hz)
        put_tile(e, (2, 0), k, tile_of(e, (2, 0), k) - half * hy)

        far_y, far_z = tile_of(ahead, (), k), tile_of(ahead, (), tiles + k)
        delta_y, delta_z = COURANT * far_z, -COURANT * far_y
        below = COURANT * down(ahead, (), tiles + k, far_z) if k > 0 else down(None, (), 0, delta_y)
        change, memory = response(delta_y, delta_z, below, COURANT * tile_of(inv, (edge,), k), gain_e if k == 0 else None)
        if k == 0:
            psi_e[0, edge] = psi_e[0, edge] + memory
        for c in range(3):
            put_tile(e, (c, edge), k, tile_of(e, (c, edge), k) + change[c])
        hy = tile_of(h, (1, edge), k) + delta_y
        hz = tile_of(h, (2, edge), k) + delta_z
        put_tile(h, (1, edge), k, hy)
        put_tile(h, (2, edge), k, hz)
        half = COURANT * tile_of(around, (), k)
        put_tile(e_ahead, (), k, tile_of(ahead, (), 2 * tiles + k) + half * hz)
        put_tile(e_ahead, (), tiles + k, tile_of(ahead, (), 3 * tiles + k) - half * hy)

        delta_y, delta_z = COURANT * old_z, -COURANT * old_y
        below = COURANT * down(back, (), tiles + k, old_z) if k > 0 else down(None, (), 0, delta_y)
        half = COURANT * tile_of(around, (), tiles + k)
        change, _ = response(delta_y, delta_z, below, half, gain_e if k == 0 else None)
        for c in range(3):
            put_tile(e_turn, (c,), k, change[c])
    for k in range(tiles):
        ex, ey, ez = (tile_of(e_turn, (c,), k) for c in range(3))
        dex_dz = up(e_turn, (0,), k, tiles, ex) - ex
        curl_y = dex_dz + ez
        if k == 0:
            curl_y = curl_y + gain_h * dex_dz
        old_y, old_z = tile_of(back, (), k), tile_of(back, (), tiles + k)
        hy = tile_of(behind, (), 2 * tiles + k) + COURANT * (old_z - curl_y + tile_of(e, (2, 0), k))
        hz = tile_of(behind, (), 3 * tiles + k) + COURANT * (ey + y_forward(ex) - old_y - tile_of(e, (1, 0), k))
        put_tile(h_behind, (), k, hy)
        put_tile(h_behind, (), tiles + k, hz)


def close_scratch(depth, width):
    return [
        pltpu.VMEM((2 * depth, width), F32),
        pltpu.VMEM((2 * depth, width), F32),
        pltpu.VMEM((3, depth, width), F32),
    ]


def middle(state, mats, back, near, far, layers):
    planes, depth, width = state[0].shape[1:]
    tiles = depth // ROWS
    rows = 2 * depth + 4 * ROWS

    def body(*refs):
        mats, back_in, near_in, far_in = refs[6:10], refs[10], refs[11], refs[12]
        state = refs[13:19]
        near, far, back, around = refs[19:23]
        ahead, behind = refs[23:25]
        scratch, outlook_refs, sent = refs[25:28], refs[28:32], refs[32]
        coef_h = pml(layers, 0.5, width)
        coef_e = pml(layers, 0.0, width)
        sort_in(near_in, far_in, ahead, behind)
        for n, ref in enumerate((ahead, behind)):
            for k in range(tiles):
                put_tile(around, (), n * tiles + k, tile_of(ref, (), 4 * tiles + k))
            for k in range(2):
                put_tile(around, (), 2 * tiles + 2 * n + k, tile_of(ref, (), 5 * tiles + k))
        close_step(state, mats, back_in, ahead, behind, around, scratch, planes, tiles, coef_h, coef_e)
        full_step(
            state, mats, planes, tiles, coef_h, coef_e, pair_of(scratch[0], 0, tiles), pair_of(scratch[1], 0, tiles)
        )
        outlook(state, mats, outlook_refs, planes, tiles, coef_h, coef_e, back, sent)
        sort_out(back, sent, near, far)

    message = pltpu.VMEM((4 * depth, width), F32)
    whole = pltpu.VMEM(near.shape, F32)
    found = pl.pallas_call(
        body,
        name="middle",
        out_shape=(*state_shapes(planes, depth, width), message, message, message, pltpu.VMEM((rows, width), F32)),
        in_specs=[VMEM] * 13,
        out_specs=(VMEM,) * 10,
        input_output_aliases={n: n for n in range(6)},
        scratch_shapes=[whole, whole, *close_scratch(depth, width), *outlook_scratch(depth, width), message],
        compiler_params=params(),
    )(*state, *mats, back, near, far)
    return found[:6], found[6], found[7], found[8], found[9]


def spectral_rows(planes):
    return -(-(2 * planes + 7) // ROWS) * ROWS


def foretold(state, mats, around, table, layers):
    planes, depth, width = state[0].shape[1:]
    tiles = depth // ROWS
    edge = planes - 1
    wide = planes + 4
    count = spectral_rows(planes)
    assert 2 <= layers <= ROWS - 2

    def body(*refs):
        mats, around, table = refs[6:10], refs[10], refs[11]
        e, h, polar, current, psi_h, psi_e = refs[12:18]
        mixed, e_one, h_one, p_one, c_one, psi_one, h_two, rows = refs[18:]
        coef_h = pml(layers, 0.5, width)
        coef_e = pml(layers, 0.0, width)
        zero = jnp.zeros((ROWS, width), F32)
        low = lambda v: jnp.where(row_ids(v) > 0, pltpu.roll(v, 1, 0), 0.0)
        high = lambda v: pltpu.roll(v, ROWS - 1, 0)
        inv_ahead, inv_behind = tile_of(around, (), 0), tile_of(around, (), tiles)
        far_ahead, drv_ahead = tile_of(around, (), 2 * tiles), tile_of(around, (), 2 * tiles + 1)
        far_behind, drv_behind = tile_of(around, (), 2 * tiles + 2), tile_of(around, (), 2 * tiles + 3)

        def get(ref, n):
            return tuple(ref[c, n] for c in range(ref.shape[0]))

        def put(ref, n, values):
            for c, value in enumerate(values):
                ref[c, n] = value

        def own(ref, i):
            return tuple(tile_of(ref, (c, i), 0) for c in range(ref.shape[0]))

        def h_first(i, last):
            here = own(e, i)
            above = tuple(up(e, (c, i), 0, tiles, here[c]) for c in range(2))
            ahead = None if last else (tile_of(e, (1, i + 1), 0), tile_of(e, (2, i + 1), 0))
            new, memory = h_values(here, above, ahead, own(h, i), (psi_h[0, i], psi_h[1, i]), coef_h)
            put(h_one, i + 2, new)
            put(psi_one, i + 2, memory)

        def e_first(i):
            here = get(h_one, i + 2)
            behind = get(h_one, i + 1)[1:]
            curl, _ = curl_of_h(here, (low(here[0]), low(here[1])), behind, (psi_e[0, i], psi_e[1, i]), coef_e)
            values = tuple(tile_of(m, (i,), 0) for m in mats)
            for c in range(3):
                found = material_step(
                    tile_of(e, (c, i), 0), curl[c], tile_of(polar, (c, i), 0), tile_of(current, (c, i), 0), values
                )
                for ref, value in zip((e_one, p_one, c_one), found):
                    ref[c, i + 2] = value

        old = own(e, 0)
        turn = (COURANT * old[2], -COURANT * old[1])
        put(h_one, 1, (zero, *turn))

        def first(i, carry):
            h_first(i, False)
            e_first(i)
            return carry

        lax.fori_loop(0, edge, first, 0)
        h_first(edge, True)
        e_first(edge)
        change, _ = response(*turn, low(turn[0]), COURANT * inv_behind, coef_e[1])
        put(e_one, 1, change)
        out = get(h_one, edge + 2)
        half = COURANT * inv_ahead
        put(e_one, planes + 2, (zero, half * out[2], -half * out[1]))

        def h_second(n, memory, old, ahead):
            here = get(e_one, n)
            new, _ = h_values(here, (high(here[0]), high(here[1])), ahead, old, memory, coef_h)
            put(h_two, n, new)

        def e_second(n, drive, inv, rest):
            hx, hy, hz = get(h_two, n)
            behind = h_two[2, n - 1]
            curl_x = y_backward(hz) - (hy - low(hy))
            curl_y = hx - low(hx) - (hz - behind)
            for c, curl in enumerate((curl_x, curl_y)):
                cur = drive * e_one[c, n]
                if rest is not None:
                    cur = cur + rest[0] * c_one[c, n] - rest[1] * p_one[c, n]
                keep(c, n, e_one[c, n] + inv * (COURANT * curl - cur))

        def keep(c, n, value):
            rows[pl.ds(c * wide + n, 1), :] = value[layers : layers + 1, :]

        rows[...] = jnp.zeros_like(rows)
        put(h_two, 0, (zero, COURANT * e_one[2, 1], -COURANT * e_one[1, 1]))
        h_second(1, (zero, zero), get(h_one, 1), get(e_one, 2)[1:])
        _, hy, hz = get(h_two, 0)
        half = COURANT * far_behind
        keep(0, 0, half * (y_backward(hz) - (hy - low(hy))))
        keep(1, 0, -half * hz)
        e_second(1, drv_behind, inv_behind, None)

        def second(n, carry):
            h_second(n, get(psi_one, n), get(h_one, n), get(e_one, n + 1)[1:])
            inv, dec, drv, spr = (tile_of(m, (n - 2,), 0) for m in mats)
            e_second(n, drv, inv, (dec, spr))
            return carry

        lax.fori_loop(2, planes + 2, second, 0)
        n = planes + 2
        h_second(n, (zero, zero), (zero, zero, zero), None)
        e_second(n, drv_ahead, inv_ahead, None)
        keep(1, n + 1, COURANT * far_ahead * h_two[2, n])
        mixed[...] = jnp.dot(rows[...], table[...], precision=lax.Precision.HIGHEST, preferred_element_type=F32)

    shape = pltpu.VMEM((3, wide, ROWS, width), F32)
    found = pl.pallas_call(
        body,
        name="foretold",
        out_shape=(*state_shapes(planes, depth, width), pltpu.VMEM((count, table.shape[1]), F32)),
        in_specs=[VMEM] * 12,
        out_specs=(VMEM,) * 7,
        input_output_aliases={n: n for n in range(6)},
        scratch_shapes=[
            shape,
            shape,
            shape,
            shape,
            pltpu.VMEM((2, wide, ROWS, width), F32),
            shape,
            pltpu.VMEM((count, width), F32),
        ],
        compiler_params=params(),
    )(*state, *mats, around, table)
    return found[:6], found[6]


def finish(state, mats, back, near, far, around, layers):
    planes, depth, width = state[0].shape[1:]
    tiles = depth // ROWS

    def body(*refs):
        mats, back, near_in, far_in, around = refs[6:10], refs[10], refs[11], refs[12], refs[13]
        state, outs = refs[14:20], refs[20:26]
        ahead, behind = refs[26:28]
        scratch, sem, sem_psi = refs[28:31], refs[31], refs[32]
        coef_h = pml(layers, 0.5, width)
        coef_e = pml(layers, 0.0, width)
        sort_in(near_in, far_in, ahead, behind)
        close_step(state, mats, back, ahead, behind, around, scratch, planes, tiles, coef_h, coef_e)

        def copies(i):
            found = [pltpu.make_async_copy(state[n].at[:, i], outs[n].at[:, i], sem.at[n, i]) for n in range(4)]
            for n in range(2):
                for c in range(2):
                    source = state[4 + n].at[c, i, 0:layers]
                    target = outs[4 + n].at[i, :, c]
                    found.append(pltpu.make_async_copy(source, target, sem_psi.at[2 * n + c, i]))
            return found

        full_step(
            state,
            mats,
            planes,
            tiles,
            coef_h,
            coef_e,
            pair_of(scratch[0], 0, tiles),
            pair_of(scratch[1], 0, tiles),
            after=lambda i: start_all(copies(i)),
        )
        for i in range(planes):
            wait_all(copies(i))

    field = jax.ShapeDtypeStruct((3, planes, depth, width), F32)
    memory = jax.ShapeDtypeStruct((planes, layers, 2, width), F32)
    whole = pltpu.VMEM(near.shape, F32)
    found = pl.pallas_call(
        body,
        name="finish",
        out_shape=(*state_shapes(planes, depth, width), field, field, field, field, memory, memory),
        in_specs=[VMEM] * 14,
        out_specs=(VMEM,) * 6 + (HBM,) * 6,
        input_output_aliases={n: n for n in range(6)},
        scratch_shapes=[
            whole,
            whole,
            *close_scratch(depth, width),
            pltpu.SemaphoreType.DMA((4, planes)),
            pltpu.SemaphoreType.DMA((4, planes)),
        ],
        compiler_params=params(),
    )(*state, *mats, back, near, far, around)
    return found[6:]


def y_table(cells):
    phase = np.arange(cells)[:, None] * (np.arange(KSPAN) - KSPAN // 2)[None, :] % cells
    phase = phase.astype(np.float64) * (2.0 * math.pi / cells)
    return np.concatenate([np.cos(phase), np.sin(phase)], axis=1).astype(np.float32)


def x_table(planes, count):
    rows = spectral_rows(planes)
    cells = planes * count
    wide = planes + 4
    comp = np.full(rows, -1)
    shift = np.zeros(rows, np.int64)
    for c in range(2):
        comp[c * wide : (c + 1) * wide] = c
        shift[c * wide : (c + 1) * wide] = np.arange(wide) - 2
    x = (np.arange(count)[:, None] * planes + shift[None, :]) % cells
    waves = np.arange(KSPAN) - KSPAN // 2
    phase = (waves[:, None, None] * x[None] % cells).astype(np.float64) * (2.0 * math.pi / cells)
    parts = []
    for c in range(2):
        for wave in (np.cos(phase), np.sin(phase)):
            parts.append(np.where(comp[None, None, :] == c, wave, 0.0).reshape(KSPAN, count * rows))
    return np.concatenate(parts, axis=0).astype(np.float32)


def packed(pieces):
    rows, width = pieces[0].shape

    def body(*refs):
        for n in range(len(pieces)):
            refs[-1][n * rows : n * rows + rows, :] = refs[n][...]

    return pl.pallas_call(
        body,
        name="packed",
        out_shape=pltpu.VMEM((rows * len(pieces), width), F32),
        in_specs=[VMEM] * len(pieces),
        out_specs=VMEM,
        compiler_params=params(),
    )(*pieces)


def gathered(block):
    count = lax.axis_size("gx")
    assert count & (count - 1) == 0
    pieces = [block]
    reach = 1
    while reach < count:
        ways = min(4, count // reach)
        held = pieces[0] if len(pieces) == 1 else packed(pieces)
        pieces = [held] + [swapped(held, reach * way) for way in range(1, ways)]
        reach *= ways
    return pieces


def prepared(orders, table_y, table_x):
    wide = orders.shape[1]
    chunk = 512 if wide % 512 == 0 else wide

    def body(orders_in, y_in, x_in, hit_y, hit_x, table_y, table_x, orders, sem):
        wanted = [(orders_in, orders), (y_in, table_y), (x_in, table_x)]
        copies = [pltpu.make_async_copy(s, d, sem.at[n]) for n, (s, d) in enumerate(wanted)]
        start_all(copies)
        wait_all(copies)
        for n in range(wide // chunk):
            span = slice(n * chunk, n * chunk + chunk)
            waves = lax.broadcasted_iota(jnp.int32, (KSPAN, chunk), 0) - KSPAN // 2
            hit = jnp.where(waves == orders[1:2, span], 1.0, 0.0).astype(jnp.bfloat16)
            for part in range(3):
                hit_y[part * KSPAN : (part + 1) * KSPAN, span] = hit
            hit_x[:, span] = jnp.where(waves == orders[0:1, span], 1.0, 0.0)

    return pl.pallas_call(
        body,
        name="prepared",
        out_shape=(
            pltpu.VMEM((3 * KSPAN, wide), jnp.bfloat16),
            pltpu.VMEM((KSPAN, wide), F32),
            pltpu.VMEM(table_y.shape, F32),
            pltpu.VMEM(table_x.shape, F32),
        ),
        in_specs=[HBM] * 3,
        out_specs=(VMEM,) * 4,
        scratch_shapes=[pltpu.VMEM(orders.shape, jnp.int32), pltpu.SemaphoreType.DMA((3,))],
        compiler_params=params(),
    )(in_hbm(orders), in_hbm(table_y), in_hbm(table_x))


def pick_orders(pieces, table, hit_y, hit_x, cells_total):
    count = lax.axis_size("gx")
    total = sum(piece.shape[0] for piece in pieces)
    rows = total // count
    wide = hit_x.shape[1]
    chunk = 512 if wide % 512 == 0 else wide
    scale = 1.0 / math.sqrt(cells_total)

    def body(*refs):
        held = refs[: len(pieces)]
        table, hit_y, hit_x, out, mixed = refs[len(pieces) :]
        here = lax.axis_index("gx")
        at = 0
        for ref in held:
            for n in range(ref.shape[0] // rows):
                slot = jnp.bitwise_xor(here, at)
                mixed[pl.ds(pl.multiple_of(slot * rows, rows), rows), :] = ref[n * rows : n * rows + rows, :]
                at += 1
        both = jnp.dot(table[...], mixed[...], precision=lax.Precision.HIGHEST, preferred_element_type=F32)
        parts = []
        for c in range(2):
            cosine = both[2 * c * KSPAN : (2 * c + 1) * KSPAN]
            sine = both[(2 * c + 1) * KSPAN : (2 * c + 2) * KSPAN]
            parts.append((cosine[:, :KSPAN] - sine[:, KSPAN:]) * scale)
            parts.append((cosine[:, KSPAN:] + sine[:, :KSPAN]) * -scale)
        spectrum = jnp.concatenate(parts, axis=0)
        high = spectrum.astype(jnp.bfloat16)
        rest = spectrum - high.astype(F32)
        mid = rest.astype(jnp.bfloat16)
        low = (rest - mid.astype(F32)).astype(jnp.bfloat16)
        split = jnp.concatenate([high, mid, low], axis=1)
        for n in range(wide // chunk):
            span = slice(n * chunk, n * chunk + chunk)
            lines = jnp.dot(split, hit_y[:, span], preferred_element_type=F32)
            hit = hit_x[:, span]
            for q in range(4):
                line = lines[q * KSPAN : (q + 1) * KSPAN] * hit
                out[q : q + 1, span] = jnp.sum(line, axis=0, keepdims=True)

    return pl.pallas_call(
        body,
        name="pick_orders",
        out_shape=jax.ShapeDtypeStruct((4, wide), F32),
        in_specs=[VMEM] * (len(pieces) + 3),
        out_specs=VMEM,
        scratch_shapes=[pltpu.VMEM((total, 2 * KSPAN), F32)],
        compiler_params=params(),
    )(*pieces, table, hit_y, hit_x)


def shards(
    e_field,
    h_field,
    polar,
    current,
    psi_h,
    psi_e,
    material,
    inv_eps_table,
    decay_table,
    drive_table,
    strength_table,
    spring_table,
    orders,
):
    planes, _, width = material.shape
    layers = psi_h.shape[2]
    count = lax.axis_size("gx")
    tables = (inv_eps_table, decay_table, drive_table, strength_table, spring_table)
    memories = tuple(jnp.transpose(psi, (1, 2, 0, 3)) for psi in (psi_h, psi_e))

    state, kinds, mats, near, far, back = begin(
        (e_field, h_field, polar, current), memories, material, tables
    )
    near, far = exchanged(near, far)
    state, mats = interior(state, mats, layers, kinds, tables)
    hit_y, hit_x, table_y, table_x = prepared(orders, jnp.asarray(y_table(width)), jnp.asarray(x_table(planes, count)))
    state, near, far, back, around = middle(state, mats, back, near, far, layers)
    near, far = exchanged(near, far)
    state, mixed = foretold(state, mats, around, table_y, layers)
    state, _ = interior(state, mats, layers)
    pieces = gathered(mixed)
    outs = finish(state, mats, back, near, far, around, layers)
    pupil = pick_orders(pieces, table_x, hit_y, hit_x, planes * count * width)
    outs = (*outs[:4], *(jnp.transpose(psi, (2, 0, 1, 3)) for psi in outs[4:]))
    return (*outs, pupil)


def solution(mesh):
    split = P(None, ("mask", "gx"), None, None)
    in_specs = (split,) * 6 + (P(("mask", "gx"), None, None),) + (P(),) * 6
    out_specs = (split,) * 6 + (P(None, "mask"),)
    return jax.shard_map(shards, mesh=mesh, in_specs=in_specs, out_specs=out_specs, check_vma=False)
```

time: 55.1 us -> 45.8 us (0.83)
  waiting for transfers between devices: 14.3 us -> 6.35 us
  local copies, waits for them, and re-layouts: 4.26 us -> 0.02 us
  starting transfers between devices: 17 us -> 18.8 us
  Pallas kernels: 18.5 us -> 19.7 us
    ppermute x4 -> x2, waiting for transfers between devices: 8.45 us -> 3.34 us  [exchanged(): far = lax.ppermute(far, 'gx', pairs)]
    unnamed x24 -> x10, local copies, waits for them, and re-layouts: 4.25 us -> 0.02 us
    ppermute x6, waiting for transfers between devices: 5.8 us -> 3 us  [swapped(): lax.ppermute(value, 'gx', [(source, source ^ mask) for source in range(co...]
    ppermute x4 -> x2, starting transfers between devices: 0.63 us -> 2.02 us  [exchanged(): near = lax.ppermute(near, 'gx', pairs)]
    pallas_call x9 -> x6, Pallas kernels: 14.9 us -> 16.1 us  [the longest x2 4.09 us: interior(): pl.pallas_call(body, name='first_interior' if fill else 'interior', out_s...]
    ppermute x4 -> x2, starting transfers between devices: 10 us -> 10.4 us  [exchanged(): far = lax.ppermute(far, 'gx', pairs)]
  transfers between devices with their start and end apart: 14 -> 10, of which waited for: 6 -> 4; matrix products, arithmetic and copies ran while one was open for 0% -> 0% of each run, Pallas kernels for 24% -> 22%
where the time goes in v3:
time: 45.8 us; the launch traced here: 45.7 us
  Pallas kernels  19.7 us (43%)
  starting transfers between devices  18.8 us (41%)
  waiting for transfers between devices  6.35 us (14%)
  between operations  0.77 us (2%)
    ppermute x2, starting transfers between devices, exchanged(): far = lax.ppermute(far, 'gx', pairs)  10.4 us
    ppermute x6, starting transfers between devices, swapped(): lax.ppermute(value, 'gx', [(source, source ^ mask) for source in range(co...  6.36 us
    pallas_call x2, Pallas kernels, interior(): pl.pallas_call(body, name='first_interior' if fill else 'interior', out_s...  4.09 us
    pallas_call x1, Pallas kernels, begin(): pl.pallas_call(body, name='begin', out_shape=(*state_shapes(planes, depth...  3.57 us
    pallas_call x1, Pallas kernels, finish(): pl.pallas_call(body, name='finish', out_shape=(*state_shapes(planes, dept...  3.41 us
    ppermute x2, waiting for transfers between devices, exchanged(): far = lax.ppermute(far, 'gx', pairs)  3.34 us
    ppermute x6, waiting for transfers between devices, swapped(): lax.ppermute(value, 'gx', [(source, source ^ mask) for source in range(co...  3 us
    pallas_call x1, Pallas kernels, foretold(): pl.pallas_call(body, name='foretold', out_shape=(*state_shapes(planes, de...  2.56 us
  transfers between devices with their start and end apart: 10, of which 4 were waited for; matrix products, arithmetic and copies ran while one was open for 0% of the time, Pallas kernels for 22%

profile of v3, /device:TPU:0, one launch (start us, length us, event | category | flops | bytes accessed | tf_op | source)
XLA Modules:
  0.0 45.7 jit_solution(12036070763418012828)
XLA Ops:
  0.6 0.0 copy-start
  0.6 0.0 copy-start.1
  0.7 0.0 copy-start.2
  0.7 0.0 copy-start.3
  0.7 0.0 copy-start.4
  0.7 3.6 %begin.1 = (f32[3,6,24,768]{3,2,1,0:T(8,128)S(1)}, f32[3,6,24,768]{3,2,1,0:T(8,128)S(1)}, f32[3,6,24,768]{3,2,1,0:T(8,128)S(1)}, f32[3,6,24,768]{3,2,1,0:T(8,128...) custom-call(f32[3,6,24,768]{3,2,1,0:T(8,128)} %refs_0_.1, ...), custom_call_target="tpu_custom_call" | custom-call | tf_op jit(solution)/shard_map/begin/pallas_call | solution.py:393
  4.3 0.6 %collective-permute-start = (f32[136,768]{1,0:T(8,128)S(1)}, f32[136,768]{1,0:T(8,128)S(1)}, u32[]{:S(2)}, u32[]{:S(2)}) collective-permute-start(f32[136,768]{1,0:T(8,128)S(1)} %get-tuple-element.86), channel_id=1, source_target_pairs={{1,0},{3,2},{5,4},{7,6},{9,8},{11,10},{13,12},{15,14},{0,1},{2,3},... | collective-permute-start | bytes 1253384 | tf_op jit(solution)/shard_map/ppermute | solution.py:42
  4.8 5.7 %collective-permute-start.1 = (f32[136,768]{1,0:T(8,128)S(1)}, f32[136,768]{1,0:T(8,128)S(1)}, u32[]{:S(2)}, u32[]{:S(2)}) collective-permute-start(f32[136,768]{1,0:T(8,128)S(1)} %get-tuple-element.87), channel_id=1, source_target_pairs={{1,2},{3,4},{5,6},{7,8},{9,10},{11,12},{13,14},{15,0},{2,1},{4,3},... | collective-permute-start | bytes 1253384 | tf_op jit(solution)/shard_map/ppermute | solution.py:40
  10.5 0.0 copy-done
  10.5 0.0 copy-done.1
  10.5 0.0 copy-done.2
  10.5 0.0 copy-done.3
  10.5 0.0 copy-done.4
  10.5 2.4 %first_interior.1 = (f32[3,6,24,768]{3,2,1,0:T(8,128)S(1)}, f32[3,6,24,768]{3,2,1,0:T(8,128)S(1)}, f32[3,6,24,768]{3,2,1,0:T(8,128)S(1)}, f32[3,6,24,768]{3,2,1,...) custom-call(f32[3,6,24,768]{3,2,1,0:T(8,128)S(1)} %get-tuple-element, ...), custom_call_target="tpu_custom_call", output_to_operand_aliasing={{0}: (0, {}), {1}: (1, {}), {2}: (2, {}), {3}: (3, {}), {4}... | custom-call | tf_op jit(solution)/shard_map/first_interior/pallas_call | solution.py:446
  13.0 0.0 collective-permute-done.refs_11_
  13.0 3.3 %collective-permute-done.1.refs_12_ = f32[136,768]{1,0:T(8,128)S(1)} collective-permute-done((f32[136,768]{1,0:T(8,128)S(1)}, f32[136,768]{1,0:T(8,128)S(1)}, u32[]{:S(2)}, u32[]{:S(2)}) %collective-permute-start.1) | collective-permute-done | bytes 417824 | tf_op jit(solution)/shard_map/ppermute | solution.py:40
  16.3 2.5 %middle.1 = (f32[3,6,24,768]{3,2,1,0:T(8,128)S(1)}, f32[3,6,24,768]{3,2,1,0:T(8,128)S(1)}, f32[3,6,24,768]{3,2,1,0:T(8,128)S(1)}, f32[3,6,24,768]{3,2,1,0:T(8,12...) custom-call(f32[3,6,24,768]{3,2,1,0:T(8,128)S(1)} %get-tuple-element, ...), custom_call_target="tpu_custom_call", output_to_operand_aliasing={{0}: (0, {}), {1}: (1, {}), {2}: (2, {}), {3}: (3, {}), {4}... | custom-call | tf_op jit(solution)/shard_map/middle/pallas_call | solution.py:543
  18.8 1.5 %collective-permute-start.2 = (f32[96,768]{1,0:T(8,128)S(1)}, f32[96,768]{1,0:T(8,128)S(1)}, u32[]{:S(2)}, u32[]{:S(2)}) collective-permute-start(f32[96,768]{1,0:T(8,128)S(1)} %get-tuple-element.109), channel_id=1, source_target_pairs={{1,0},{3,2},{5,4},{7,6},{9,8},{11,10},{13,12},{15,14},{0,1},{2,3},... | collective-permute-start | bytes 884744 | tf_op jit(solution)/shard_map/ppermute | solution.py:42
  20.2 4.8 %collective-permute-start.3 = (f32[96,768]{1,0:T(8,128)S(1)}, f32[96,768]{1,0:T(8,128)S(1)}, u32[]{:S(2)}, u32[]{:S(2)}) collective-permute-start(f32[96,768]{1,0:T(8,128)S(1)} %get-tuple-element.110), channel_id=1, source_target_pairs={{1,2},{3,4},{5,6},{7,8},{9,10},{11,12},{13,14},{15,0},{2,1},{4,3},... | collective-permute-start | bytes 884744 | tf_op jit(solution)/shard_map/ppermute | solution.py:40
  25.0 1.4 %prepared.1 = (bf16[192,4096]{1,0:T(8,128)(2,1)S(1)}, f32[64,4096]{1,0:T(8,128)S(1)}, f32[768,128]{1,0:T(8,128)S(1)}, f32[256,384]{1,0:T(8,128)S(1)}) custom-call(s32[2,4096]{1,0:T(2,128)} %orders_in.1, f32[768,128]{1,0:T(8,128)} %constant.4.clone.y_in, f32[256,384]{1,0:T(8,128)} %constant.5.clone.x_in), custom_call_target="tpu_custom_call" | custom-call | tf_op jit(solution)/shard_map/prepared/pallas_call | solution.py:823
  26.4 2.6 %foretold.1 = (f32[3,6,24,768]{3,2,1,0:T(8,128)S(1)}, f32[3,6,24,768]{3,2,1,0:T(8,128)S(1)}, f32[3,6,24,768]{3,2,1,0:T(8,128)S(1)}, f32[3,6,24,768]{3,2,1,0:T(8,...) custom-call(f32[3,6,24,768]{3,2,1,0:T(8,128)S(1)} %get-tuple-element, ...), custom_call_target="tpu_custom_call", output_to_operand_aliasing={{0}: (0, {}), {1}: (1, {}), {2}: (2, {}), {3}: (3, {}), {4}... | custom-call | tf_op jit(solution)/shard_map/foretold/pallas_call | solution.py:671
  29.0 0.1 collective-permute-start.6
  29.0 0.1 collective-permute-start.5
  29.1 1.8 %collective-permute-start.4 = (f32[24,128]{1,0:T(8,128)S(1)}, f32[24,128]{1,0:T(8,128)S(1)}, u32[]{:S(2)}, u32[]{:S(2)}) collective-permute-start(f32[24,128]{1,0:T(8,128)S(1)} %get-tuple-element.117.refs_0_), channel_id=1, source_target_pairs={{0,1},{1,0},{2,3},{3,2},{4,5},{5,4},{6,7},{7,6},{8,9},{9,8},{10,11... | collective-permute-start | bytes 36872 | tf_op jit(solution)/shard_map/ppermute | solution.py:76
  30.9 1.3 %collective-permute-done.6.refs_3_ = f32[24,128]{1,0:T(8,128)S(1)} collective-permute-done((f32[24,128]{1,0:T(8,128)S(1)}, f32[24,128]{1,0:T(8,128)S(1)}, u32[]{:S(2)}, u32[]{:S(2)}) %collective-permute-start.6) | collective-permute-done | bytes 12320 | tf_op jit(solution)/shard_map/ppermute | solution.py:76
  32.1 0.7 %collective-permute-done.5.refs_2_ = f32[24,128]{1,0:T(8,128)S(1)} collective-permute-done((f32[24,128]{1,0:T(8,128)S(1)}, f32[24,128]{1,0:T(8,128)S(1)}, u32[]{:S(2)}, u32[]{:S(2)}) %collective-permute-start.5) | collective-permute-done | bytes 12320 | tf_op jit(solution)/shard_map/ppermute | solution.py:76
  32.8 0.0 collective-permute-done.4.refs_1_
  32.8 1.7 %collective-permute-start.9 = (f32[96,128]{1,0:T(8,128)S(1)}, f32[96,128]{1,0:T(8,128)S(1)}, u32[]{:S(2)}, u32[]{:S(2)}) collective-permute-start(f32[96,128]{1,0:T(8,128)S(1)} %packed.1.refs_0_), channel_id=1, source_target_pairs={{0,12},{1,13},{2,14},{3,15},{4,8},{5,9},{6,10},{7,11},{8,4},{9,5},... | collective-permute-start | bytes 147464 | tf_op jit(solution)/shard_map/ppermute | solution.py:76
  34.6 0.0 collective-permute-start.8
  34.6 2.7 %collective-permute-start.7 = (f32[96,128]{1,0:T(8,128)S(1)}, f32[96,128]{1,0:T(8,128)S(1)}, u32[]{:S(2)}, u32[]{:S(2)}) collective-permute-start(f32[96,128]{1,0:T(8,128)S(1)} %packed.1.refs_0_), channel_id=1, source_target_pairs={{0,4},{1,5},{2,6},{3,7},{4,0},{5,1},{6,2},{7,3},{8,12},{9,13},{10,... | collective-permute-start | bytes 147464 | tf_op jit(solution)/shard_map/ppermute | solution.py:76
  37.3 1.6 %interior.1 = (f32[3,6,24,768]{3,2,1,0:T(8,128)S(1)}, f32[3,6,24,768]{3,2,1,0:T(8,128)S(1)}, f32[3,6,24,768]{3,2,1,0:T(8,128)S(1)}, f32[3,6,24,768]{3,2,1,0:T(8,...) custom-call(f32[3,6,24,768]{3,2,1,0:T(8,128)S(1)} %get-tuple-element, ...), custom_call_target="tpu_custom_call", output_to_operand_aliasing={{0}: (0, {}), {1}: (1, {}), {2}: (2, {}), {3}: (3, {}), {4}... | custom-call | tf_op jit(solution)/shard_map/interior/pallas_call | solution.py:446
  38.9 0.0 collective-permute-done.9.refs_3_
  38.9 1.1 %collective-permute-done.8.refs_2_ = f32[96,128]{1,0:T(8,128)S(1)} collective-permute-done((f32[96,128]{1,0:T(8,128)S(1)}, f32[96,128]{1,0:T(8,128)S(1)}, u32[]{:S(2)}, u32[]{:S(2)}) %collective-permute-start.8) | collective-permute-done | bytes 49184 | tf_op jit(solution)/shard_map/ppermute | solution.py:76
  40.0 0.0 collective-permute-done.7.refs_1_
  40.0 2.3 %pick_orders.1 = f32[4,4096]{1,0:T(4,128)} custom-call(f32[96,128]{1,0:T(8,128)S(1)} %packed.1.refs_0_, f32[96,128]{1,0:T(8,128)S(1)} %collective-permute-done.7.refs_1_, f32[96,128]{1,0:T(8,128)S(1)} %collective-permute-done.8.refs_2_, f32[96,128]{1,0:T(8,128)S(1)} %collective-permute-done.9.refs_3_, f32[256,384]{1,0:T(8,128)S(1)} %get-tuple-element.118.refs_4_, ...), custom_call_target="tpu_custom_call" | custom-call | tf_op jit(solution)/shard_map/pick_orders/pallas_call | solution.py:878
  42.3 0.0 collective-permute-done.2.refs_11_
  42.3 0.0 collective-permute-done.3.refs_12_
  42.3 3.4 %finish.1 = (f32[3,6,24,768]{3,2,1,0:T(8,128)S(1)}, f32[3,6,24,768]{3,2,1,0:T(8,128)S(1)}, f32[3,6,24,768]{3,2,1,0:T(8,128)S(1)}, f32[3,6,24,768]{3,2,1,0:T(8,12...) custom-call(f32[3,6,24,768]{3,2,1,0:T(8,128)S(1)} %get-tuple-element, ...), custom_call_target="tpu_custom_call", output_to_operand_aliasing={{0}: (0, {}), {1}: (1, {}), {2}: (2, {}), {3}: (3, {}), {4}... | custom-call | tf_op jit(solution)/shard_map/finish/pallas_call | solution.py:732
  (1 shorter events, 0.0 us)
Async XLA Ops:
  0.6 9.8 %copy-start = (f32[4]{0:T(128)S(1)}, f32[4]{0:T(128)}, u32[]{:S(2)}) copy-start(f32[4]{0:T(128)} %refs_11_.3) | copy-start | bytes 52
  0.6 9.8 %copy-start.1 = (f32[4]{0:T(128)S(1)}, f32[4]{0:T(128)}, u32[]{:S(2)}) copy-start(f32[4]{0:T(128)} %refs_12_.1) | copy-start | bytes 52
  0.7 9.8 %copy-start.2 = (f32[4]{0:T(128)S(1)}, f32[4]{0:T(128)}, u32[]{:S(2)}) copy-start(f32[4]{0:T(128)} %refs_13_.1) | copy-start | bytes 52
  0.7 9.8 %copy-start.3 = (f32[4]{0:T(128)S(1)}, f32[4]{0:T(128)}, u32[]{:S(2)}) copy-start(f32[4]{0:T(128)} %refs_14_.1) | copy-start | bytes 52
  0.7 9.8 %copy-start.4 = (f32[4]{0:T(128)S(1)}, f32[4]{0:T(128)}, u32[]{:S(2)}) copy-start(f32[4]{0:T(128)} %refs_15_.1) | copy-start | bytes 52
  4.3 8.7 %collective-permute-start = (f32[136,768]{1,0:T(8,128)S(1)}, f32[136,768]{1,0:T(8,128)S(1)}, u32[]{:S(2)}, u32[]{:S(2)}) collective-permute-start(f32[136,768]{1,0:T(8,128)S(1)} %get-tuple-element.86), channel_id=1, source_target_pairs={{1,0},{3,2},{5,4},{7,6},{9,8},{11,10},{13,12},{15,14},{0,1},{2,3},... | collective-permute-start | bytes 1253384 | tf_op jit(solution)/shard_map/ppermute | solution.py:42
  4.8 11.5 %collective-permute-start.1 = (f32[136,768]{1,0:T(8,128)S(1)}, f32[136,768]{1,0:T(8,128)S(1)}, u32[]{:S(2)}, u32[]{:S(2)}) collective-permute-start(f32[136,768]{1,0:T(8,128)S(1)} %get-tuple-element.87), channel_id=1, source_target_pairs={{1,2},{3,4},{5,6},{7,8},{9,10},{11,12},{13,14},{15,0},{2,1},{4,3},... | collective-permute-start | bytes 1253384 | tf_op jit(solution)/shard_map/ppermute | solution.py:40
  18.8 23.5 %collective-permute-start.2 = (f32[96,768]{1,0:T(8,128)S(1)}, f32[96,768]{1,0:T(8,128)S(1)}, u32[]{:S(2)}, u32[]{:S(2)}) collective-permute-start(f32[96,768]{1,0:T(8,128)S(1)} %get-tuple-element.109), channel_id=1, source_target_pairs={{1,0},{3,2},{5,4},{7,6},{9,8},{11,10},{13,12},{15,14},{0,1},{2,3},... | collective-permute-start | bytes 884744 | tf_op jit(solution)/shard_map/ppermute | solution.py:42
  20.2 22.0 %collective-permute-start.3 = (f32[96,768]{1,0:T(8,128)S(1)}, f32[96,768]{1,0:T(8,128)S(1)}, u32[]{:S(2)}, u32[]{:S(2)}) collective-permute-start(f32[96,768]{1,0:T(8,128)S(1)} %get-tuple-element.110), channel_id=1, source_target_pairs={{1,2},{3,4},{5,6},{7,8},{9,10},{11,12},{13,14},{15,0},{2,1},{4,3},... | collective-permute-start | bytes 884744 | tf_op jit(solution)/shard_map/ppermute | solution.py:40
  29.0 3.2 %collective-permute-start.6 = (f32[24,128]{1,0:T(8,128)S(1)}, f32[24,128]{1,0:T(8,128)S(1)}, u32[]{:S(2)}, u32[]{:S(2)}) collective-permute-start(f32[24,128]{1,0:T(8,128)S(1)} %get-tuple-element.117.refs_0_), channel_id=1, source_target_pairs={{0,3},{1,2},{2,1},{3,0},{4,7},{5,6},{6,5},{7,4},{8,11},{9,10},{10,... | collective-permute-start | bytes 36872 | tf_op jit(solution)/shard_map/ppermute | solution.py:76
  29.0 3.8 %collective-permute-start.5 = (f32[24,128]{1,0:T(8,128)S(1)}, f32[24,128]{1,0:T(8,128)S(1)}, u32[]{:S(2)}, u32[]{:S(2)}) collective-permute-start(f32[24,128]{1,0:T(8,128)S(1)} %get-tuple-element.117.refs_0_), channel_id=1, source_target_pairs={{0,2},{1,3},{2,0},{3,1},{4,6},{5,7},{6,4},{7,5},{8,10},{9,11},{10,... | collective-permute-start | bytes 36872 | tf_op jit(solution)/shard_map/ppermute | solution.py:76
  29.1 3.7 %collective-permute-start.4 = (f32[24,128]{1,0:T(8,128)S(1)}, f32[24,128]{1,0:T(8,128)S(1)}, u32[]{:S(2)}, u32[]{:S(2)}) collective-permute-start(f32[24,128]{1,0:T(8,128)S(1)} %get-tuple-element.117.refs_0_), channel_id=1, source_target_pairs={{0,1},{1,0},{2,3},{3,2},{4,5},{5,4},{6,7},{7,6},{8,9},{9,8},{10,11... | collective-permute-start | bytes 36872 | tf_op jit(solution)/shard_map/ppermute | solution.py:76
  32.8 6.1 %collective-permute-start.9 = (f32[96,128]{1,0:T(8,128)S(1)}, f32[96,128]{1,0:T(8,128)S(1)}, u32[]{:S(2)}, u32[]{:S(2)}) collective-permute-start(f32[96,128]{1,0:T(8,128)S(1)} %packed.1.refs_0_), channel_id=1, source_target_pairs={{0,12},{1,13},{2,14},{3,15},{4,8},{5,9},{6,10},{7,11},{8,4},{9,5},... | collective-permute-start | bytes 147464 | tf_op jit(solution)/shard_map/ppermute | solution.py:76
  34.6 5.5 %collective-permute-start.8 = (f32[96,128]{1,0:T(8,128)S(1)}, f32[96,128]{1,0:T(8,128)S(1)}, u32[]{:S(2)}, u32[]{:S(2)}) collective-permute-start(f32[96,128]{1,0:T(8,128)S(1)} %packed.1.refs_0_), channel_id=1, source_target_pairs={{0,8},{1,9},{2,10},{3,11},{4,12},{5,13},{6,14},{7,15},{8,0},{9,1},... | collective-permute-start | bytes 147464 | tf_op jit(solution)/shard_map/ppermute | solution.py:76
  34.6 5.5 %collective-permute-start.7 = (f32[96,128]{1,0:T(8,128)S(1)}, f32[96,128]{1,0:T(8,128)S(1)}, u32[]{:S(2)}, u32[]{:S(2)}) collective-permute-start(f32[96,128]{1,0:T(8,128)S(1)} %packed.1.refs_0_), channel_id=1, source_target_pairs={{0,4},{1,5},{2,6},{3,7},{4,0},{5,1},{6,2},{7,3},{8,12},{9,13},{10,... | collective-permute-start | bytes 147464 | tf_op jit(solution)/shard_map/ppermute | solution.py:76
